TPU v7x, 32 devices: a whole 2x2x4 slice. The times are simulated.
32 devices in a mesh: inp: 4 (over y, core), hid: 8 (over z, x).
Axes of the slice: x: 2, y: 2, z: 4, core: 2. Of those that a mesh axis runs over, the one named last changes fastest.
Arguments:
- inputs: bfloat16 [128, 16384], P(None, 'inp'), may hold values from -6 to 6
- out_grad: bfloat16 [128, 16384], P(None, 'inp'), may hold values from -6 to 6
- gate_index: int32 [8192, 26624], P('inp', 'hid'), may hold values from 0 to 255, as said below
- up_index: int32 [8192, 26624], P('inp', 'hid'), may hold values from 0 to 255, as said below
- down_index: int32 [13312, 16384], P('hid', 'inp'), may hold values from 0 to 255, as said below
- gate_table: float32 [16, 26624], P(None, 'hid'), may hold values from -0.046875 to 0.046875
- up_table: float32 [16, 26624], P(None, 'hid'), may hold values from -0.046875 to 0.046875
- down_table: float32 [16, 16384], P(None, 'inp'), may hold values from -0.0390625 to 0.0390625
Outputs:
- input_grad: bfloat16 [128, 16384], P('hid', 'inp')
- gate_table_grad: float32 [16, 26624], P(None, 'hid')
- up_table_grad: float32 [16, 26624], P(None, 'hid')
- down_table_grad: float32 [16, 16384], P(None, 'inp')
Inputs may be any that keep to these rules, and one draw needn't show every extreme that they name: `gate_index`: each word holds two independent 4-bit table entries. `up_index`: each word holds two independent 4-bit table entries. `down_index`: each word holds two independent 4-bit table entries.
All inputs are finite; a program needn't handle non-finite values.
Results may differ from a plain program's by a relative error of at most 0.0072.
Values may be sent and summed in bfloat16 or wider, within the bound.
A program may use at most 512 MiB of HBM per device.

v0:
```python
import functools
import math

import jax
import jax.numpy as jnp
from jax import lax
from jax.experimental import pallas as pl
from jax.experimental.pallas import tpu as pltpu
from jax.sharding import PartitionSpec as P

LANES = 128
SUB = 16
F32 = jnp.float32
BF16 = jnp.bfloat16


def divisor(size, most, unit=LANES):
    best = unit
    for cand in range(unit, most + 1, unit):
        if size % cand == 0:
            best = cand
    return best


def bit_masks(words, parity):
    return [(words & jnp.int16(1 << (4 * parity + bit))) != 0 for bit in range(4)]


def look_up(levels, masks):
    for mask in masks:
        levels = [jnp.where(mask, levels[i + 1], levels[i]) for i in range(0, len(levels), 2)]
    return levels[0]


def table_rows(table_ref, lanes):
    return [
        jnp.broadcast_to(table_ref[k : k + 1, lanes], (SUB, LANES)).astype(BF16)
        for k in range(16)
    ]


def pipelined(count, make, use):
    make(0, 0)

    def body(j, carry):
        make(2 * j + 1, 1)
        use(2 * j, 0)
        make(2 * j + 2, 0)
        use(2 * j + 1, 1)
        return carry

    lax.fori_loop(0, (count - 1) // 2, body, 0)
    if count % 2 == 0:
        make(count - 1, 1)
        use(count - 2, 0)
        use(count - 1, 1)
    else:
        use(count - 1, 0)


def decode_tile(idx_ref, table_ref, weight_ref, half):
    words, cols = idx_ref.shape
    for chunk in range(cols // LANES):
        lanes = slice(chunk * LANES, (chunk + 1) * LANES)
        table = table_rows(table_ref, lanes)

        def body(i, carry):
            for step in range(half // SUB):
                piece = idx_ref[pl.ds(pl.multiple_of(i * half + step * SUB, SUB), SUB), lanes].astype(jnp.int16)
                for parity in range(2):
                    row = pl.multiple_of((2 * i + parity) * half + step * SUB, SUB)
                    weight_ref[pl.ds(row, SUB), lanes] = look_up(table, bit_masks(piece, parity))
            return carry

        lax.fori_loop(0, words // half, body, 0)


def up_kernel(x_ref, idx_ref, table_ref, pre_ref, weight_ref):
    count, _, block = x_ref.shape
    decode_tile(idx_ref, table_ref, weight_ref, block // 2)
    pre_ref[...] = sum(
        jnp.dot(x_ref[i], weight_ref[i * block : (i + 1) * block, :], preferred_element_type=F32)
        for i in range(count)
    )


def up_product(x_blocks, index, lookup):
    count, tokens, block = x_blocks.shape
    words, width = index.shape
    cols = divisor(width, 256)
    return pl.pallas_call(
        up_kernel,
        grid=(width // cols,),
        in_specs=[
            pl.BlockSpec((count, tokens, block), lambda j: (0, 0, 0)),
            pl.BlockSpec((words, cols), lambda j: (0, j)),
            pl.BlockSpec((16, cols), lambda j: (0, j)),
        ],
        out_specs=[
            pl.BlockSpec((tokens, cols), lambda j: (0, j)),
            pl.BlockSpec((2 * words, cols), lambda j: (0, j)),
        ],
        out_shape=[
            jax.ShapeDtypeStruct((tokens, width), F32),
            jax.ShapeDtypeStruct((2 * words, width), BF16),
        ],
        name="up_product",
    )(x_blocks, index, lookup)


def down_kernel(og_ref, idx_ref, table_ref, out_ref, weight_ref):
    count, _, block = out_ref.shape

    @pl.when(pl.program_id(0) == 0)
    def _():
        out_ref[...] = jnp.zeros_like(out_ref)

    decode_tile(idx_ref, table_ref, weight_ref, block // 2)
    for i in range(count):
        out_ref[i] += contract_cols(og_ref[...], weight_ref[i * block : (i + 1) * block, :])


def down_product(out_grad, index, lookup):
    tokens = out_grad.shape[0]
    words, width = index.shape
    cols = divisor(width, 256)
    block = math.gcd(2 * words, 256)
    count = 2 * words // block
    return pl.pallas_call(
        down_kernel,
        grid=(width // cols,),
        in_specs=[
            pl.BlockSpec((tokens, cols), lambda j: (0, j)),
            pl.BlockSpec((words, cols), lambda j: (0, j)),
            pl.BlockSpec((16, cols), lambda j: (0, j)),
        ],
        out_specs=pl.BlockSpec((count, tokens, block), lambda j: (0, 0, 0)),
        out_shape=jax.ShapeDtypeStruct((count, tokens, block), F32),
        scratch_shapes=[pltpu.VMEM((2 * words, cols), BF16)],
        name="down_product",
    )(out_grad, index, lookup)


def contract_cols(left, right):
    return lax.dot_general(left, right, (((1,), (1,)), ((), ())), preferred_element_type=F32)


def input_kernel(gate_ref, up_ref, wg_ref, wu_ref, out_ref):
    count, _, block = out_ref.shape

    @pl.when(pl.program_id(0) == 0)
    def _():
        out_ref[...] = jnp.zeros_like(out_ref)

    gate, up = gate_ref[...], up_ref[...]

    def body(i, carry):
        rows = pl.ds(pl.multiple_of(i * block, block), block)
        out_ref[i] += contract_cols(gate, wg_ref[rows, :]) + contract_cols(up, wu_ref[rows, :])
        return carry

    lax.fori_loop(0, count, body, 0, unroll=2 if count % 2 == 0 else 1)


def input_product(gate_grad, up_grad, w_gate, w_up):
    tokens, width = gate_grad.shape
    rows = w_gate.shape[0]
    cols = divisor(width, 256)
    block = math.gcd(rows, 256)
    grad = pl.BlockSpec((tokens, cols), lambda j: (0, j))
    weight = pl.BlockSpec((rows, cols), lambda j: (0, j))
    return pl.pallas_call(
        input_kernel,
        grid=(width // cols,),
        in_specs=[grad, grad, weight, weight],
        out_specs=pl.BlockSpec((rows // block, tokens, block), lambda j: (0, 0, 0)),
        out_shape=jax.ShapeDtypeStruct((rows // block, tokens, block), F32),
        name="input_product",
    )(gate_grad, up_grad, w_gate, w_up)


def leaves(value, masks):
    b0, b1, b2, b3 = masks
    zero = jnp.zeros_like(value)
    out = []
    for part in (jnp.where(b3, zero, value), jnp.where(b3, value, zero)):
        for piece in (jnp.where(b2, zero, part), jnp.where(b2, part, zero)):
            one = jnp.where(b1, piece, zero)
            out += [piece, jnp.where(b0, piece, zero), one, jnp.where(b0, one, zero)]
    return out


def write_bins(acc_ref, out_ref, scale):
    rows = [jnp.sum(acc_ref[8 * k : 8 * k + 8, :], axis=0, keepdims=True) for k in range(16)]
    for k in range(0, 16, 4):
        none, low, high, both = rows[k : k + 4]
        out_ref[k : k + 1, :] = ((none - low) - (high - both)) * scale
        out_ref[k + 1 : k + 2, :] = (low - both) * scale
        out_ref[k + 2 : k + 3, :] = (high - both) * scale
        out_ref[k + 3 : k + 4, :] = both * scale


def bins_kernel(scale, left_ref, right_ref, idx_ref, out_ref, acc_ref, *slots):
    count, block, _ = left_ref.shape
    half = block // 2
    cols = idx_ref.shape[1]
    acc_ref[...] = jnp.zeros_like(acc_ref)

    def make(i, slot):
        slots[slot][...] = jnp.dot(left_ref[i], right_ref[...], preferred_element_type=F32).astype(BF16)

    def use(i, slot):
        for chunk in range(cols // LANES):
            lanes = slice(chunk * LANES, (chunk + 1) * LANES)
            sums = None
            for step in range(half // SUB):
                row = pl.multiple_of(i * half + step * SUB, SUB)
                words = idx_ref[pl.ds(row, SUB), lanes].astype(jnp.int16)
                for parity in range(2):
                    first = parity * half + step * SUB
                    parts = leaves(slots[slot][first : first + SUB, lanes], bit_masks(words, parity))
                    sums = parts if sums is None else [a + b for a, b in zip(sums, parts)]
            for k, total in enumerate(sums):
                wide = total.astype(F32)
                acc_ref[8 * k : 8 * k + 8, lanes] += wide[:8] + wide[8:]

    pipelined(count, make, use)
    write_bins(acc_ref, out_ref, scale)


def bins(left_blocks, right, index, scale):
    count, tokens, block = left_blocks.shape
    words, width = index.shape
    cols = divisor(width, 256)
    return pl.pallas_call(
        functools.partial(bins_kernel, scale),
        grid=(width // cols,),
        in_specs=[
            pl.BlockSpec((count, block, tokens), lambda j: (0, 0, 0)),
            pl.BlockSpec((tokens, cols), lambda j: (0, j)),
            pl.BlockSpec((words, cols), lambda j: (0, j)),
        ],
        out_specs=pl.BlockSpec((16, cols), lambda j: (0, j)),
        out_shape=jax.ShapeDtypeStruct((16, width), F32),
        scratch_shapes=[pltpu.VMEM((128, cols), F32)] + [pltpu.VMEM((block, cols), BF16)] * 2,
        name="bins",
    )(jnp.swapaxes(left_blocks, 1, 2), right, index)


def pairing(block, dtype):
    row = jnp.arange(block)[:, None]
    col = jnp.arange(block)[None, :]
    half = block // 2
    return (row == 2 * (col % half) + col // half).astype(dtype)


def to_blocks(array):
    rows, cols = array.shape
    block = math.gcd(cols, 256)
    out = lax.dot_general(
        array.reshape(rows, cols // block, block), pairing(block, array.dtype), (((2,), (0,)), ((), ())),
        preferred_element_type=F32,
    )
    return jnp.swapaxes(out.astype(array.dtype), 0, 1)


def from_blocks(blocks):
    count, rows, block = blocks.shape
    out = lax.dot_general(
        blocks, pairing(block, blocks.dtype), (((2,), (1,)), ((), ())), precision=lax.Precision.HIGHEST,
        preferred_element_type=F32,
    )
    return jnp.swapaxes(out, 0, 1).reshape(rows, count * block)


def exchange(array, axis, size, bit):
    return lax.ppermute(array, axis, [(i, i ^ bit) for i in range(size)])


def axis_bits(size):
    return [1 << i for i in range(size.bit_length() - 1)]


def sum_scatter(array, axis):
    size = lax.axis_size(axis)
    if size & (size - 1):
        return lax.psum_scatter(array, axis, scatter_dimension=0, tiled=True)
    me = lax.axis_index(axis)
    rows, cols = array.shape
    array = array.reshape(size, rows // size, cols)
    for bit in axis_bits(size):
        pairs = array.reshape(array.shape[0] // 2, 2, rows // size, cols)
        mine = jnp.bitwise_and(me // bit, 1)
        sent = exchange(lax.dynamic_index_in_dim(pairs, 1 - mine, 1, False), axis, size, bit)
        array = lax.dynamic_index_in_dim(pairs, mine, 1, False) + sent
    return array.reshape(rows // size, cols)


def gather(array, axis):
    size = lax.axis_size(axis)
    if size & (size - 1):
        return lax.all_gather(array, axis, axis=0, tiled=True)
    me = lax.axis_index(axis)
    rows, cols = array.shape
    array = array[None]
    for bit in reversed(axis_bits(size)):
        other = exchange(array, axis, size, bit)
        first = jnp.bitwise_and(me // bit, 1) == 0
        low, high = jnp.where(first, array, other), jnp.where(first, other, array)
        array = jnp.stack([low, high], axis=1).reshape(-1, rows, cols)
    return array.reshape(size * rows, cols)


def sum_all(array, axis):
    size = lax.axis_size(axis)
    if size & (size - 1):
        return lax.psum(array, axis)
    for bit in axis_bits(size):
        array = array + exchange(array, axis, size, bit)
    return array


def after(array, *done):
    return lax.optimization_barrier((array, *done))[0]


def local_hidden(pre_gate, pre_up, hidden_grad):
    sig_gate = jax.nn.sigmoid(pre_gate)
    silu_gate = pre_gate * sig_gate
    activ = (silu_gate * pre_up).astype(BF16)
    gate_grad = (hidden_grad * pre_up * sig_gate * (1.0 + pre_gate * (1.0 - sig_gate))).astype(BF16)
    up_grad = (hidden_grad * silu_gate).astype(BF16)
    return activ, gate_grad, up_grad


def shards(inputs, out_grad, gate_index, up_index, down_index, gate_table, up_table, down_table):
    tokens = inputs.shape[0]
    width = gate_index.shape[1]
    scale = 1.0 / tokens
    hid_blocks = down_product(out_grad, down_index, down_table)
    count, _, block = hid_blocks.shape
    hid = lax.psum_scatter(hid_blocks, "inp", scatter_dimension=1, tiled=True)
    x_blocks = to_blocks(inputs)
    pre_gate, w_gate = up_product(x_blocks, gate_index, after(gate_table, hid_blocks))
    gate_share = lax.psum_scatter(pre_gate, "inp", scatter_dimension=0, tiled=True)
    pre_up, w_up = up_product(x_blocks, up_index, after(up_table, pre_gate))
    up_share = sum_scatter(pre_up, "inp")
    activ, gate_grad, up_grad = local_hidden(gate_share, up_share, from_blocks(hid))
    grads = gather(jnp.concatenate([gate_grad, up_grad], axis=1), "inp")
    gate_grad, up_grad = grads[:, :width], grads[:, width:]
    acts = gather(after(activ, gate_grad), "inp")
    din_blocks = input_product(gate_grad, up_grad, w_gate, w_up)
    din = lax.psum_scatter(din_blocks, "hid", scatter_dimension=1, tiled=True)
    input_grad = from_blocks(din).astype(BF16)
    act_blocks = to_blocks(after(acts, din_blocks))
    down_part = bins(act_blocks, out_grad, down_index, scale)
    down_sum = lax.psum(after(down_part, din), "hid")
    gate_part = bins(x_blocks, after(gate_grad, down_part, din), gate_index, scale)
    up_part = bins(x_blocks, after(up_grad, gate_part, down_sum), up_index, scale)
    up_width = up_part.shape[1]
    sums = sum_all(jnp.concatenate([gate_part, up_part], axis=1), "inp")
    gate_sum, up_sum = sums[:, :up_width], sums[:, up_width:]
    return input_grad, gate_sum, up_sum, down_sum


def solution(mesh):
    in_specs = (
        P(None, "inp"),
        P(None, "inp"),
        P("inp", "hid"),
        P("inp", "hid"),
        P("hid", "inp"),
        P(None, "hid"),
        P(None, "hid"),
        P(None, "inp"),
    )
    out_specs = (P("hid", "inp"), P(None, "hid"), P(None, "hid"), P(None, "inp"))
    return jax.shard_map(shards, mesh=mesh, in_specs=in_specs, out_specs=out_specs, check_vma=False)
```

profile of v0, /device:TPU:0, one launch (start us, length us, event | category | flops | bytes accessed | tf_op | source)
XLA Modules:
  0.0 427.8 jit_solution(3384131667653121954)
XLA Ops:
  7.2 40.7 %down_product.1 = f32[13,128,256]{2,1,0:T(8,128)} custom-call(bf16[128,4096]{1,0:T(8,128)(2,1)} %right_ref.1, s32[1664,4096]{1,0:T(8,128)} %idx_ref.9, f32[16,4096]{1,0:T(8,128)} %table_ref.1), custom_call_target="tpu_custom_call" | custom-call | tf_op jit(solution)/shard_map/down_product/pallas_call | solution.py:129
  48.0 1.1 copy-done.3
  49.7 1.3 copy.23.x_ref
  51.0 35.4 %up_product.2 = (f32[128,3328]{1,0:T(8,128)}, bf16[4096,3328]{1,0:T(8,128)(2,1)}) custom-call(bf16[16,128,256]{2,1,0:T(8,128)(2,1)} %copy.23.x_ref, s32[2048,3328]{1,0:T(8,128)} %idx_ref.10, f32[16,3328]{1,0:T(8,128)} %table_ref.2), custom_call_target="tpu_custom_call" | custom-call | tf_op jit(solution)/shard_map/up_product/pallas_call | solution.py:91
  86.5 35.4 %up_product.3 = (f32[128,3328]{1,0:T(8,128)}, bf16[4096,3328]{1,0:T(8,128)(2,1)}) custom-call(bf16[16,128,256]{2,1,0:T(8,128)(2,1)} %copy.23.x_ref, s32[2048,3328]{1,0:T(8,128)} %idx_ref.11, f32[16,3328]{1,0:T(8,128)} %table_ref.3), custom_call_target="tpu_custom_call" | custom-call | tf_op jit(solution)/shard_map/up_product/pallas_call | solution.py:91
  121.9 1.3 dynamic-slice_bitcast_fusion
  123.8 2.0 collective-permute-done
  125.9 2.9 collective-permute-start.1
  128.9 1.4 convolution_bitcast_fusion
  130.3 8.7 %collective-permute-done.1 = f32[1,32,3328]{2,1,0:T(8,128)S(1)} collective-permute-done((f32[1,32,3328]{2,1,0:T(8,128)S(1)}, f32[1,32,3328]{2,1,0:T(8,128)S(1)}, u32[]{:S(2)}, u32[]{:S(2)}) %collective-permute-start.1) | collective-permute-done | bytes 426016 | tf_op jit(solution)/shard_map/ppermute | solution.py:277
  139.0 1.2 fusion.7
  140.3 1.8 collective-permute-start.2
  142.1 9.5 %collective-permute-done.2 = bf16[1,32,6656]{2,1,0:T(8,128)(2,1)S(1)} collective-permute-done((bf16[1,32,6656]{2,1,0:T(8,128)(2,1)S(1)}, bf16[1,32,6656]{2,1,0:T(8,128)(2,1)S(1)}, u32[]{:S(2)}, u32[]{:S(2)}) %collective-permute-start.2) | collective-permute-done | bytes 426016 | tf_op jit(solution)/shard_map/ppermute | solution.py:277
  151.9 2.4 collective-permute-done.3
  154.7 1.3 fusion.24
  156.0 36.6 %input_product.1 = f32[16,128,256]{2,1,0:T(8,128)} custom-call(bf16[128,3328]{1,0:T(8,128)(2,1)} %get-tuple-element.23.gate_ref.right_ref, bf16[128,3328]{1,0:T(8,128)(2,1)} %get-tuple-element.25.up_ref.right_ref, bf16[4096,3328]{1,0:T(8,128)(2,1)} %get-tuple-element.19.wg_ref, bf16[4096,3328]{1,0:T(8,128)(2,1)} %get-tuple-element.20.wu_ref), custom_call_target="tpu_custom_call" | custom-call | tf_op jit(solution)/shard_map/input_product/pallas_call | solution.py:172
  192.6 1.5 collective-permute-start.4
  194.2 5.8 %collective-permute-done.4 = bf16[1,32,3328]{2,1,0:T(8,128)(2,1)S(1)} collective-permute-done((bf16[1,32,3328]{2,1,0:T(8,128)(2,1)S(1)}, bf16[1,32,3328]{2,1,0:T(8,128)(2,1)S(1)}, u32[]{:S(2)}, u32[]{:S(2)}) %collective-permute-start.4) | collective-permute-done | bytes 213024 | tf_op jit(solution)/shard_map/ppermute | solution.py:277
  200.2 1.8 collective-permute-done.5
  202.8 1.4 fusion.left_ref
  204.1 63.3 %bins.3 = f32[16,4096]{1,0:T(8,128)} custom-call(bf16[13,256,128]{2,1,0:T(8,128)(2,1)} %fusion.left_ref, bf16[128,4096]{1,0:T(8,128)(2,1)} %right_ref.1, s32[1664,4096]{1,0:T(8,128)} %idx_ref.9), custom_call_target="tpu_custom_call" | custom-call | tf_op jit(solution)/shard_map/bins/pallas_call | solution.py:235
  267.5 64.1 %bins.4 = f32[16,3328]{1,0:T(8,128)} custom-call(bf16[16,256,128]{2,1,0:T(8,128)(2,1)} %bitcast.85, bf16[128,3328]{1,0:T(8,128)(2,1)} %get-tuple-element.23.gate_ref.right_ref, s32[2048,3328]{1,0:T(8,128)} %idx_ref.10), custom_call_target="tpu_custom_call" | custom-call | tf_op jit(solution)/shard_map/bins/pallas_call | solution.py:235
  331.5 8.4 %all-reduce.2.cloned.1.call-done = f32[16,4096]{1,0:T(8,128)} async-done(((f32[16,4096]{1,0:T(8,128)}), f32[16,4096]{1,0:T(8,128)}) %all-reduce.2.cloned.1.call-update) | async-done | bytes 262160 | tf_op jit(solution)/shard_map/psum | solution.py:357
  339.9 64.0 %bins.5 = f32[16,3328]{1,0:T(8,128)} custom-call(bf16[16,256,128]{2,1,0:T(8,128)(2,1)} %bitcast.86, bf16[128,3328]{1,0:T(8,128)(2,1)} %get-tuple-element.25.up_ref.right_ref, s32[2048,3328]{1,0:T(8,128)} %idx_ref.11), custom_call_target="tpu_custom_call" | custom-call | tf_op jit(solution)/shard_map/bins/pallas_call | solution.py:235
  403.9 1.0 pad_maximum_fusion.2
  405.0 1.8 collective-permute-done.6
  406.8 1.0 fusion.23
  407.8 1.5 collective-permute-start.7
  409.7 0.7 copy.36
  410.4 9.4 %collective-permute-done.7 = f32[16,6656]{1,0:T(8,128)S(1)} collective-permute-done((f32[16,6656]{1,0:T(8,128)S(1)}, f32[16,6656]{1,0:T(8,128)S(1)}, u32[]{:S(2)}, u32[]{:S(2)}) %collective-permute-start.7) | collective-permute-done | bytes 426016 | tf_op jit(solution)/shard_map/ppermute | solution.py:277
  419.8 0.8 fusion.25
  420.6 0.7 copy.42
  (45 shorter events, 3.6 us)
Async XLA Ops:
  7.2 121.7 %reduce-scatter.4.cloned.1.call-start = ((), (), s32[]{:S(2)}) async-start(), calls=%async_computation.3 | async-start | bytes 2129920 | tf_op jit(solution)/shard_map/reduce_scatter | solution.py:342
  47.9 1.2 copy-start.3
  48.0 91.0 %reduce-scatter.6.cloned.1.call-start = ((), (), s32[]{:S(2)}) async-start(), calls=%async_computation.4 | async-start | bytes 2129920 | tf_op jit(solution)/shard_map/reduce_scatter | solution.py:345
  49.7 36.7 %copy-start = (bf16[256,128,16]{1,0,2:T(8,128)(2,1)}, bf16[256,128,16]{1,0,2:T(8,128)(2,1)S(1)}, u32[]{:S(2)}) copy-start(bf16[256,128,16]{1,0,2:T(8,128)(2,1)S(1)} %convolution_convert_fusion) | copy-start | bytes 3145732
  86.4 181.0 %reduce-scatter.8.cloned.1.call-start = ((), (), s32[]{:S(2)}) async-start(), calls=%async_computation.5 | async-start | bytes 2359296 | tf_op jit(solution)/shard_map/reduce_scatter | solution.py:353
  121.9 3.9 copy-start.2
  123.2 2.6 collective-permute-start
  125.9 13.1 %collective-permute-start.1 = (f32[1,32,3328]{2,1,0:T(8,128)S(1)}, f32[1,32,3328]{2,1,0:T(8,128)S(1)}, u32[]{:S(2)}, u32[]{:S(2)}) collective-permute-start(f32[1,32,3328]{2,1,0:T(8,128)S(1)} %constant_dynamic-slice_fusion), channel_id=1, source_target_pairs={{0,16},{8,24},{16,0},{24,8},{1,17},{9,25},{17,1},{25,9},{2,18},{10... | collective-permute-start | bytes 1277960 | tf_op jit(solution)/shard_map/ppermute | solution.py:277
  140.3 11.3 %collective-permute-start.2 = (bf16[1,32,6656]{2,1,0:T(8,128)(2,1)S(1)}, bf16[1,32,6656]{2,1,0:T(8,128)(2,1)S(1)}, u32[]{:S(2)}, u32[]{:S(2)}) collective-permute-start(bf16[1,32,6656]{2,1,0:T(8,128)(2,1)S(1)} %maximum_bitcast_fusion.1), channel_id=1, source_target_pairs={{0,16},{8,24},{16,0},{24,8},{1,17},{9,25},{17,1},{25,9},{2,18},{10... | collective-permute-start | bytes 1277960 | tf_op jit(solution)/shard_map/ppermute | solution.py:277
  151.8 2.4 collective-permute-start.3
  192.6 147.3 %all-reduce.2.cloned.1.call-start = ((), (), s32[]{:S(2)}) async-start(), calls=%async_computation.6 | async-start | bytes 524288 | tf_op jit(solution)/shard_map/psum | solution.py:357
  192.6 7.4 %collective-permute-start.4 = (bf16[1,32,3328]{2,1,0:T(8,128)(2,1)S(1)}, bf16[1,32,3328]{2,1,0:T(8,128)(2,1)S(1)}, u32[]{:S(2)}, u32[]{:S(2)}) collective-permute-start(bf16[1,32,3328]{2,1,0:T(8,128)(2,1)S(1)} %bitcast.94), channel_id=1, source_target_pairs={{0,16},{8,24},{16,0},{24,8},{1,17},{9,25},{17,1},{25,9},{2,18},{10... | collective-permute-start | bytes 638984 | tf_op jit(solution)/shard_map/ppermute | solution.py:277
  200.1 1.8 collective-permute-start.5
  331.5 72.4 %copy-start.1 = (f32[16,3328]{1,0:T(8,128)S(1)}, f32[16,3328]{1,0:T(8,128)}, u32[]{:S(2)}) copy-start(f32[16,3328]{1,0:T(8,128)} %bins.4) | copy-start | bytes 638980
  403.9 5.4 %copy-start.4 = (f32[16,16,256]{2,1,0:T(8,128)S(1)}, f32[16,16,256]{2,1,0:T(8,128)}, u32[]{:S(2)}) copy-start(f32[16,16,256]{2,1,0:T(8,128)} %reduce-scatter.8.cloned.1.call-done) | copy-start | bytes 786436
  405.0 1.8 collective-permute-start.6
  407.8 12.8 %copy-start.5 = (f32[16,4096]{1,0:T(8,128)S(1)}, f32[16,4096]{1,0:T(8,128)}, u32[]{:S(2)}) copy-start(f32[16,4096]{1,0:T(8,128)} %all-reduce.2.cloned.1.call-done) | copy-start | bytes 786436
  407.8 11.9 %collective-permute-start.7 = (f32[16,6656]{1,0:T(8,128)S(1)}, f32[16,6656]{1,0:T(8,128)S(1)}, u32[]{:S(2)}, u32[]{:S(2)}) collective-permute-start(f32[16,6656]{1,0:T(8,128)S(1)} %fusion.23), channel_id=1, source_target_pairs={{0,16},{8,24},{16,0},{24,8},{1,17},{9,25},{17,1},{25,9},{2,18},{10... | collective-permute-start | bytes 1277960 | tf_op jit(solution)/shard_map/ppermute | solution.py:277
Sparse Core Ops, SparseCore 0:
  48.1 31.4 reduce-scatter.3
  86.5 31.5 reduce-scatter.5
  192.7 69.8 reduce-scatter.7
  267.6 72.2 all-reduce.1
where the time goes:
time: 428 us
  Pallas kernels  339 us (79%)
  waiting for transfers between devices  49.7 us (12%)
  between operations  14 us (3%)
  starting transfers between devices  8.75 us (2%)
  local copies, waits for them, and re-layouts  8.1 us (2%)
    pallas_call x3, Pallas kernels, bins(): pl.pallas_call(functools.partial(bins_kernel, scale), grid=(width // cols...  191 us
    pallas_call x2, Pallas kernels, up_product(): pl.pallas_call(up_kernel, grid=(width // cols,), in_specs=[pl.BlockSpec((...  70.8 us
    ppermute x8, waiting for transfers between devices, exchange(): return lax.ppermute(array, axis, [(i, i ^ bit) for i in range(size)])  41.3 us
    pallas_call x1, Pallas kernels, down_product(): pl.pallas_call(down_kernel, grid=(width // cols,), in_specs=[pl.BlockSpec...  40.7 us
    pallas_call x1, Pallas kernels, input_product(): pl.pallas_call(input_kernel, grid=(width // cols,), in_specs=[grad, grad,...  36.6 us
    ppermute x8, starting transfers between devices, exchange(): return lax.ppermute(array, axis, [(i, i ^ bit) for i in range(size)])  8.58 us
  transfers between devices with their start and end apart: 12, of which 9 were waited for; matrix products, arithmetic and copies ran while one was open for 2% of the time, Pallas kernels for 46%

commit v1 on v0

v1 whole, which is shorter than its diff:
```python
import functools
import math

import jax
import jax.numpy as jnp
from jax import lax
from jax.experimental import pallas as pl
from jax.experimental.pallas import tpu as pltpu
from jax.sharding import PartitionSpec as P

LANES = 128
SUB = 16
ENTRIES = 16
F32 = jnp.float32
BF16 = jnp.bfloat16
LOOKUP = lax.GatherDimensionNumbers(
    offset_dims=(), collapsed_slice_dims=(0,), start_index_map=(0,),
    operand_batching_dims=(1,), start_indices_batching_dims=(1,),
)


def divisor(size, most, unit=LANES):
    best = unit
    for cand in range(unit, most + 1, unit):
        if size % cand == 0:
            best = cand
    return best


def cost(flops, nbytes):
    return pl.CostEstimate(flops=int(flops), bytes_accessed=int(nbytes), transcendentals=0)


def look_up(table, index):
    return lax.gather(
        table, index[..., None], LOOKUP, (1, 1), mode=lax.GatherScatterMode.PROMISE_IN_BOUNDS
    )


def nibbles(words):
    low = jnp.bitwise_and(words.astype(jnp.int16), jnp.int16(15))
    return low, jnp.right_shift(words, 4).astype(jnp.int16)


def lane_chunks(cols):
    return [slice(c * LANES, (c + 1) * LANES) for c in range(cols // LANES)]


def tables_of(table_ref):
    return [table_ref[:, lanes].astype(BF16) for lanes in lane_chunks(table_ref.shape[1])]


def decode_block(idx_ref, tables, i, half):
    columns = []
    for lanes, table in zip(lane_chunks(idx_ref.shape[1]), tables):
        pieces = [[], []]
        for step in range(half // SUB):
            row = pl.multiple_of(i * half + step * SUB, SUB)
            for piece, index in zip(pieces, nibbles(idx_ref[pl.ds(row, SUB), lanes])):
                piece.append(look_up(table, index))
        columns.append(jnp.concatenate(pieces[0] + pieces[1], axis=0))
    return jnp.concatenate(columns, axis=1)


def contract_cols(left, right):
    return lax.dot_general(left, right, (((1,), (1,)), ((), ())), preferred_element_type=F32)


def grouped(count, most, body):
    size = min(count, most)

    def step(j, carry):
        body(j * size, size)
        return carry

    lax.fori_loop(0, count // size, step, 0)
    if count % size:
        body(count - count % size, count % size)


def up_kernel(x_ref, idx_ref, table_ref, pre_ref):
    count, _, block = x_ref.shape
    tables = tables_of(table_ref)
    pre_ref[...] = jnp.zeros_like(pre_ref)

    def body(first, n):
        pre_ref[...] += sum(
            jnp.dot(
                x_ref[first + k], decode_block(idx_ref, tables, first + k, block // 2), preferred_element_type=F32
            )
            for k in range(n)
        )

    grouped(count, 8, body)


def up_product(x_blocks, index, lookup):
    count, tokens, block = x_blocks.shape
    words, width = index.shape
    cols = divisor(width, 256)
    return pl.pallas_call(
        up_kernel,
        grid=(width // cols,),
        in_specs=[
            pl.BlockSpec((count, tokens, block), lambda j: (0, 0, 0)),
            pl.BlockSpec((words, cols), lambda j: (0, j)),
            pl.BlockSpec((ENTRIES, cols), lambda j: (0, j)),
        ],
        out_specs=pl.BlockSpec((tokens, cols), lambda j: (0, j)),
        out_shape=jax.ShapeDtypeStruct((tokens, width), F32),
        cost_estimate=cost(4 * tokens * words * width, 4 * words * width),
        name="up_product",
    )(x_blocks, index, lookup)


def down_kernel(og_ref, idx_ref, table_ref, out_ref):
    count, _, block = out_ref.shape
    tables = tables_of(table_ref)

    @pl.when(pl.program_id(0) == 0)
    def _():
        out_ref[...] = jnp.zeros_like(out_ref)

    def body(first, n):
        for k in range(n):
            out_ref[first + k] += contract_cols(
                og_ref[...], decode_block(idx_ref, tables, first + k, block // 2)
            )

    grouped(count, 3, body)


def down_product(out_grad, index, lookup):
    tokens = out_grad.shape[0]
    words, width = index.shape
    cols = divisor(width, 512)
    block = math.gcd(2 * words, 256)
    count = 2 * words // block
    return pl.pallas_call(
        down_kernel,
        grid=(width // cols,),
        in_specs=[
            pl.BlockSpec((tokens, cols), lambda j: (0, j)),
            pl.BlockSpec((words, cols), lambda j: (0, j)),
            pl.BlockSpec((ENTRIES, cols), lambda j: (0, j)),
        ],
        out_specs=pl.BlockSpec((count, tokens, block), lambda j: (0, 0, 0)),
        out_shape=jax.ShapeDtypeStruct((count, tokens, block), F32),
        cost_estimate=cost(4 * tokens * words * width, 4 * words * width),
        name="down_product",
    )(out_grad, index, lookup)


def signed_sums(sums, value, signs):
    parts = [value]
    for sign in signs:
        parts = parts + [sign * part for part in parts]
    parts = parts[1:]
    return parts if sums is None else [a + b for a, b in zip(sums, parts)]


def write_bins(sums, out_ref, scale):
    step = 1
    while step < ENTRIES:
        mixed = list(sums)
        for k in range(ENTRIES):
            if not k & step:
                mixed[k], mixed[k | step] = sums[k] + sums[k | step], sums[k] - sums[k | step]
        sums = mixed
        step *= 2
    for k in range(ENTRIES):
        out_ref[k : k + 1, :] = sums[k] * (scale / ENTRIES)


def bins_kernel(scale, with_grad, with_start, *refs):
    left_ref, right_ref, total_ref, idx_ref, sign_ref, ones_ref = refs[:6]
    refs = refs[6:]
    if with_grad:
        table_ref, refs = refs[0], refs[1:]
        if with_start:
            start_ref, refs = refs[0], refs[1:]
    out_ref, refs = refs[0], refs[1:]
    if with_grad:
        grad_ref, refs = refs[0], refs[1:]
    acc_ref, values, leaves = refs[0], refs[1:3], refs[3:5]
    count, block, _ = left_ref.shape
    half = block // 2
    cols = idx_ref.shape[1]
    signs = [sign_ref[SUB * b : SUB * b + SUB, :] for b in range(4)]
    if with_grad:
        tables = tables_of(table_ref)

        @pl.when(pl.program_id(0) == 0)
        def _():
            grad_ref[...] = start_ref[...] if with_start else jnp.zeros_like(grad_ref)

    acc_ref[...] = jnp.zeros_like(acc_ref)
    leaves[0][0:SUB, :] = jnp.zeros((SUB, cols), BF16)
    leaves[1][...] = jnp.zeros_like(leaves[1])

    def make(i, slot):
        values[slot][...] = jnp.dot(left_ref[i], right_ref[...], preferred_element_type=F32)

    def grad(i):
        if with_grad:
            grad_ref[i] += contract_cols(right_ref[...], decode_block(idx_ref, tables, i, half))

    def use(i, slot):
        for lanes in lane_chunks(cols):
            sums = None
            for step in range(half // SUB):
                row = pl.multiple_of(i * half + step * SUB, SUB)
                for parity, index in enumerate(nibbles(idx_ref[pl.ds(row, SUB), lanes])):
                    first = parity * half + step * SUB
                    value = values[slot][first : first + SUB, lanes].astype(BF16)
                    sums = signed_sums(sums, value, [look_up(sign, index) for sign in signs])
            for a, total in enumerate(sums):
                leaves[slot][SUB * (a + 1) : SUB * (a + 2), lanes] = total

    def close(slot):
        acc_ref[...] += jnp.dot(ones_ref[...], leaves[slot][...], preferred_element_type=F32)

    make(0, 0)

    def body(j, carry):
        close(1)
        make(2 * j + 1, 1)
        grad(2 * j)
        grad(2 * j + 1)
        use(2 * j, 0)
        close(0)
        make(2 * j + 2, 0)
        use(2 * j + 1, 1)
        return carry

    lax.fori_loop(0, (count - 1) // 2, body, 0)
    close(1)
    last = count - 1
    if count % 2 == 0:
        make(last, 1)
        grad(last - 1)
        grad(last)
        use(last - 1, 0)
        close(0)
        use(last, 1)
        close(1)
    else:
        grad(last)
        use(last, 0)
        close(0)
    whole = jnp.concatenate(
        [
            jnp.sum(right_ref[:, lanes].astype(F32) * total_ref[...], axis=0, keepdims=True)
            for lanes in lane_chunks(cols)
        ],
        axis=1,
    )
    write_bins([whole] + [acc_ref[k : k + 1, :] for k in range(1, ENTRIES)], out_ref, scale)


def sign_table():
    entry = jnp.arange(ENTRIES)[None, :, None]
    bit = jnp.arange(4)[:, None, None]
    sign = 1 - 2 * jnp.bitwise_and(jnp.right_shift(entry, bit), 1)
    return jnp.broadcast_to(sign, (4, ENTRIES, LANES)).reshape(4 * ENTRIES, LANES).astype(BF16)


def group_ones():
    row = jnp.arange(ENTRIES)[:, None]
    col = jnp.arange(ENTRIES * SUB)[None, :]
    return (row == col // SUB).astype(BF16)


def bins(left, total, right, index, scale, lookup=None, start=None):
    count, block, tokens = left.shape
    words, width = index.shape
    cols = divisor(width, 256)
    with_grad, with_start = lookup is not None, start is not None
    whole3 = pl.BlockSpec((count, tokens, block), lambda j: (0, 0, 0))
    in_specs = [
        pl.BlockSpec((count, block, tokens), lambda j: (0, 0, 0)),
        pl.BlockSpec((tokens, cols), lambda j: (0, j)),
        pl.BlockSpec((tokens, LANES), lambda j: (0, 0)),
        pl.BlockSpec((words, cols), lambda j: (0, j)),
        pl.BlockSpec((4 * ENTRIES, LANES), lambda j: (0, 0)),
        pl.BlockSpec((ENTRIES, ENTRIES * SUB), lambda j: (0, 0)),
    ]
    args = [left, right, total, index, sign_table(), group_ones()]
    out_specs = [pl.BlockSpec((ENTRIES, cols), lambda j: (0, j))]
    out_shape = [jax.ShapeDtypeStruct((ENTRIES, width), F32)]
    scratch = [pltpu.VMEM((ENTRIES, cols), F32)]
    scratch += [pltpu.VMEM((block, cols), F32)] * 2 + [pltpu.VMEM((ENTRIES * SUB, cols), BF16)] * 2
    if with_grad:
        in_specs.append(pl.BlockSpec((ENTRIES, cols), lambda j: (0, j)))
        args.append(lookup)
        if with_start:
            in_specs.append(whole3)
            args.append(start)
        out_specs.append(whole3)
        out_shape.append(jax.ShapeDtypeStruct((count, tokens, block), F32))
    out = pl.pallas_call(
        functools.partial(bins_kernel, scale, with_grad, with_start),
        grid=(width // cols,),
        in_specs=in_specs,
        out_specs=out_specs,
        out_shape=out_shape,
        scratch_shapes=scratch,
        cost_estimate=cost(40 * tokens * words * width, 4 * words * width),
        name="bins_grad" if with_grad else "bins",
    )(*args)
    return out if with_grad else out[0]


def row_totals(array):
    total = jnp.sum(array.astype(F32), axis=1, keepdims=True)
    return jnp.broadcast_to(total, (array.shape[0], LANES))


def pairing(block, dtype):
    row = jnp.arange(block)[:, None]
    col = jnp.arange(block)[None, :]
    half = block // 2
    return (row == 2 * (col % half) + col // half).astype(dtype)


def to_blocks(array):
    rows, cols = array.shape
    block = math.gcd(cols, 256)
    out = lax.dot_general(
        array.reshape(rows, cols // block, block), pairing(block, array.dtype), (((2,), (0,)), ((), ())),
        preferred_element_type=F32,
    )
    return jnp.swapaxes(out.astype(array.dtype), 0, 1)


def from_blocks(blocks):
    count, rows, block = blocks.shape
    out = lax.dot_general(
        blocks, pairing(block, blocks.dtype), (((2,), (1,)), ((), ())), precision=lax.Precision.HIGHEST,
        preferred_element_type=F32,
    )
    return jnp.swapaxes(out, 0, 1).reshape(rows, count * block)


def shift(array, axis, size, by):
    return lax.ppermute(array, axis, [(i, i ^ by) for i in range(size)])


def axis_bits(size):
    return [1 << i for i in range(size.bit_length() - 1)]


def power_of_two(size):
    return size & (size - 1) == 0


def sum_scatter(array, axis, dim):
    size = lax.axis_size(axis)
    if not power_of_two(size):
        return lax.psum_scatter(array, axis, scatter_dimension=dim, tiled=True)
    me = lax.axis_index(axis)
    shape = array.shape
    rows = shape[dim] // size
    left = size
    for bit in axis_bits(size):
        left //= 2
        pairs = array.reshape(shape[:dim] + (left, 2, rows) + shape[dim + 1 :])
        mine = jnp.bitwise_and(me // bit, 1)
        sent = lax.dynamic_index_in_dim(pairs, 1 - mine, dim + 1, False).astype(BF16)
        kept = lax.dynamic_index_in_dim(pairs, mine, dim + 1, False)
        array = kept + shift(sent, axis, size, bit).astype(F32)
    return array.reshape(shape[:dim] + (rows,) + shape[dim + 1 :])


def sum_scatter_direct(array, axis, dim):
    size = lax.axis_size(axis)
    if not power_of_two(size):
        return lax.psum_scatter(array, axis, scatter_dimension=dim, tiled=True), []
    me = lax.axis_index(axis)
    rows = array.shape[dim] // size
    total = lax.dynamic_slice_in_dim(array, me * rows, rows, dim)
    sent = [
        shift(
            lax.dynamic_slice_in_dim(array, jnp.bitwise_xor(me, by) * rows, rows, dim).astype(BF16), axis, size, by
        )
        for by in range(1, size)
    ]
    return total, sent


def gather(array, axis):
    size = lax.axis_size(axis)
    if not power_of_two(size):
        return lax.all_gather(array, axis, axis=0, tiled=True)
    me = lax.axis_index(axis)
    rows, cols = array.shape
    array = array[None]
    for bit in reversed(axis_bits(size)):
        other = shift(array, axis, size, bit)
        first = jnp.bitwise_and(me // bit, 1) == 0
        low, high = jnp.where(first, array, other), jnp.where(first, other, array)
        array = jnp.stack([low, high], axis=1).reshape(-1, rows, cols)
    return array.reshape(size * rows, cols)


def sum_all(array, axis):
    size = lax.axis_size(axis)
    if not power_of_two(size):
        return lax.psum(array, axis)
    for bit in axis_bits(size):
        array = array + shift(array, axis, size, bit)
    return array


def after(array, *done):
    return lax.optimization_barrier((array, *done))[0]


def local_hidden(pre_gate, pre_up, hidden_grad):
    sig_gate = jax.nn.sigmoid(pre_gate)
    silu_gate = pre_gate * sig_gate
    activ = (silu_gate * pre_up).astype(BF16)
    gate_grad = (hidden_grad * pre_up * sig_gate * (1.0 + pre_gate * (1.0 - sig_gate))).astype(BF16)
    up_grad = (hidden_grad * silu_gate).astype(BF16)
    return activ, gate_grad, up_grad


def shards(inputs, out_grad, gate_index, up_index, down_index, gate_table, up_table, down_table):
    tokens = inputs.shape[0]
    scale = 1.0 / tokens
    hid_blocks = down_product(out_grad, down_index, down_table)
    hid = sum_scatter(hid_blocks, "inp", 1)
    x_blocks = to_blocks(inputs)
    x_turned = jnp.swapaxes(x_blocks, 1, 2)
    x_total = row_totals(inputs)
    pre_gate = up_product(x_blocks, gate_index, after(gate_table, hid_blocks))
    gate_share = sum_scatter(pre_gate, "inp", 0)
    pre_up = up_product(x_blocks, up_index, after(up_table, pre_gate))
    up_share = sum_scatter(pre_up, "inp", 0)
    activ, gate_grad, up_grad = local_hidden(gate_share, up_share, from_blocks(hid))
    gate_grad = gather(gate_grad, "inp")
    up_grad = gather(after(up_grad, gate_grad), "inp")
    acts = gather(after(activ, gate_grad), "inp")
    gate_part, din_blocks = bins(x_turned, x_total, gate_grad, gate_index, scale, gate_table)
    up_part, din_blocks = bins(
        x_turned, x_total, after(up_grad, gate_part), up_index, scale, up_table, din_blocks
    )
    gate_sum = sum_all(gate_part, "inp")
    din_own, din_sent = sum_scatter_direct(din_blocks, "hid", 1)
    acts = after(acts, up_part)
    down_part = bins(
        jnp.swapaxes(to_blocks(acts), 1, 2), row_totals(acts), out_grad, down_index, scale
    )
    up_sum = sum_all(up_part, "inp")
    down_sum = sum_all(down_part, "hid")
    din = din_own
    for piece in din_sent:
        din = din + after(piece, down_part).astype(F32)
    input_grad = from_blocks(din).astype(BF16)
    return input_grad, gate_sum, up_sum, down_sum


def solution(mesh):
    in_specs = (
        P(None, "inp"),
        P(None, "inp"),
        P("inp", "hid"),
        P("inp", "hid"),
        P("hid", "inp"),
        P(None, "hid"),
        P(None, "hid"),
        P(None, "inp"),
    )
    out_specs = (P("hid", "inp"), P(None, "hid"), P(None, "hid"), P(None, "inp"))
    return jax.shard_map(shards, mesh=mesh, in_specs=in_specs, out_specs=out_specs, check_vma=False)
```

time: 428 us -> 332 us (0.78)
  Pallas kernels: 339 us -> 229 us
  starting transfers between devices: 8.75 us -> 35.2 us
  waiting for transfers between devices: 49.7 us -> 35.7 us
  between operations: 14 us -> 0.98 us
  local copies, waits for them, and re-layouts: 8.1 us -> 15.1 us
  other arithmetic: 4.14 us -> 9.94 us
    pallas_call x4 -> x3, Pallas kernels: 228 us -> 172 us  [bins(): pl.pallas_call(functools.partial(bins_kernel, scale, with_grad, with_star...]
    pallas_call x2, Pallas kernels: 70.8 us -> 38.2 us  [up_product(): pl.pallas_call(up_kernel, grid=(width // cols,), in_specs=[pl.BlockSpec((...]
    ppermute x8 -> x26, starting transfers between devices: 8.58 us -> 35.2 us  [shift(): return lax.ppermute(array, axis, [(i, i ^ by) for i in range(size)])]
    pallas_call x1, Pallas kernels: 40.7 us -> 18.6 us  [down_product(): pl.pallas_call(down_kernel, grid=(width // cols,), in_specs=[pl.BlockSpec...]
    psum x1 -> x0, waiting for transfers between devices: 8.39 us -> none  [shards(): down_sum = lax.psum(after(down_part, din), 'hid')]
    convert_element_type x0 -> x7, local copies, waits for them, and re-layouts: none -> 7.26 us  [the longest x6 6.45 us: sum_scatter(): lax.dynamic_index_in_dim(pairs, 1 - mine, dim + 1, False).astype(BF16)]
    ppermute x8 -> x26, waiting for transfers between devices: 41.3 us -> 35.7 us  [shift(): return lax.ppermute(array, axis, [(i, i ^ by) for i in range(size)])]
    add x3 -> x10, other arithmetic: 1.13 us -> 6.51 us  [the longest x3 3.31 us: sum_scatter(): array = kept + shift(sent, axis, size, bit).astype(F32)]
  transfers between devices with their start and end apart: 12 -> 26, of which waited for: 9 -> 12; matrix products, arithmetic and copies ran while one was open for 2% -> 6% of each run, Pallas kernels for 46% -> 17%
where the time goes in v1:
time: 332 us; the launch traced here: 331 us
  Pallas kernels  229 us (69%)
  waiting for transfers between devices  35.7 us (11%)
  starting transfers between devices  35.2 us (11%)
  local copies, waits for them, and re-layouts  15.1 us (5%)
  other arithmetic  9.94 us (3%)
  matrix products  5.12 us (2%)
    pallas_call x3, Pallas kernels, bins(): pl.pallas_call(functools.partial(bins_kernel, scale, with_grad, with_star...  172 us
    pallas_call x2, Pallas kernels, up_product(): pl.pallas_call(up_kernel, grid=(width // cols,), in_specs=[pl.BlockSpec((...  38.2 us
    ppermute x26, waiting for transfers between devices, shift(): return lax.ppermute(array, axis, [(i, i ^ by) for i in range(size)])  35.7 us
    ppermute x26, starting transfers between devices, shift(): return lax.ppermute(array, axis, [(i, i ^ by) for i in range(size)])  35.2 us
    pallas_call x1, Pallas kernels, down_product(): pl.pallas_call(down_kernel, grid=(width // cols,), in_specs=[pl.BlockSpec...  18.6 us
  transfers between devices with their start and end apart: 26, of which 12 were waited for; matrix products, arithmetic and copies ran while one was open for 6% of the time, Pallas kernels for 17%

profile of v1, /device:TPU:0, one launch (start us, length us, event | category | flops | bytes accessed | tf_op | source)
XLA Modules:
  0.0 331.1 jit_solution(9081039338247623588)
XLA Ops:
  0.6 1.7 convolution_convert_fusion
  3.7 18.6 %down_product.1 = f32[13,128,256]{2,1,0:T(8,128)} custom-call(bf16[128,4096]{1,0:T(8,128)(2,1)} %refs_1_.1, s32[1664,4096]{1,0:T(8,128)} %refs_3_.5, f32[16,4096]{1,0:T(8,128)} %table_ref.1), custom_call_target="tpu_custom_call" | custom-call | flops 3489660928 | bytes 27262976 | tf_op jit(solution)/shard_map/down_product/pallas_call | solution.py:139
  22.3 19.1 %up_product.2 = f32[128,3328]{1,0:T(8,128)} custom-call(bf16[16,128,256]{2,1,0:T(8,128)(2,1)} %copy.28.x_ref, s32[2048,3328]{1,0:T(8,128)} %refs_3_.3, f32[16,3328]{1,0:T(8,128)} %refs_6_.2), custom_call_target="tpu_custom_call" | custom-call | flops 3489660928 | bytes 27262976 | tf_op jit(solution)/shard_map/up_product/pallas_call | solution.py:101
  41.4 19.1 %up_product.3 = f32[128,3328]{1,0:T(8,128)} custom-call(bf16[16,128,256]{2,1,0:T(8,128)(2,1)} %copy.28.x_ref, s32[2048,3328]{1,0:T(8,128)} %refs_3_.4, f32[16,3328]{1,0:T(8,128)} %refs_6_.3), custom_call_target="tpu_custom_call" | custom-call | flops 3489660928 | bytes 27262976 | tf_op jit(solution)/shard_map/up_product/pallas_call | solution.py:101
  60.5 2.1 fusion.6
  63.9 2.0 fusion.4
  66.5 1.6 convert_reduce_fusion
  70.0 2.5 collective-permute-start.5
  75.6 2.0 collective-permute-start.3
  77.6 5.8 %collective-permute-done.1 = bf16[13,1,32,256]{3,2,0,1:T(8,128)(2,1)S(1)} collective-permute-done((bf16[13,1,32,256]{3,2,0,1:T(8,128)(2,1)S(1)}, bf16[13,1,32,256]{3,2,0,1:T(8,128)(2,1)S(1)}, u32[]{:S(2)}, u32[]{:S(2)}) %collective-permute-start.1) | collective-permute-done | bytes 213024 | tf_op jit(solution)/shard_map/ppermute | solution.py:346
  84.1 3.6 %collective-permute-done.3 = bf16[1,32,3328]{2,1,0:T(8,128)(2,1)S(1)} collective-permute-done((bf16[1,32,3328]{2,1,0:T(8,128)(2,1)}, bf16[1,32,3328]{2,1,0:T(8,128)(2,1)S(1)}, u32[]{:S(2)}, u32[]{:S(2)}) %collective-permute-start.3) | collective-permute-done | bytes 213024 | tf_op jit(solution)/shard_map/ppermute | solution.py:346
  88.0 1.8 collective-permute-start.6
  90.4 4.7 %collective-permute-done.6 = bf16[1,32,3328]{2,1,0:T(8,128)(2,1)S(1)} collective-permute-done((bf16[1,32,3328]{2,1,0:T(8,128)(2,1)S(1)}, bf16[1,32,3328]{2,1,0:T(8,128)(2,1)S(1)}, u32[]{:S(2)}, u32[]{:S(2)}) %collective-permute-start.6) | collective-permute-done | bytes 213024 | tf_op jit(solution)/shard_map/ppermute | solution.py:346
  95.5 1.6 collective-permute-done.7
  98.2 1.5 collective-permute-start.11
  101.6 56.4 %bins_grad.2 = (f32[16,3328]{1,0:T(8,128)}, f32[16,128,256]{2,1,0:T(8,128)}) custom-call(bf16[16,256,128]{2,1,0:T(8,128)(2,1)} %bitcast.132, bf16[128,3328]{1,0:T(8,128)(2,1)} %bitcast.141, f32[128,128]{1,0:T(8,128)} %broadcast_in_dim.15.refs_2_, s32[2048,3328]{1,0:T(8,128)} %refs_3_.3, bf16[64,128]{1,0:T(8,128)(2,1)} %broadcast_in_dim.16.refs_4_, ...), custom_call_target="tpu_custom_call" | custom-call | flops 34896609280 | bytes 27262976 | tf_op jit(solution)/shard_map/bins_grad/pallas_call | solution.py:301
  161.4 57.2 %bins_grad.3 = (f32[16,3328]{1,0:T(8,128)}, f32[16,128,256]{2,1,0:T(8,128)}) custom-call(bf16[16,256,128]{2,1,0:T(8,128)(2,1)} %bitcast.133, bf16[128,3328]{1,0:T(8,128)(2,1)} %bitcast.140, f32[128,128]{1,0:T(8,128)} %broadcast_in_dim.15.refs_2_, s32[2048,3328]{1,0:T(8,128)} %refs_3_.4, bf16[64,128]{1,0:T(8,128)(2,1)} %broadcast_in_dim.16.refs_4_, ...), custom_call_target="tpu_custom_call" | custom-call | flops 34896609280 | bytes 27262976 | tf_op jit(solution)/shard_map/bins_grad/pallas_call | solution.py:301
  219.4 1.4 fusion.refs_0_
  221.5 58.7 %bins.1 = f32[16,4096]{1,0:T(8,128)} custom-call(bf16[13,256,128]{2,1,0:T(8,128)(2,1)} %fusion.refs_0_, bf16[128,4096]{1,0:T(8,128)(2,1)} %refs_1_.1, f32[128,128]{1,0:T(8,128)} %broadcast_in_dim.18.refs_2_, s32[1664,4096]{1,0:T(8,128)} %refs_3_.5, bf16[64,128]{1,0:T(8,128)(2,1)} %broadcast_in_dim.16.refs_4_, bf16[16,256]{1,0:T(8,128)(2,1)} %fusion.41.refs_5_), custom_call_target="tpu_custom_call" | custom-call | flops 34896609280 | bytes 27262976 | tf_op jit(solution)/shard_map/bins/pallas_call | solution.py:301
  280.2 1.4 collective-permute-start.23
  281.6 1.5 collective-permute-done.19
  283.1 1.6 collective-permute-start.20
  284.7 4.0 %collective-permute-done.23 = f32[16,4096]{1,0:T(8,128)S(1)} collective-permute-done((f32[16,4096]{1,0:T(8,128)}, f32[16,4096]{1,0:T(8,128)S(1)}, u32[]{:S(2)}, u32[]{:S(2)}) %collective-permute-start.23) | collective-permute-done | bytes 262176 | tf_op jit(solution)/shard_map/ppermute | solution.py:346
  289.7 1.6 collective-permute-start.24
  292.1 3.4 %collective-permute-start.18 = (bf16[16,16,256]{2,1,0:T(8,128)(2,1)S(1)}, bf16[16,16,256]{2,1,0:T(8,128)(2,1)S(1)}, u32[]{:S(2)}, u32[]{:S(2)}) collective-permute-start(bf16[16,16,256]{2,1,0:T(8,128)(2,1)S(1)} %get-tuple-element.39), channel_id=1, source_target_pairs={{0,7},{1,6},{2,5},{3,4},{4,3},{5,2},{6,1},{7,0},{8,15},{9,14},{10,... | collective-permute-start | bytes 393224 | tf_op jit(solution)/shard_map/ppermute | solution.py:346
  297.6 7.1 %collective-permute-done.18 = bf16[16,16,256]{2,1,0:T(8,128)(2,1)S(1)} collective-permute-done((bf16[16,16,256]{2,1,0:T(8,128)(2,1)S(1)}, bf16[16,16,256]{2,1,0:T(8,128)(2,1)S(1)}, u32[]{:S(2)}, u32[]{:S(2)}) %collective-permute-start.18) | collective-permute-done | bytes 131104 | tf_op jit(solution)/shard_map/ppermute | solution.py:346
  304.8 6.9 %collective-permute-start.15 = (bf16[16,16,256]{2,1,0:T(8,128)(2,1)S(1)}, bf16[16,16,256]{2,1,0:T(8,128)(2,1)S(1)}, u32[]{:S(2)}, u32[]{:S(2)}) collective-permute-start(bf16[16,16,256]{2,1,0:T(8,128)(2,1)S(1)} %get-tuple-element.42), channel_id=1, source_target_pairs={{0,4},{1,5},{2,6},{3,7},{4,0},{5,1},{6,2},{7,3},{8,12},{9,13},{10,... | collective-permute-start | bytes 393224 | tf_op jit(solution)/shard_map/ppermute | solution.py:346
  312.6 3.1 collective-permute-done.16
  316.6 4.7 %collective-permute-start.25 = (f32[16,4096]{1,0:T(8,128)S(1)}, f32[16,4096]{1,0:T(8,128)S(1)}, u32[]{:S(2)}, u32[]{:S(2)}) collective-permute-start(f32[16,4096]{1,0:T(8,128)S(1)} %add.209), channel_id=1, source_target_pairs={{0,4},{1,5},{2,6},{3,7},{4,0},{5,1},{6,2},{7,3},{8,12},{9,13},{10,... | collective-permute-start | bytes 786440 | tf_op jit(solution)/shard_map/ppermute | solution.py:346
  322.1 1.5 collective-permute-start.22
  324.6 1.6 fusion.1
  328.6 1.8 collective-permute-done.25
  (105 shorter events, 28.5 us)
Async XLA Ops:
  2.4 19.9 %copy-start.5 = (bf16[256,128,16]{1,0,2:T(8,128)(2,1)}, bf16[256,128,16]{1,0,2:T(8,128)(2,1)S(1)}, u32[]{:S(2)}) copy-start(bf16[256,128,16]{1,0,2:T(8,128)(2,1)S(1)} %convolution_convert_fusion) | copy-start | bytes 3145732
  41.4 21.7 %copy-start = (f32[128,3328]{1,0:T(8,128)S(1)}, f32[128,3328]{1,0:T(8,128)}, u32[]{:S(2)}) copy-start(f32[128,3328]{1,0:T(8,128)} %up_product.2) | copy-start | bytes 5111812
  62.6 5.5 %collective-permute-start.4 = (bf16[2,32,3328]{2,1,0:T(8,128)(2,1)}, bf16[2,32,3328]{2,1,0:T(8,128)(2,1)}, u32[]{:S(2)}, u32[]{:S(2)}) collective-permute-start(bf16[2,32,3328]{2,1,0:T(8,128)(2,1)} %fusion.6), channel_id=1, source_target_pairs={{0,8},{8,0},{16,24},{24,16},{1,9},{9,1},{17,25},{25,17},{2,10},{10... | collective-permute-start | bytes 1277960 | tf_op jit(solution)/shard_map/ppermute | solution.py:346
  63.9 9.9 %collective-permute-start.2 = (bf16[2,32,3328]{2,1,0:T(8,128)(2,1)}, bf16[2,32,3328]{2,1,0:T(8,128)(2,1)}, u32[]{:S(2)}, u32[]{:S(2)}) collective-permute-start(bf16[2,32,3328]{2,1,0:T(8,128)(2,1)} %fusion.5), channel_id=1, source_target_pairs={{0,8},{8,0},{16,24},{24,16},{1,9},{9,1},{17,25},{25,17},{2,10},{10... | collective-permute-start | bytes 1277960 | tf_op jit(solution)/shard_map/ppermute | solution.py:346
  65.9 6.6 %collective-permute-start = (bf16[13,2,32,256]{3,2,0,1:T(8,128)(2,1)}, bf16[13,2,32,256]{3,2,0,1:T(8,128)(2,1)}, u32[]{:S(2)}, u32[]{:S(2)}) collective-permute-start(bf16[13,2,32,256]{3,2,0,1:T(8,128)(2,1)} %fusion.4), channel_id=1, source_target_pairs={{0,8},{8,0},{16,24},{24,16},{1,9},{9,1},{17,25},{25,17},{2,10},{10... | collective-permute-start | bytes 1277960 | tf_op jit(solution)/shard_map/ppermute | solution.py:346
  70.0 14.1 %collective-permute-start.5 = (bf16[1,32,3328]{2,1,0:T(8,128)(2,1)}, bf16[1,32,3328]{2,1,0:T(8,128)(2,1)S(1)}, u32[]{:S(2)}, u32[]{:S(2)}) collective-permute-start(bf16[1,32,3328]{2,1,0:T(8,128)(2,1)} %dynamic-slice_convert_fusion), channel_id=1, source_target_pairs={{0,16},{8,24},{16,0},{24,8},{1,17},{9,25},{17,1},{25,9},{2,18},{10... | collective-permute-start | bytes 638984 | tf_op jit(solution)/shard_map/ppermute | solution.py:346
  73.7 9.7 %collective-permute-start.1 = (bf16[13,1,32,256]{3,2,0,1:T(8,128)(2,1)S(1)}, bf16[13,1,32,256]{3,2,0,1:T(8,128)(2,1)S(1)}, u32[]{:S(2)}, u32[]{:S(2)}) collective-permute-start(bf16[13,1,32,256]{3,2,0,1:T(8,128)(2,1)S(1)} %dynamic-slice_convert_fusion.2), channel_id=1, source_target_pairs={{0,16},{8,24},{16,0},{24,8},{1,17},{9,25},{17,1},{25,9},{2,18},{10... | collective-permute-start | bytes 638984 | tf_op jit(solution)/shard_map/ppermute | solution.py:346
  75.6 12.2 %collective-permute-start.3 = (bf16[1,32,3328]{2,1,0:T(8,128)(2,1)}, bf16[1,32,3328]{2,1,0:T(8,128)(2,1)S(1)}, u32[]{:S(2)}, u32[]{:S(2)}) collective-permute-start(bf16[1,32,3328]{2,1,0:T(8,128)(2,1)} %dynamic-slice_convert_fusion.1), channel_id=1, source_target_pairs={{0,16},{8,24},{16,0},{24,8},{1,17},{9,25},{17,1},{25,9},{2,18},{10... | collective-permute-start | bytes 638984 | tf_op jit(solution)/shard_map/ppermute | solution.py:346
  88.0 7.2 %collective-permute-start.6 = (bf16[1,32,3328]{2,1,0:T(8,128)(2,1)S(1)}, bf16[1,32,3328]{2,1,0:T(8,128)(2,1)S(1)}, u32[]{:S(2)}, u32[]{:S(2)}) collective-permute-start(bf16[1,32,3328]{2,1,0:T(8,128)(2,1)S(1)} %multiply_convert_fusion), channel_id=1, source_target_pairs={{0,16},{8,24},{16,0},{24,8},{1,17},{9,25},{17,1},{25,9},{2,18},{10... | collective-permute-start | bytes 638984 | tf_op jit(solution)/shard_map/ppermute | solution.py:346
  95.2 1.8 collective-permute-start.7
  98.2 59.9 %collective-permute-start.11 = (bf16[1,32,3328]{2,1,0:T(8,128)(2,1)S(1)}, bf16[1,32,3328]{2,1,0:T(8,128)(2,1)S(1)}, u32[]{:S(2)}, u32[]{:S(2)}) collective-permute-start(bf16[1,32,3328]{2,1,0:T(8,128)(2,1)S(1)} %bitcast.138), channel_id=1, source_target_pairs={{0,16},{8,24},{16,0},{24,8},{1,17},{9,25},{17,1},{25,9},{2,18},{10... | collective-permute-start | bytes 638984 | tf_op jit(solution)/shard_map/ppermute | solution.py:346
  99.6 58.4 %collective-permute-start.8 = (bf16[1,32,3328]{2,1,0:T(8,128)(2,1)S(1)}, bf16[1,32,3328]{2,1,0:T(8,128)(2,1)S(1)}, u32[]{:S(2)}, u32[]{:S(2)}) collective-permute-start(bf16[1,32,3328]{2,1,0:T(8,128)(2,1)S(1)} %bitcast.139), channel_id=1, source_target_pairs={{0,16},{8,24},{16,0},{24,8},{1,17},{9,25},{17,1},{25,9},{2,18},{10... | collective-permute-start | bytes 638984 | tf_op jit(solution)/shard_map/ppermute | solution.py:346
  158.2 1.8 collective-permute-start.9
  158.3 2.9 collective-permute-start.12
  221.5 60.1 %copy-start.8 = (f32[16,3328]{1,0:T(8,128)S(1)}, f32[16,3328]{1,0:T(8,128)}, u32[]{:S(2)}) copy-start(f32[16,3328]{1,0:T(8,128)} %get-tuple-element.24) | copy-start | bytes 638980
  221.5 69.8 %copy-start.6 = (f32[16,128,256]{2,1,0:T(8,128)S(1)}, f32[16,128,256]{2,1,0:T(8,128)}, u32[]{:S(2)}) copy-start(f32[16,128,256]{2,1,0:T(8,128)} %get-tuple-element.27) | copy-start | bytes 6291460
  280.2 15.3 %copy-start.7 = (f32[16,3328]{1,0:T(8,128)S(1)}, f32[16,3328]{1,0:T(8,128)}, u32[]{:S(2)}) copy-start(f32[16,3328]{1,0:T(8,128)} %get-tuple-element.29) | copy-start | bytes 638980
  280.2 8.6 %collective-permute-start.23 = (f32[16,4096]{1,0:T(8,128)}, f32[16,4096]{1,0:T(8,128)S(1)}, u32[]{:S(2)}, u32[]{:S(2)}) collective-permute-start(f32[16,4096]{1,0:T(8,128)} %bins.1), channel_id=1, source_target_pairs={{0,1},{1,0},{2,3},{3,2},{4,5},{5,4},{6,7},{7,6},{8,9},{9,8},{10,11... | collective-permute-start | bytes 786440 | tf_op jit(solution)/shard_map/ppermute | solution.py:346
  281.6 1.5 collective-permute-start.19
  283.1 13.8 %collective-permute-start.20 = (f32[16,3328]{1,0:T(8,128)S(1)}, f32[16,3328]{1,0:T(8,128)S(1)}, u32[]{:S(2)}, u32[]{:S(2)}) collective-permute-start(f32[16,3328]{1,0:T(8,128)S(1)} %add.204), channel_id=1, source_target_pairs={{0,16},{8,24},{16,0},{24,8},{1,17},{9,25},{17,1},{25,9},{2,18},{10... | collective-permute-start | bytes 638984 | tf_op jit(solution)/shard_map/ppermute | solution.py:346
  289.7 26.0 %collective-permute-start.24 = (f32[16,4096]{1,0:T(8,128)S(1)}, f32[16,4096]{1,0:T(8,128)S(1)}, u32[]{:S(2)}, u32[]{:S(2)}) collective-permute-start(f32[16,4096]{1,0:T(8,128)S(1)} %add.208), channel_id=1, source_target_pairs={{0,2},{1,3},{2,0},{3,1},{4,6},{5,7},{6,4},{7,5},{8,10},{9,11},{10,... | collective-permute-start | bytes 786440 | tf_op jit(solution)/shard_map/ppermute | solution.py:346
  292.1 12.6 %collective-permute-start.18 = (bf16[16,16,256]{2,1,0:T(8,128)(2,1)S(1)}, bf16[16,16,256]{2,1,0:T(8,128)(2,1)S(1)}, u32[]{:S(2)}, u32[]{:S(2)}) collective-permute-start(bf16[16,16,256]{2,1,0:T(8,128)(2,1)S(1)} %get-tuple-element.39), channel_id=1, source_target_pairs={{0,7},{1,6},{2,5},{3,4},{4,3},{5,2},{6,1},{7,0},{8,15},{9,14},{10,... | collective-permute-start | bytes 393224 | tf_op jit(solution)/shard_map/ppermute | solution.py:346
  295.5 21.1 %collective-permute-start.21 = (f32[16,3328]{1,0:T(8,128)S(1)}, f32[16,3328]{1,0:T(8,128)S(1)}, u32[]{:S(2)}, u32[]{:S(2)}) collective-permute-start(f32[16,3328]{1,0:T(8,128)S(1)} %copy-done.7), channel_id=1, source_target_pairs={{0,8},{8,0},{16,24},{24,16},{1,9},{9,1},{17,25},{25,17},{2,10},{10... | collective-permute-start | bytes 638984 | tf_op jit(solution)/shard_map/ppermute | solution.py:346
  295.5 16.2 %collective-permute-start.17 = (bf16[16,16,256]{2,1,0:T(8,128)(2,1)S(1)}, bf16[16,16,256]{2,1,0:T(8,128)(2,1)S(1)}, u32[]{:S(2)}, u32[]{:S(2)}) collective-permute-start(bf16[16,16,256]{2,1,0:T(8,128)(2,1)S(1)} %get-tuple-element.40), channel_id=1, source_target_pairs={{0,6},{1,7},{2,4},{3,5},{4,2},{5,3},{6,0},{7,1},{8,14},{9,15},{10,... | collective-permute-start | bytes 393224 | tf_op jit(solution)/shard_map/ppermute | solution.py:346
  296.9 18.8 %collective-permute-start.16 = (bf16[16,16,256]{2,1,0:T(8,128)(2,1)S(1)}, bf16[16,16,256]{2,1,0:T(8,128)(2,1)S(1)}, u32[]{:S(2)}, u32[]{:S(2)}) collective-permute-start(bf16[16,16,256]{2,1,0:T(8,128)(2,1)S(1)} %get-tuple-element.41), channel_id=1, source_target_pairs={{0,5},{1,4},{2,7},{3,6},{4,1},{5,0},{6,3},{7,2},{8,13},{9,12},{10,... | collective-permute-start | bytes 393224 | tf_op jit(solution)/shard_map/ppermute | solution.py:346
  304.8 16.6 %copy-start.9 = (bf16[16,16,256]{2,1,0:T(8,128)(2,1)}, bf16[16,16,256]{2,1,0:T(8,128)(2,1)S(1)}, u32[]{:S(2)}) copy-start(bf16[16,16,256]{2,1,0:T(8,128)(2,1)S(1)} %collective-permute-done.18) | copy-start | bytes 393220
  304.8 16.6 %collective-permute-start.15 = (bf16[16,16,256]{2,1,0:T(8,128)(2,1)S(1)}, bf16[16,16,256]{2,1,0:T(8,128)(2,1)S(1)}, u32[]{:S(2)}, u32[]{:S(2)}) collective-permute-start(bf16[16,16,256]{2,1,0:T(8,128)(2,1)S(1)} %get-tuple-element.42), channel_id=1, source_target_pairs={{0,4},{1,5},{2,6},{3,7},{4,0},{5,1},{6,2},{7,3},{8,12},{9,13},{10,... | collective-permute-start | bytes 393224 | tf_op jit(solution)/shard_map/ppermute | solution.py:346
  311.7 12.6 %collective-permute-start.14 = (bf16[16,16,256]{2,1,0:T(8,128)(2,1)}, bf16[16,16,256]{2,1,0:T(8,128)(2,1)}, u32[]{:S(2)}, u32[]{:S(2)}) collective-permute-start(bf16[16,16,256]{2,1,0:T(8,128)(2,1)} %get-tuple-element.43), channel_id=1, source_target_pairs={{0,3},{1,2},{2,1},{3,0},{4,7},{5,6},{6,5},{7,4},{8,11},{9,10},{10,... | collective-permute-start | bytes 393224 | tf_op jit(solution)/shard_map/ppermute | solution.py:346
  315.7 8.9 %collective-permute-start.13 = (bf16[16,16,256]{2,1,0:T(8,128)(2,1)}, bf16[16,16,256]{2,1,0:T(8,128)(2,1)}, u32[]{:S(2)}, u32[]{:S(2)}) collective-permute-start(bf16[16,16,256]{2,1,0:T(8,128)(2,1)} %get-tuple-element.44), channel_id=1, source_target_pairs={{0,2},{1,3},{2,0},{3,1},{4,6},{5,7},{6,4},{7,5},{8,10},{9,11},{10,... | collective-permute-start | bytes 393224 | tf_op jit(solution)/shard_map/ppermute | solution.py:346
  315.7 8.9 %collective-permute-start.10 = (bf16[16,16,256]{2,1,0:T(8,128)(2,1)}, bf16[16,16,256]{2,1,0:T(8,128)(2,1)}, u32[]{:S(2)}, u32[]{:S(2)}) collective-permute-start(bf16[16,16,256]{2,1,0:T(8,128)(2,1)} %get-tuple-element.38), channel_id=1, source_target_pairs={{0,1},{1,0},{2,3},{3,2},{4,5},{5,4},{6,7},{7,6},{8,9},{9,8},{10,11... | collective-permute-start | bytes 393224 | tf_op jit(solution)/shard_map/ppermute | solution.py:346
  316.6 13.7 %collective-permute-start.25 = (f32[16,4096]{1,0:T(8,128)S(1)}, f32[16,4096]{1,0:T(8,128)S(1)}, u32[]{:S(2)}, u32[]{:S(2)}) collective-permute-start(f32[16,4096]{1,0:T(8,128)S(1)} %add.209), channel_id=1, source_target_pairs={{0,4},{1,5},{2,6},{3,7},{4,0},{5,1},{6,2},{7,3},{8,12},{9,13},{10,... | collective-permute-start | bytes 786440 | tf_op jit(solution)/shard_map/ppermute | solution.py:346
  322.1 5.8 %collective-permute-start.22 = (f32[16,3328]{1,0:T(8,128)S(1)}, f32[16,3328]{1,0:T(8,128)S(1)}, u32[]{:S(2)}, u32[]{:S(2)}) collective-permute-start(f32[16,3328]{1,0:T(8,128)S(1)} %add.206), channel_id=1, source_target_pairs={{0,16},{8,24},{16,0},{24,8},{1,17},{9,25},{17,1},{25,9},{2,18},{10... | collective-permute-start | bytes 638984 | tf_op jit(solution)/shard_map/ppermute | solution.py:346
  (7 other events, 47.5 us)

commit v2 on v1

--- a/solution.py
+++ b/solution.py
@@ -159,7 +159,69 @@
     return parts if sums is None else [a + b for a, b in zip(sums, parts)]
 
 
-def write_bins(sums, out_ref, scale):
+def bins_tile(left_ref, right_ref, total_ref, idx_ref, sign_ref, ones_ref, acc_ref, values, leaves, grad):
+    count, block, _ = left_ref.shape
+    half = block // 2
+    cols = idx_ref.shape[1]
+    signs = [sign_ref[SUB * b : SUB * b + SUB, :] for b in range(4)]
+    acc_ref[...] = jnp.zeros_like(acc_ref)
+    leaves[0][0:SUB, :] = jnp.zeros((SUB, cols), BF16)
+    leaves[1][...] = jnp.zeros_like(leaves[1])
+
+    def make(i, slot):
+        values[slot][...] = jnp.dot(left_ref[i], right_ref[...], preferred_element_type=F32)
+
+    def use(i, slot):
+        for lanes in lane_chunks(cols):
+            runs = []
+            sums = None
+            for step in range(half // SUB):
+                row = pl.multiple_of(i * half + step * SUB, SUB)
+                for parity, index in enumerate(nibbles(idx_ref[pl.ds(row, SUB), lanes])):
+                    first = parity * half + step * SUB
+                    value = values[slot][first : first + SUB, lanes].astype(BF16)
+                    sums = signed_sums(sums, value, [look_up(sign, index) for sign in signs])
+                if step % 4 == 3 or step == half // SUB - 1:
+                    runs.append(sums)
+                    sums = None
+            while len(runs) > 1:
+                runs = [[a + b for a, b in zip(*runs[:2])]] + runs[2:]
+            for a, total in enumerate(runs[0]):
+                leaves[slot][SUB * (a + 1) : SUB * (a + 2), lanes] = total
+
+    def close(slot):
+        acc_ref[...] += jnp.dot(ones_ref[...], leaves[slot][...], preferred_element_type=F32)
+
+    make(0, 0)
+
+    def body(j, carry):
+        close(1)
+        make(2 * j + 1, 1)
+        grad(2 * j)
+        grad(2 * j + 1)
+        use(2 * j, 0)
+        close(0)
+        make(jnp.minimum(2 * j + 2, count - 1), 0)
+        use(2 * j + 1, 1)
+        return carry
+
+    lax.fori_loop(0, count // 2, body, 0)
+    close(1)
+    if count % 2:
+        grad(count - 1)
+        use(count - 1, 0)
+        close(0)
+    whole = jnp.concatenate(
+        [
+            jnp.sum(right_ref[:, lanes].astype(F32) * total_ref[...], axis=0, keepdims=True)
+            for lanes in lane_chunks(cols)
+        ],
+        axis=1,
+    )
+    return [whole] + [acc_ref[k : k + 1, :] for k in range(1, ENTRIES)]
+
+
+def entry_sums(sums):
     step = 1
     while step < ENTRIES:
         mixed = list(sums)
@@ -168,94 +230,179 @@
                 mixed[k], mixed[k | step] = sums[k] + sums[k | step], sums[k] - sums[k | step]
         sums = mixed
         step *= 2
-    for k in range(ENTRIES):
-        out_ref[k : k + 1, :] = sums[k] * (scale / ENTRIES)
-
-
-def bins_kernel(scale, with_grad, with_start, *refs):
-    left_ref, right_ref, total_ref, idx_ref, sign_ref, ones_ref = refs[:6]
-    refs = refs[6:]
-    if with_grad:
-        table_ref, refs = refs[0], refs[1:]
-        if with_start:
-            start_ref, refs = refs[0], refs[1:]
-    out_ref, refs = refs[0], refs[1:]
-    if with_grad:
-        grad_ref, refs = refs[0], refs[1:]
-    acc_ref, values, leaves = refs[0], refs[1:3], refs[3:5]
-    count, block, _ = left_ref.shape
-    half = block // 2
+    return sums
+
+
+def grad_kernel(starts, shares, *refs):
+    left_ref, right_ref, total_ref, idx_ref, sign_ref, ones_ref, table_ref = refs[:7]
+    refs = refs[7:]
+    if starts:
+        start_ref, refs = refs[0], refs[1:]
+    out_ref, sum_ref, acc_ref = refs[:3]
+    values, leaves = refs[3:5], refs[5:7]
+    grad_ref = refs[7] if shares else sum_ref
+    count, _, block = grad_ref.shape
+    tables = tables_of(table_ref)
+
+    @pl.when(pl.program_id(0) == 0)
+    def _():
+        grad_ref[...] = start_ref[...] if starts else jnp.zeros_like(grad_ref)
+
+    def grad(i):
+        grad_ref[i] += contract_cols(right_ref[...], decode_block(idx_ref, tables, i, block // 2))
+
+    sums = bins_tile(
+        left_ref, right_ref, total_ref, idx_ref, sign_ref, ones_ref, acc_ref, values, leaves, grad
+    )
+    for k, total in enumerate(entry_sums(sums)):
+        out_ref[k : k + 1, :] = total
+
+    if shares:
+        rows = sum_ref.shape[2]
+
+        @pl.when(pl.program_id(0) == pl.num_programs(0) - 1)
+        def _():
+            for p in range(shares):
+                sum_ref[p] = grad_ref[:, p * rows : (p + 1) * rows, :].astype(BF16)
+
+
+def down_bins_kernel(n_hid, n_inp, *refs):
+    (left_ref, right_ref, total_ref, idx_ref, sign_ref, ones_ref, gate_ref, up_ref, shares_ref) = refs[:9]
+    out_ref, gate_out, up_out, grad_out = refs[9:13]
+    acc_ref, values, leaves = refs[13], refs[14:16], refs[16:18]
+    (own_ref, got_ref, gate_got, up_got, part_ref, part_got, final_ref) = refs[18:25]
+    (own_sem, share_send, share_recv, table_send, table_recv, part_send, part_recv, final_send, final_recv) = refs[25:]
+    step, steps = pl.program_id(0), pl.num_programs(0)
+    hid, inp = lax.axis_index("hid"), lax.axis_index("inp")
     cols = idx_ref.shape[1]
-    signs = [sign_ref[SUB * b : SUB * b + SUB, :] for b in range(4)]
-    if with_grad:
-        tables = tables_of(table_ref)
-
-        @pl.when(pl.program_id(0) == 0)
-        def _():
-            grad_ref[...] = start_ref[...] if with_start else jnp.zeros_like(grad_ref)
-
-    acc_ref[...] = jnp.zeros_like(acc_ref)
-    leaves[0][0:SUB, :] = jnp.zeros((SUB, cols), BF16)
-    leaves[1][...] = jnp.zeros_like(leaves[1])
-
-    def make(i, slot):
-        values[slot][...] = jnp.dot(left_ref[i], right_ref[...], preferred_element_type=F32)
-
-    def grad(i):
-        if with_grad:
-            grad_ref[i] += contract_cols(right_ref[...], decode_block(idx_ref, tables, i, half))
-
-    def use(i, slot):
-        for lanes in lane_chunks(cols):
-            sums = None
-            for step in range(half // SUB):
-                row = pl.multiple_of(i * half + step * SUB, SUB)
-                for parity, index in enumerate(nibbles(idx_ref[pl.ds(row, SUB), lanes])):
-                    first = parity * half + step * SUB
-                    value = values[slot][first : first + SUB, lanes].astype(BF16)
-                    sums = signed_sums(sums, value, [look_up(sign, index) for sign in signs])
-            for a, total in enumerate(sums):
-                leaves[slot][SUB * (a + 1) : SUB * (a + 2), lanes] = total
-
-    def close(slot):
-        acc_ref[...] += jnp.dot(ones_ref[...], leaves[slot][...], preferred_element_type=F32)
-
-    make(0, 0)
-
-    def body(j, carry):
-        close(1)
-        make(2 * j + 1, 1)
-        grad(2 * j)
-        grad(2 * j + 1)
-        use(2 * j, 0)
-        close(0)
-        make(2 * j + 2, 0)
-        use(2 * j + 1, 1)
-        return carry
-
-    lax.fori_loop(0, (count - 1) // 2, body, 0)
-    close(1)
-    last = count - 1
-    if count % 2 == 0:
-        make(last, 1)
-        grad(last - 1)
-        grad(last)
-        use(last - 1, 0)
-        close(0)
-        use(last, 1)
-        close(1)
-    else:
-        grad(last)
-        use(last, 0)
-        close(0)
-    whole = jnp.concatenate(
-        [
-            jnp.sum(right_ref[:, lanes].astype(F32) * total_ref[...], axis=0, keepdims=True)
-            for lanes in lane_chunks(cols)
+    rows = ENTRIES // n_hid
+    peers = [(k, lax.rem(hid + k, n_hid)) for k in range(1, n_hid)]
+    mates = [(k, lax.rem(inp + k, n_inp)) for k in range(1, n_inp)]
+
+    def copies():
+        out = []
+        for k, peer in peers:
+            out.append(pltpu.make_async_remote_copy(
+                src_ref=shares_ref.at[peer], dst_ref=got_ref.at[k - 1], send_sem=share_send.at[k - 1],
+                recv_sem=share_recv.at[k - 1], device_id={"hid": peer}, device_id_type=pl.DeviceIdType.MESH))
+        for k, mate in mates:
+            for t, (src, dst) in enumerate(((gate_ref, gate_got), (up_ref, up_got))):
+                out.append(pltpu.make_async_remote_copy(
+                    src_ref=src, dst_ref=dst.at[k - 1], send_sem=table_send.at[2 * (k - 1) + t],
+                    recv_sem=table_recv.at[2 * (k - 1) + t], device_id={"inp": mate},
+                    device_id_type=pl.DeviceIdType.MESH))
+        return out
+
+    def own_copy():
+        return pltpu.make_async_copy(shares_ref.at[hid], own_ref, own_sem)
+
+    def lanes_of(tile):
+        return pl.ds(pl.multiple_of(tile * cols, LANES), cols)
+
+    def part_copy(tile, k, peer):
+        return pltpu.make_async_remote_copy(
+            src_ref=part_ref.at[peer, :, lanes_of(tile)], dst_ref=part_got.at[k - 1, :, lanes_of(tile)],
+            send_sem=part_send.at[tile, k - 1], recv_sem=part_recv.at[tile, k - 1], device_id={"hid": peer},
+            device_id_type=pl.DeviceIdType.MESH)
+
+    def final_copy(tile, k, peer):
+        return pltpu.make_async_remote_copy(
+            src_ref=final_ref.at[hid, :, lanes_of(tile)], dst_ref=final_ref.at[hid, :, lanes_of(tile)],
+            send_sem=final_send.at[tile, k - 1], recv_sem=final_recv.at[tile, k - 1], device_id={"hid": peer},
+            device_id_type=pl.DeviceIdType.MESH)
+
+    @pl.when(step == 0)
+    def _():
+        barrier = pltpu.get_barrier_semaphore()
+        for _, peer in peers:
+            pl.semaphore_signal(barrier, inc=1, device_id={"hid": peer}, device_id_type=pl.DeviceIdType.MESH)
+        for _, mate in mates:
+            pl.semaphore_signal(barrier, inc=1, device_id={"inp": mate}, device_id_type=pl.DeviceIdType.MESH)
+        pl.semaphore_wait(barrier, n_hid + n_inp - 2)
+        for copy in copies():
+            copy.start()
+        own_copy().start()
+
+    def settle(tile):
+        for k, peer in peers:
+            part_copy(tile, k, peer).wait()
+        lanes = lanes_of(tile)
+        total = part_ref[hid, :, lanes]
+        for k, _ in peers:
+            total = total + part_got[k - 1, :, lanes]
+        final_ref[hid, :, lanes] = total
+        for k, peer in peers:
+            final_copy(tile, k, peer).start()
+
+    @pl.when(step == steps - 1)
+    def _():
+        def early(tile, carry):
+            settle(tile)
+            return carry
+
+        lax.fori_loop(0, steps - 1, early, 0)
+
+    sums = bins_tile(
+        left_ref, right_ref, total_ref, idx_ref, sign_ref, ones_ref, acc_ref, values, leaves, lambda i: None
+    )
+    for k, total in enumerate(entry_sums(sums)):
+        part_ref[k // rows, k % rows : k % rows + 1, lanes_of(step)] = total
+    for k, peer in peers:
+        part_copy(step, k, peer).start()
+
+    @pl.when(step == steps - 1)
+    def _():
+        for copy in copies():
+            copy.wait()
+        own_copy().wait()
+        for out, own, got in ((gate_out, gate_ref, gate_got), (up_out, up_ref, up_got)):
+            total = own[...]
+            for k, _ in mates:
+                total = total + got[k - 1]
+            out[...] = total
+        count, _, block = own_ref.shape
+        for i in range(count):
+            total = own_ref[i].astype(F32)
+            for k, _ in peers:
+                total = total + got_ref[k - 1, i].astype(F32)
+            grad_out[i] = total
+        settle(steps - 1)
+
+        def finish(tile, carry):
+            for k, peer in peers:
+                final_copy(tile, k, peer).wait()
+            return carry
+
+        lax.fori_loop(0, steps, finish, 0)
+        out_ref[...] = final_ref[...]
+
+
+def finish_kernel(scale, down_ref, gate_ref, up_ref, grad_ref, order_ref, down_out, gate_out, up_out, grad_out):
+    groups, rows, _ = down_ref.shape
+    for k in range(groups):
+        down_out[k * rows : (k + 1) * rows, :] = down_ref[k] * scale
+    gate_out[...] = gate_ref[...] * scale
+    up_out[...] = up_ref[...] * scale
+    count, _, block = grad_ref.shape
+    for i in range(count):
+        grad_out[:, i * block : (i + 1) * block] = contract_cols(
+            grad_ref[i].astype(BF16), order_ref[...]
+        ).astype(BF16)
+
+
+def finish(down, gate, up, grad, order, scale):
+    count, rows, block = grad.shape
+    return pl.pallas_call(
+        functools.partial(finish_kernel, scale),
+        out_shape=[
+            jax.ShapeDtypeStruct((ENTRIES, down.shape[2]), F32),
+            jax.ShapeDtypeStruct(gate.shape, F32),
+            jax.ShapeDtypeStruct(up.shape, F32),
+            jax.ShapeDtypeStruct((rows, count * block), BF16),
         ],
-        axis=1,
-    )
-    write_bins([whole] + [acc_ref[k : k + 1, :] for k in range(1, ENTRIES)], out_ref, scale)
+        cost_estimate=cost(rows * count * block * block, 8 * gate.size),
+        name="finish",
+    )(down, gate, up, grad, order)
 
 
 def sign_table():
@@ -271,44 +418,100 @@
     return (row == col // SUB).astype(BF16)
 
 
-def bins(left, total, right, index, scale, lookup=None, start=None):
+def fixed(shape):
+    return pl.BlockSpec(shape, lambda j: (0,) * len(shape))
+
+
+def bins_operands(left, total, right, index, most):
     count, block, tokens = left.shape
     words, width = index.shape
-    cols = divisor(width, 256)
-    with_grad, with_start = lookup is not None, start is not None
-    whole3 = pl.BlockSpec((count, tokens, block), lambda j: (0, 0, 0))
-    in_specs = [
-        pl.BlockSpec((count, block, tokens), lambda j: (0, 0, 0)),
+    cols = divisor(width, most)
+    specs = [
+        fixed((count, block, tokens)),
         pl.BlockSpec((tokens, cols), lambda j: (0, j)),
-        pl.BlockSpec((tokens, LANES), lambda j: (0, 0)),
+        fixed((tokens, LANES)),
         pl.BlockSpec((words, cols), lambda j: (0, j)),
-        pl.BlockSpec((4 * ENTRIES, LANES), lambda j: (0, 0)),
-        pl.BlockSpec((ENTRIES, ENTRIES * SUB), lambda j: (0, 0)),
+        fixed((4 * ENTRIES, LANES)),
+        fixed((ENTRIES, ENTRIES * SUB)),
     ]
-    args = [left, right, total, index, sign_table(), group_ones()]
-    out_specs = [pl.BlockSpec((ENTRIES, cols), lambda j: (0, j))]
-    out_shape = [jax.ShapeDtypeStruct((ENTRIES, width), F32)]
     scratch = [pltpu.VMEM((ENTRIES, cols), F32)]
     scratch += [pltpu.VMEM((block, cols), F32)] * 2 + [pltpu.VMEM((ENTRIES * SUB, cols), BF16)] * 2
-    if with_grad:
-        in_specs.append(pl.BlockSpec((ENTRIES, cols), lambda j: (0, j)))
-        args.append(lookup)
-        if with_start:
-            in_specs.append(whole3)
-            args.append(start)
-        out_specs.append(whole3)
-        out_shape.append(jax.ShapeDtypeStruct((count, tokens, block), F32))
-    out = pl.pallas_call(
-        functools.partial(bins_kernel, scale, with_grad, with_start),
+    return cols, specs, [left, right, total, index, sign_table(), group_ones()], scratch
+
+
+def grad_bins(left, total, right, index, lookup, start=None, shares=0):
+    count, block, tokens = left.shape
+    words, width = index.shape
+    cols, specs, args, scratch = bins_operands(left, total, right, index, 256)
+    specs.append(pl.BlockSpec((ENTRIES, cols), lambda j: (0, j)))
+    args.append(lookup)
+    blocks = (count, tokens, block)
+    if start is not None:
+        specs.append(fixed(blocks))
+        args.append(start)
+    if shares:
+        grad = jax.ShapeDtypeStruct((shares, count, tokens // shares, block), BF16)
+        scratch = scratch + [pltpu.VMEM(blocks, F32)]
+    else:
+        grad = jax.ShapeDtypeStruct(blocks, F32)
+    return pl.pallas_call(
+        functools.partial(grad_kernel, start is not None, shares),
         grid=(width // cols,),
-        in_specs=in_specs,
-        out_specs=out_specs,
-        out_shape=out_shape,
+        in_specs=specs,
+        out_specs=[pl.BlockSpec((ENTRIES, cols), lambda j: (0, j)), fixed(grad.shape)],
+        out_shape=[jax.ShapeDtypeStruct((ENTRIES, width), F32), grad],
         scratch_shapes=scratch,
         cost_estimate=cost(40 * tokens * words * width, 4 * words * width),
-        name="bins_grad" if with_grad else "bins",
+        name="grad_bins",
     )(*args)
-    return out if with_grad else out[0]
+
+
+def down_bins(left, total, right, index, gate_part, up_part, shares):
+    count, block, tokens = left.shape
+    words, width = index.shape
+    n_hid, n_inp = lax.axis_size("hid"), lax.axis_size("inp")
+    cols, specs, args, scratch = bins_operands(left, total, right, index, 512)
+    steps = width // cols
+    table = gate_part.shape
+    share = shares.shape[1:]
+    specs += [fixed(table), fixed(table), pl.BlockSpec(memory_space=pl.ANY)]
+    args += [gate_part, up_part, shares]
+    rows = ENTRIES // n_hid
+    groups = (n_hid, rows, width)
+    scratch = scratch + [
+        pltpu.VMEM(share, BF16),
+        pltpu.VMEM((n_hid - 1,) + share, BF16),
+        pltpu.VMEM((n_inp - 1,) + table, F32),
+        pltpu.VMEM((n_inp - 1,) + table, F32),
+        pltpu.VMEM(groups, F32),
+        pltpu.VMEM((n_hid - 1, rows, width), F32),
+        pltpu.VMEM(groups, F32),
+        pltpu.SemaphoreType.DMA(()),
+        pltpu.SemaphoreType.DMA((n_hid - 1,)),
+        pltpu.SemaphoreType.DMA((n_hid - 1,)),
+        pltpu.SemaphoreType.DMA((2 * (n_inp - 1),)),
+        pltpu.SemaphoreType.DMA((2 * (n_inp - 1),)),
+        pltpu.SemaphoreType.DMA((steps, n_hid - 1)),
+        pltpu.SemaphoreType.DMA((steps, n_hid - 1)),
+        pltpu.SemaphoreType.DMA((steps, n_hid - 1)),
+        pltpu.SemaphoreType.DMA((steps, n_hid - 1)),
+    ]
+    return pl.pallas_call(
+        functools.partial(down_bins_kernel, n_hid, n_inp),
+        grid=(steps,),
+        in_specs=specs,
+        out_specs=[fixed(groups), fixed(table), fixed(table), fixed(share)],
+        out_shape=[
+            jax.ShapeDtypeStruct(groups, F32),
+            jax.ShapeDtypeStruct(table, F32),
+            jax.ShapeDtypeStruct(table, F32),
+            jax.ShapeDtypeStruct(share, F32),
+        ],
+        scratch_shapes=scratch,
+        compiler_params=pltpu.CompilerParams(collective_id=0, has_side_effects=True),
+        cost_estimate=cost(40 * tokens * words * width, 4 * words * width),
+        name="down_bins",
+    )(*args)
 
 
 def row_totals(array):
@@ -372,22 +575,6 @@
     return array.reshape(shape[:dim] + (rows,) + shape[dim + 1 :])
 
 
-def sum_scatter_direct(array, axis, dim):
-    size = lax.axis_size(axis)
-    if not power_of_two(size):
-        return lax.psum_scatter(array, axis, scatter_dimension=dim, tiled=True), []
-    me = lax.axis_index(axis)
-    rows = array.shape[dim] // size
-    total = lax.dynamic_slice_in_dim(array, me * rows, rows, dim)
-    sent = [
-        shift(
-            lax.dynamic_slice_in_dim(array, jnp.bitwise_xor(me, by) * rows, rows, dim).astype(BF16), axis, size, by
-        )
-        for by in range(1, size)
-    ]
-    return total, sent
-
-
 def gather(array, axis):
     size = lax.axis_size(axis)
     if not power_of_two(size):
@@ -403,15 +590,6 @@
     return array.reshape(size * rows, cols)
 
 
-def sum_all(array, axis):
-    size = lax.axis_size(axis)
-    if not power_of_two(size):
-        return lax.psum(array, axis)
-    for bit in axis_bits(size):
-        array = array + shift(array, axis, size, bit)
-    return array
-
-
 def after(array, *done):
     return lax.optimization_barrier((array, *done))[0]
 
@@ -427,7 +605,6 @@
 
 def shards(inputs, out_grad, gate_index, up_index, down_index, gate_table, up_table, down_table):
     tokens = inputs.shape[0]
-    scale = 1.0 / tokens
     hid_blocks = down_product(out_grad, down_index, down_table)
     hid = sum_scatter(hid_blocks, "inp", 1)
     x_blocks = to_blocks(inputs)
@@ -441,22 +618,16 @@
     gate_grad = gather(gate_grad, "inp")
     up_grad = gather(after(up_grad, gate_grad), "inp")
     acts = gather(after(activ, gate_grad), "inp")
-    gate_part, din_blocks = bins(x_turned, x_total, gate_grad, gate_index, scale, gate_table)
-    up_part, din_blocks = bins(
-        x_turned, x_total, after(up_grad, gate_part), up_index, scale, up_table, din_blocks
-    )
-    gate_sum = sum_all(gate_part, "inp")
-    din_own, din_sent = sum_scatter_direct(din_blocks, "hid", 1)
-    acts = after(acts, up_part)
-    down_part = bins(
-        jnp.swapaxes(to_blocks(acts), 1, 2), row_totals(acts), out_grad, down_index, scale
-    )
-    up_sum = sum_all(up_part, "inp")
-    down_sum = sum_all(down_part, "hid")
-    din = din_own
-    for piece in din_sent:
-        din = din + after(piece, down_part).astype(F32)
-    input_grad = from_blocks(din).astype(BF16)
+    gate_part, din_blocks = grad_bins(x_turned, x_total, gate_grad, gate_index, gate_table)
+    up_part, shares = grad_bins(
+        x_turned, x_total, after(up_grad, gate_part), up_index, up_table, din_blocks, lax.axis_size("hid")
+    )
+    sums = down_bins(
+        jnp.swapaxes(to_blocks(acts), 1, 2), row_totals(acts), out_grad, down_index, gate_part, up_part, shares
+    )
+    down_sum, gate_sum, up_sum, input_grad = finish(
+        *sums, pairing(x_blocks.shape[2], BF16), 1.0 / (tokens * ENTRIES)
+    )
     return input_grad, gate_sum, up_sum, down_sum
 
 

time: 332 us -> 303 us (0.913)
  starting transfers between devices: 35.2 us -> 10.2 us
  waiting for transfers between devices: 35.7 us -> 14.2 us
  Pallas kernels: 229 us -> 249 us
    ppermute x26 -> x12, starting transfers between devices: 35.2 us -> 10.2 us  [shift(): return lax.ppermute(array, axis, [(i, i ^ by) for i in range(size)])]
    ppermute x26 -> x12, waiting for transfers between devices: 35.7 us -> 14.2 us  [shift(): return lax.ppermute(array, axis, [(i, i ^ by) for i in range(size)])]
    pallas_call x3 -> x4, Pallas kernels: 172 us -> 193 us  [the longest x2 117 us: grad_bins(): pl.pallas_call(functools.partial(grad_kernel, start is not None, shares),...]
  transfers between devices with their start and end apart: 26 -> 12, of which waited for: 12 -> 6; matrix products, arithmetic and copies ran while one was open for 6% -> 7% of each run, Pallas kernels for 17% -> 32%
where the time goes in v2:
time: 303 us; the launch traced here: 302 us
  Pallas kernels  249 us (82%)
  local copies, waits for them, and re-layouts  14.2 us (5%)
  waiting for transfers between devices  14.2 us (5%)
  starting transfers between devices  10.2 us (3%)
  other arithmetic  10.1 us (3%)
    pallas_call x2, Pallas kernels, grad_bins(): pl.pallas_call(functools.partial(grad_kernel, start is not None, shares),...  117 us
    pallas_call x1, Pallas kernels, down_bins(): pl.pallas_call(functools.partial(down_bins_kernel, n_hid, n_inp), grid=(s...  73.4 us
    pallas_call x2, Pallas kernels, up_product(): pl.pallas_call(up_kernel, grid=(width // cols,), in_specs=[pl.BlockSpec((...  38.1 us
    pallas_call x1, Pallas kernels, down_product(): pl.pallas_call(down_kernel, grid=(width // cols,), in_specs=[pl.BlockSpec...  18.7 us
    ppermute x12, waiting for transfers between devices, shift(): return lax.ppermute(array, axis, [(i, i ^ by) for i in range(size)])  14.2 us
    ppermute x12, starting transfers between devices, shift(): return lax.ppermute(array, axis, [(i, i ^ by) for i in range(size)])  10.2 us
    convert_element_type x6, local copies, waits for them, and re-layouts, sum_scatter(): lax.dynamic_index_in_dim(pairs, 1 - mine, dim + 1, False).astype(BF16)  7.61 us
  transfers between devices with their start and end apart: 12, of which 6 were waited for; matrix products, arithmetic and copies ran while one was open for 7% of the time, Pallas kernels for 32%

profile of v2, /device:TPU:0, one launch (start us, length us, event | category | flops | bytes accessed | tf_op | source)
XLA Modules:
  0.0 301.5 jit_solution(14614060368514451893)
XLA Ops:
  0.7 18.7 %down_product.1 = f32[13,128,256]{2,1,0:T(8,128)} custom-call(bf16[128,4096]{1,0:T(8,128)(2,1)} %refs_1_.1, s32[1664,4096]{1,0:T(8,128)} %refs_3_.5, f32[16,4096]{1,0:T(8,128)} %table_ref.1), custom_call_target="tpu_custom_call" | custom-call | flops 3489660928 | bytes 27262976 | tf_op jit(solution)/shard_map/down_product/pallas_call | solution.py:139
  19.3 2.0 fusion.4
  22.4 1.4 copy.40.x_ref
  23.7 19.1 %up_product.2 = f32[128,3328]{1,0:T(8,128)} custom-call(bf16[16,128,256]{2,1,0:T(8,128)(2,1)} %copy.40.x_ref, s32[2048,3328]{1,0:T(8,128)} %refs_3_.3, f32[16,3328]{1,0:T(8,128)} %refs_6_.2), custom_call_target="tpu_custom_call" | custom-call | flops 3489660928 | bytes 27262976 | tf_op jit(solution)/shard_map/up_product/pallas_call | solution.py:101
  42.8 2.0 fusion.5
  44.8 19.0 %up_product.3 = f32[128,3328]{1,0:T(8,128)} custom-call(bf16[16,128,256]{2,1,0:T(8,128)(2,1)} %copy.40.x_ref, s32[2048,3328]{1,0:T(8,128)} %refs_3_.4, f32[16,3328]{1,0:T(8,128)} %refs_6_.3), custom_call_target="tpu_custom_call" | custom-call | flops 3489660928 | bytes 27262976 | tf_op jit(solution)/shard_map/up_product/pallas_call | solution.py:101
  63.8 2.1 fusion.6
  66.4 1.5 convert_reduce_fusion
  68.7 1.1 bitcast_add_fusion
  69.8 2.7 collective-permute-start.5
  72.5 1.1 bitcast_add_fusion.2
  73.6 0.7 dynamic-slice_convert_fusion.2
  74.4 1.1 bitcast_add_fusion.1
  75.5 0.7 dynamic-slice_convert_fusion.1
  76.2 1.9 collective-permute-start.3
  79.4 3.8 %collective-permute-done.1 = bf16[1,32,3328]{2,1,0:T(8,128)(2,1)S(1)} collective-permute-done((bf16[1,32,3328]{2,1,0:T(8,128)(2,1)}, bf16[1,32,3328]{2,1,0:T(8,128)(2,1)S(1)}, u32[]{:S(2)}, u32[]{:S(2)}) %collective-permute-start.1) | collective-permute-done | bytes 213024 | tf_op jit(solution)/shard_map/ppermute | solution.py:549
  83.2 4.3 %collective-permute-done.3 = bf16[1,32,3328]{2,1,0:T(8,128)(2,1)S(1)} collective-permute-done((bf16[1,32,3328]{2,1,0:T(8,128)(2,1)}, bf16[1,32,3328]{2,1,0:T(8,128)(2,1)S(1)}, u32[]{:S(2)}, u32[]{:S(2)}) %collective-permute-start.3) | collective-permute-done | bytes 213024 | tf_op jit(solution)/shard_map/ppermute | solution.py:549
  87.7 1.8 collective-permute-start.6
  90.1 4.6 %collective-permute-done.6 = bf16[1,32,3328]{2,1,0:T(8,128)(2,1)S(1)} collective-permute-done((bf16[1,32,3328]{2,1,0:T(8,128)(2,1)S(1)}, bf16[1,32,3328]{2,1,0:T(8,128)(2,1)S(1)}, u32[]{:S(2)}, u32[]{:S(2)}) %collective-permute-start.6) | collective-permute-done | bytes 213024 | tf_op jit(solution)/shard_map/ppermute | solution.py:549
  94.9 1.2 multiply_convert_fusion
  96.8 1.0 copy.47
  97.8 1.5 collective-permute-start.10
  100.5 0.7 broadcast_in_dim.20.refs_2_
  101.2 58.2 %grad_bins.2 = (f32[16,3328]{1,0:T(8,128)}, f32[16,128,256]{2,1,0:T(8,128)}) custom-call(bf16[16,256,128]{2,1,0:T(8,128)(2,1)} %bitcast.124, bf16[128,3328]{1,0:T(8,128)(2,1)} %bitcast.131, f32[128,128]{1,0:T(8,128)} %broadcast_in_dim.20.refs_2_, s32[2048,3328]{1,0:T(8,128)} %refs_3_.3, bf16[64,128]{1,0:T(8,128)(2,1)} %broadcast_in_dim.19.refs_4_, ...), custom_call_target="tpu_custom_call" | custom-call | flops 34896609280 | bytes 27262976 | tf_op jit(solution)/shard_map/grad_bins/pallas_call | solution.py:457
  159.6 0.8 maximum_bitcast_fusion.2
  162.5 1.7 fusion.refs_0_
  164.2 1.1 select_bitcast_fusion.1
  165.3 1.0 copy.53
  166.3 58.3 %grad_bins.3 = (f32[16,3328]{1,0:T(8,128)}, bf16[8,16,16,256]{3,2,1,0:T(8,128)(2,1)}) custom-call(bf16[16,256,128]{2,1,0:T(8,128)(2,1)} %bitcast.125, bf16[128,3328]{1,0:T(8,128)(2,1)} %bitcast.132, f32[128,128]{1,0:T(8,128)} %broadcast_in_dim.20.refs_2_, s32[2048,3328]{1,0:T(8,128)} %refs_3_.4, bf16[64,128]{1,0:T(8,128)(2,1)} %broadcast_in_dim.19.refs_4_, ...), custom_call_target="tpu_custom_call" | custom-call | flops 34896609280 | bytes 27262976 | tf_op jit(solution)/shard_map/grad_bins/pallas_call | solution.py:457
  224.6 0.7 broadcast_in_dim.18.refs_2_
  225.3 73.4 %down_bins.1 = (f32[8,2,4096]{2,1,0:T(2,128)}, f32[16,3328]{1,0:T(8,128)}, f32[16,3328]{1,0:T(8,128)}, f32[16,16,256]{2,1,0:T(8,128)}) custom-call(bf16[13,256,128]{2,1,0:T(8,128)(2,1)} %fusion.refs_0_, bf16[128,4096]{1,0:T(8,128)(2,1)} %refs_1_.1, f32[128,128]{1,0:T(8,128)} %broadcast_in_dim.18.refs_2_, s32[1664,4096]{1,0:T(8,128)} %refs_3_.5, ...), custom_call_target="tpu_custom_call" | custom-call | flops 34896609280 | bytes 27262976 | tf_op jit(solution)/shard_map/down_bins/pallas_call | solution.py:499
  298.8 2.7 finish.1
  (63 shorter events, 8.9 us)
Async XLA Ops:
  0.6 21.2 %copy-start.3 = (bf16[128,4096]{1,0:T(8,128)(2,1)S(1)}, bf16[128,4096]{1,0:T(8,128)(2,1)}, u32[]{:S(2)}) copy-start(bf16[128,4096]{1,0:T(8,128)(2,1)} %param.8) | copy-start | bytes 3145732
  21.3 47.3 %collective-permute-start.4 = (bf16[13,2,32,256]{3,2,0,1:T(8,128)(2,1)}, bf16[13,2,32,256]{3,2,0,1:T(8,128)(2,1)}, u32[]{:S(2)}, u32[]{:S(2)}) collective-permute-start(bf16[13,2,32,256]{3,2,0,1:T(8,128)(2,1)} %fusion.4), channel_id=1, source_target_pairs={{0,8},{8,0},{16,24},{24,16},{1,9},{9,1},{17,25},{25,17},{2,10},{10... | collective-permute-start | bytes 1277960 | tf_op jit(solution)/shard_map/ppermute | solution.py:549
  22.3 20.4 %copy-start.4 = (bf16[256,128,16]{1,0,2:T(8,128)(2,1)}, bf16[256,128,16]{1,0,2:T(8,128)(2,1)S(1)}, u32[]{:S(2)}) copy-start(bf16[256,128,16]{1,0,2:T(8,128)(2,1)S(1)} %convolution_convert_fusion) | copy-start | bytes 3145732
  44.8 27.7 %collective-permute-start = (bf16[2,32,3328]{2,1,0:T(8,128)(2,1)}, bf16[2,32,3328]{2,1,0:T(8,128)(2,1)}, u32[]{:S(2)}, u32[]{:S(2)}) collective-permute-start(bf16[2,32,3328]{2,1,0:T(8,128)(2,1)} %fusion.5), channel_id=1, source_target_pairs={{0,8},{8,0},{16,24},{24,16},{1,9},{9,1},{17,25},{25,17},{2,10},{10... | collective-permute-start | bytes 1277960 | tf_op jit(solution)/shard_map/ppermute | solution.py:549
  63.8 4.9 %copy-start.2 = (f32[13,128,256]{2,1,0:T(8,128)S(1)}, f32[13,128,256]{2,1,0:T(8,128)}, u32[]{:S(2)}) copy-start(f32[13,128,256]{2,1,0:T(8,128)} %down_product.1) | copy-start | bytes 5111812
  65.9 6.6 %copy-start.1 = (f32[128,3328]{1,0:T(8,128)S(1)}, f32[128,3328]{1,0:T(8,128)}, u32[]{:S(2)}) copy-start(f32[128,3328]{1,0:T(8,128)} %up_product.2) | copy-start | bytes 5111812
  65.9 8.5 %collective-permute-start.2 = (bf16[2,32,3328]{2,1,0:T(8,128)(2,1)}, bf16[2,32,3328]{2,1,0:T(8,128)(2,1)}, u32[]{:S(2)}, u32[]{:S(2)}) collective-permute-start(bf16[2,32,3328]{2,1,0:T(8,128)(2,1)} %fusion.6), channel_id=1, source_target_pairs={{0,8},{8,0},{16,24},{24,16},{1,9},{9,1},{17,25},{25,17},{2,10},{10... | collective-permute-start | bytes 1277960 | tf_op jit(solution)/shard_map/ppermute | solution.py:549
  69.8 4.6 %copy-start = (f32[128,3328]{1,0:T(8,128)S(1)}, f32[128,3328]{1,0:T(8,128)}, u32[]{:S(2)}) copy-start(f32[128,3328]{1,0:T(8,128)} %up_product.3) | copy-start | bytes 5111812
  69.8 8.8 %collective-permute-start.5 = (bf16[13,1,32,256]{3,2,0,1:T(8,128)(2,1)S(1)}, bf16[13,1,32,256]{3,2,0,1:T(8,128)(2,1)S(1)}, u32[]{:S(2)}, u32[]{:S(2)}) collective-permute-start(bf16[13,1,32,256]{3,2,0,1:T(8,128)(2,1)S(1)} %dynamic-slice_convert_fusion), channel_id=1, source_target_pairs={{0,16},{8,24},{16,0},{24,8},{1,17},{9,25},{17,1},{25,9},{2,18},{10... | collective-permute-start | bytes 638984 | tf_op jit(solution)/shard_map/ppermute | solution.py:549
  74.3 8.9 %collective-permute-start.1 = (bf16[1,32,3328]{2,1,0:T(8,128)(2,1)}, bf16[1,32,3328]{2,1,0:T(8,128)(2,1)S(1)}, u32[]{:S(2)}, u32[]{:S(2)}) collective-permute-start(bf16[1,32,3328]{2,1,0:T(8,128)(2,1)} %dynamic-slice_convert_fusion.2), channel_id=1, source_target_pairs={{0,16},{8,24},{16,0},{24,8},{1,17},{9,25},{17,1},{25,9},{2,18},{10... | collective-permute-start | bytes 638984 | tf_op jit(solution)/shard_map/ppermute | solution.py:549
  76.2 11.2 %collective-permute-start.3 = (bf16[1,32,3328]{2,1,0:T(8,128)(2,1)}, bf16[1,32,3328]{2,1,0:T(8,128)(2,1)S(1)}, u32[]{:S(2)}, u32[]{:S(2)}) collective-permute-start(bf16[1,32,3328]{2,1,0:T(8,128)(2,1)} %dynamic-slice_convert_fusion.1), channel_id=1, source_target_pairs={{0,16},{8,24},{16,0},{24,8},{1,17},{9,25},{17,1},{25,9},{2,18},{10... | collective-permute-start | bytes 638984 | tf_op jit(solution)/shard_map/ppermute | solution.py:549
  83.2 11.7 %copy-start.7 = (bf16[1,32,3328]{2,1,0:T(8,128)(2,1)}, bf16[1,32,3328]{2,1,0:T(8,128)(2,1)S(1)}, u32[]{:S(2)}) copy-start(bf16[1,32,3328]{2,1,0:T(8,128)(2,1)S(1)} %collective-permute-done.1) | copy-start | bytes 638980
  87.5 7.4 %copy-start.8 = (bf16[1,32,3328]{2,1,0:T(8,128)(2,1)}, bf16[1,32,3328]{2,1,0:T(8,128)(2,1)S(1)}, u32[]{:S(2)}) copy-start(bf16[1,32,3328]{2,1,0:T(8,128)(2,1)S(1)} %collective-permute-done.3) | copy-start | bytes 638980
  87.7 7.1 %collective-permute-start.6 = (bf16[1,32,3328]{2,1,0:T(8,128)(2,1)S(1)}, bf16[1,32,3328]{2,1,0:T(8,128)(2,1)S(1)}, u32[]{:S(2)}, u32[]{:S(2)}) collective-permute-start(bf16[1,32,3328]{2,1,0:T(8,128)(2,1)S(1)} %multiply_convert_fusion.1), channel_id=1, source_target_pairs={{0,16},{8,24},{16,0},{24,8},{1,17},{9,25},{17,1},{25,9},{2,18},{10... | collective-permute-start | bytes 638984 | tf_op jit(solution)/shard_map/ppermute | solution.py:549
  94.8 1.8 collective-permute-start.7
  96.1 3.1 %copy-start.5 = (bf16[32,3328]{1,0:T(8,128)(2,1)}, bf16[32,3328]{1,0:T(8,128)(2,1)S(1)}, u32[]{:S(2)}) copy-start(bf16[32,3328]{1,0:T(8,128)(2,1)S(1)} %get-tuple-element.23) | copy-start | bytes 638980
  97.8 61.6 %collective-permute-start.10 = (bf16[1,32,3328]{2,1,0:T(8,128)(2,1)S(1)}, bf16[1,32,3328]{2,1,0:T(8,128)(2,1)S(1)}, u32[]{:S(2)}, u32[]{:S(2)}) collective-permute-start(bf16[1,32,3328]{2,1,0:T(8,128)(2,1)S(1)} %bitcast.129), channel_id=1, source_target_pairs={{0,16},{8,24},{16,0},{24,8},{1,17},{9,25},{17,1},{25,9},{2,18},{10... | collective-permute-start | bytes 638984 | tf_op jit(solution)/shard_map/ppermute | solution.py:549
  99.2 60.2 %collective-permute-start.8 = (bf16[1,32,3328]{2,1,0:T(8,128)(2,1)S(1)}, bf16[1,32,3328]{2,1,0:T(8,128)(2,1)S(1)}, u32[]{:S(2)}, u32[]{:S(2)}) collective-permute-start(bf16[1,32,3328]{2,1,0:T(8,128)(2,1)S(1)} %bitcast.130), channel_id=1, source_target_pairs={{0,16},{8,24},{16,0},{24,8},{1,17},{9,25},{17,1},{25,9},{2,18},{10... | collective-permute-start | bytes 638984 | tf_op jit(solution)/shard_map/ppermute | solution.py:549
  101.2 58.2 %copy-start.6 = (bf16[32,3328]{1,0:T(8,128)(2,1)S(1)}, bf16[32,3328]{1,0:T(8,128)(2,1)}, u32[]{:S(2)}) copy-start(bf16[32,3328]{1,0:T(8,128)(2,1)} %copy-done.5) | copy-start | bytes 638980
  159.5 1.8 collective-permute-start.9
  160.4 3.7 %collective-permute-start.11 = (bf16[2,32,3328]{2,1,0:T(8,128)(2,1)}, bf16[2,32,3328]{2,1,0:T(8,128)(2,1)}, u32[]{:S(2)}, u32[]{:S(2)}) collective-permute-start(bf16[2,32,3328]{2,1,0:T(8,128)(2,1)} %maximum_bitcast_fusion.2), channel_id=1, source_target_pairs={{0,8},{8,0},{16,24},{24,16},{1,9},{9,1},{17,25},{25,17},{2,10},{10... | collective-permute-start | bytes 1277960 | tf_op jit(solution)/shard_map/ppermute | solution.py:549

commit v3 on v2

--- a/solution.py
+++ b/solution.py
@@ -40,6 +40,10 @@
 def nibbles(words):
     low = jnp.bitwise_and(words.astype(jnp.int16), jnp.int16(15))
     return low, jnp.right_shift(words, 4).astype(jnp.int16)
+
+
+def fixed(shape):
+    return pl.BlockSpec(shape, lambda j: (0,) * len(shape))
 
 
 def lane_chunks(cols):
@@ -78,77 +82,303 @@
         body(count - count % size, count % size)
 
 
-def up_kernel(x_ref, idx_ref, table_ref, pre_ref):
+LAG_CHIP = 2
+LAG_HIDDEN = 5
+LAG_RELAY = 8
+
+
+def mesh_copy(src, dst, send, recv, **device):
+    return pltpu.make_async_remote_copy(
+        src_ref=src, dst_ref=dst, send_sem=send, recv_sem=recv, device_id=device,
+        device_id_type=pl.DeviceIdType.MESH,
+    )
+
+
+def repeat(first, last, body):
+    def step(i, carry):
+        body(i)
+        return carry
+
+    lax.fori_loop(first, last, step, 0)
+
+
+def hidden_kernel(size, down_steps, *refs):
+    (og_ref, x_ref, down_ref, down_table, gate_ref, gate_table, up_ref, up_table, order_ref) = refs[:9]
+    (out_ref, hid_acc, hid_part, hid_sib, hid_chip, hid_got, part, sib, chip, chip_got, all_ref) = refs[9:20]
+    (hid_send, hid_recv, hid_chip_send, hid_chip_recv, sib_send, sib_recv) = refs[20:26]
+    (chip_send, chip_recv, pair_send, pair_recv, far_send, far_recv, relay_send, relay_recv) = refs[26:]
+    step, steps = pl.program_id(0), pl.num_programs(0)
     count, _, block = x_ref.shape
-    tables = tables_of(table_ref)
-    pre_ref[...] = jnp.zeros_like(pre_ref)
-
-    def body(first, n):
-        pre_ref[...] += sum(
-            jnp.dot(
-                x_ref[first + k], decode_block(idx_ref, tables, first + k, block // 2), preferred_element_type=F32
+    hid_count, tokens, cols = hid_acc.shape
+    tiles = hid_count
+    chips = size // 2
+    rows = tokens // size
+    me = lax.axis_index("inp")
+    my_chip, side = me // 2, lax.rem(me, 2)
+    other = 1 - side
+    sibling = 2 * my_chip + other
+    far = [(k, lax.rem(my_chip + k, chips)) for k in range(1, chips)]
+
+    def lanes_of(tile):
+        return pl.ds(pl.multiple_of(tile * cols, LANES), cols)
+
+    def hid_copy():
+        return mesh_copy(hid_part.at[other], hid_sib, hid_send, hid_recv, inp=sibling)
+
+    def hid_far(k, there):
+        return mesh_copy(
+            hid_chip.at[there], hid_got.at[k - 1], hid_chip_send.at[k - 1], hid_chip_recv.at[k - 1],
+            inp=2 * there + side,
+        )
+
+    def sib_copy(a, tile):
+        lanes = lanes_of(tile)
+        return mesh_copy(
+            part.at[a, other, :, :, lanes], sib.at[a, :, :, lanes], sib_send.at[a, tile], sib_recv.at[a, tile],
+            inp=sibling,
+        )
+
+    def chip_copy(a, tile, k, there):
+        lanes = lanes_of(tile)
+        return mesh_copy(
+            chip.at[a, there, :, lanes], chip_got.at[a, k - 1, :, lanes], chip_send.at[a, tile, k - 1],
+            chip_recv.at[a, tile, k - 1], inp=2 * there + side,
+        )
+
+    def pair_copy(tile):
+        own = all_ref.at[me, :, :, lanes_of(tile)]
+        return mesh_copy(own, own, pair_send.at[tile], pair_recv.at[tile], inp=sibling)
+
+    def far_copy(tile, k, there):
+        own = all_ref.at[me, :, :, lanes_of(tile)]
+        return mesh_copy(
+            own, own, far_send.at[tile, k - 1], far_recv.at[tile, k - 1], inp=2 * there + side
+        )
+
+    def relay_copy(tile, k):
+        source = 2 * lax.rem(my_chip + chips - k, chips) + side
+        theirs = all_ref.at[source, :, :, lanes_of(tile)]
+        return mesh_copy(theirs, theirs, relay_send.at[tile, k - 1], relay_recv.at[tile, k - 1], inp=sibling)
+
+    def hid_sum():
+        hid_copy().wait_recv()
+        for c in range(chips):
+            for i in range(hid_count):
+                hid_chip[c, i] = (hid_part[side, c, i].astype(F32) + hid_sib[c, i].astype(F32)).astype(BF16)
+        for k, there in far:
+            hid_far(k, there).start()
+
+    def chip_sum(u):
+        a, tile = u // tiles, lax.rem(u, tiles)
+        lanes = lanes_of(tile)
+        sib_copy(a, tile).wait_recv()
+        for c in range(chips):
+            total = part[a, side, c, :, lanes].astype(F32) + sib[a, c, :, lanes].astype(F32)
+            chip[a, c, :, lanes] = total.astype(BF16)
+        for k, there in far:
+            chip_copy(a, tile, k, there).start()
+
+    def hidden(tile):
+        lanes = lanes_of(tile)
+        shares = []
+        for a in range(2):
+            total = chip[a, my_chip, :, lanes].astype(F32)
+            for k, there in far:
+                chip_copy(a, tile, k, there).wait_recv()
+                total = total + chip_got[a, k - 1, :, lanes].astype(F32)
+            shares.append(total)
+        total = hid_chip[my_chip, tile].astype(F32)
+        for k, _ in far:
+            total = total + hid_got[k - 1, tile].astype(F32)
+        high = total.astype(BF16)
+        low = (total - high.astype(F32)).astype(BF16)
+        grad = contract_cols(high, order_ref[...]) + contract_cols(low, order_ref[...])
+        gate_grad, up_grad, activ = local_hidden(shares[0], shares[1], grad)
+        all_ref[me, 0, :, lanes] = gate_grad
+        all_ref[me, 1, :, lanes] = up_grad
+        all_ref[me, 2, :, lanes] = activ
+        pair_copy(tile).start()
+        for k, there in far:
+            far_copy(tile, k, there).start()
+
+    def relay(tile):
+        for k, there in far:
+            far_copy(tile, k, there).wait_recv()
+            relay_copy(tile, k).start()
+
+    @pl.when(step == 0)
+    def _():
+        barrier = pltpu.get_barrier_semaphore()
+        pl.semaphore_signal(barrier, inc=1, device_id={"inp": sibling}, device_id_type=pl.DeviceIdType.MESH)
+        for _, there in far:
+            pl.semaphore_signal(
+                barrier, inc=1, device_id={"inp": 2 * there + side}, device_id_type=pl.DeviceIdType.MESH
             )
-            for k in range(n)
-        )
-
-    grouped(count, 8, body)
-
-
-def up_product(x_blocks, index, lookup):
+        pl.semaphore_wait(barrier, chips)
+        hid_acc[...] = jnp.zeros_like(hid_acc)
+
+    @pl.when(step == down_steps + LAG_CHIP)
+    def _():
+        hid_sum()
+
+    unit = step - down_steps - LAG_CHIP
+
+    @pl.when(unit >= 0)
+    def _():
+        chip_sum(unit)
+
+    ready = step - down_steps - tiles - LAG_HIDDEN
+
+    @pl.when(ready == 0)
+    def _():
+        for k, there in far:
+            hid_far(k, there).wait_recv()
+
+    @pl.when(ready >= 0)
+    def _():
+        hidden(ready)
+
+    @pl.when(step >= down_steps + tiles + LAG_RELAY)
+    def _():
+        relay(step - down_steps - tiles - LAG_RELAY)
+
+    @pl.when(step < down_steps)
+    def _():
+        tables = tables_of(down_table)
+
+        def body(first, n):
+            for k in range(n):
+                hid_acc[first + k] += contract_cols(
+                    og_ref[...], decode_block(down_ref, tables, first + k, cols // 2)
+                )
+
+        grouped(hid_count, 3, body)
+
+    @pl.when(step == down_steps - 1)
+    def _():
+        for c in range(chips):
+            for s in range(2):
+                first = (2 * c + s) * rows
+                for i in range(hid_count):
+                    hid_part[s, c, i] = hid_acc[i, first : first + rows, :].astype(BF16)
+        hid_copy().start()
+
+    def product(a, idx_ref, table_ref, tile):
+        tables = tables_of(table_ref)
+        pre_ref = hid_acc.at[0]
+        pre_ref[...] = jnp.zeros_like(pre_ref)
+
+        def body(first, n):
+            pre_ref[...] += sum(
+                jnp.dot(
+                    x_ref[first + k], decode_block(idx_ref, tables, first + k, block // 2),
+                    preferred_element_type=F32,
+                )
+                for k in range(n)
+            )
+
+        grouped(count, 8, body)
+        for c in range(chips):
+            for s in range(2):
+                first = (2 * c + s) * rows
+                part[a, s, c, :, lanes_of(tile)] = pre_ref[first : first + rows, :].astype(BF16)
+        sib_copy(a, tile).start()
+
+    @pl.when(jnp.logical_and(step >= down_steps, step < down_steps + tiles))
+    def _():
+        product(0, gate_ref, gate_table, step - down_steps)
+
+    @pl.when(step >= down_steps + tiles)
+    def _():
+        product(1, up_ref, up_table, step - down_steps - tiles)
+
+    @pl.when(step == steps - 1)
+    def _():
+        repeat(2 * tiles - LAG_CHIP, 2 * tiles, chip_sum)
+        repeat(tiles - LAG_HIDDEN, tiles, hidden)
+        repeat(tiles - LAG_RELAY, tiles, relay)
+        hid_copy().wait_send()
+        for k, there in far:
+            hid_far(k, there).wait_send()
+
+        def finish_tile(tile):
+            for a in range(2):
+                sib_copy(a, tile).wait_send()
+                for k, there in far:
+                    chip_copy(a, tile, k, there).wait_send()
+            pair_copy(tile).wait()
+            for k, there in far:
+                far_copy(tile, k, there).wait_send()
+                relay_copy(tile, k).wait()
+
+        repeat(0, tiles, finish_tile)
+        out_ref[...] = all_ref[...]
+
+
+def hidden_grads(x_blocks, out_grad, gate_index, up_index, down_index, gate_table, up_table, down_table, order):
     count, tokens, block = x_blocks.shape
-    words, width = index.shape
-    cols = divisor(width, 256)
+    words, width = gate_index.shape
+    down_words, model = down_index.shape
+    size = lax.axis_size("inp")
+    chips, rows = size // 2, tokens // size
+    cols = math.gcd(width, 256)
+    tiles = width // cols
+    wide = divisor(model, 512)
+    down_steps = model // wide
+    gathered = (size, 3, rows, width)
+
+    def at(first, last):
+        return lambda j: (0, jnp.clip(j - first, 0, last - 1))
+
+    blocks = (tiles, rows, cols)
+    dma = pltpu.SemaphoreType.DMA
     return pl.pallas_call(
-        up_kernel,
-        grid=(width // cols,),
+        functools.partial(hidden_kernel, size, down_steps),
+        grid=(down_steps + 2 * tiles,),
         in_specs=[
-            pl.BlockSpec((count, tokens, block), lambda j: (0, 0, 0)),
-            pl.BlockSpec((words, cols), lambda j: (0, j)),
-            pl.BlockSpec((ENTRIES, cols), lambda j: (0, j)),
+            pl.BlockSpec((tokens, wide), at(0, down_steps)),
+            fixed((count, tokens, block)),
+            pl.BlockSpec((down_words, wide), at(0, down_steps)),
+            pl.BlockSpec((ENTRIES, wide), at(0, down_steps)),
+            pl.BlockSpec((words, cols), at(down_steps, tiles)),
+            pl.BlockSpec((ENTRIES, cols), at(down_steps, tiles)),
+            pl.BlockSpec((words, cols), at(down_steps + tiles, tiles)),
+            pl.BlockSpec((ENTRIES, cols), at(down_steps + tiles, tiles)),
+            fixed(order.shape),
         ],
-        out_specs=pl.BlockSpec((tokens, cols), lambda j: (0, j)),
-        out_shape=jax.ShapeDtypeStruct((tokens, width), F32),
-        cost_estimate=cost(4 * tokens * words * width, 4 * words * width),
-        name="up_product",
-    )(x_blocks, index, lookup)
-
-
-def down_kernel(og_ref, idx_ref, table_ref, out_ref):
-    count, _, block = out_ref.shape
-    tables = tables_of(table_ref)
-
-    @pl.when(pl.program_id(0) == 0)
-    def _():
-        out_ref[...] = jnp.zeros_like(out_ref)
-
-    def body(first, n):
-        for k in range(n):
-            out_ref[first + k] += contract_cols(
-                og_ref[...], decode_block(idx_ref, tables, first + k, block // 2)
-            )
-
-    grouped(count, 3, body)
-
-
-def down_product(out_grad, index, lookup):
-    tokens = out_grad.shape[0]
-    words, width = index.shape
-    cols = divisor(width, 512)
-    block = math.gcd(2 * words, 256)
-    count = 2 * words // block
-    return pl.pallas_call(
-        down_kernel,
-        grid=(width // cols,),
-        in_specs=[
-            pl.BlockSpec((tokens, cols), lambda j: (0, j)),
-            pl.BlockSpec((words, cols), lambda j: (0, j)),
-            pl.BlockSpec((ENTRIES, cols), lambda j: (0, j)),
+        out_specs=fixed(gathered),
+        out_shape=jax.ShapeDtypeStruct(gathered, BF16),
+        scratch_shapes=[
+            pltpu.VMEM((tiles, tokens, cols), F32),
+            pltpu.VMEM((2, chips) + blocks, BF16),
+            pltpu.VMEM((chips,) + blocks, BF16),
+            pltpu.VMEM((chips,) + blocks, BF16),
+            pltpu.VMEM((chips - 1,) + blocks, BF16),
+            pltpu.VMEM((2, 2, chips, rows, width), BF16),
+            pltpu.VMEM((2, chips, rows, width), BF16),
+            pltpu.VMEM((2, chips, rows, width), BF16),
+            pltpu.VMEM((2, chips - 1, rows, width), BF16),
+            pltpu.VMEM(gathered, BF16),
+            dma(()), dma(()), dma((chips - 1,)), dma((chips - 1,)),
+            dma((2, tiles)), dma((2, tiles)), dma((2, tiles, chips - 1)), dma((2, tiles, chips - 1)),
+            dma((tiles,)), dma((tiles,)), dma((tiles, chips - 1)), dma((tiles, chips - 1)),
+            dma((tiles, chips - 1)), dma((tiles, chips - 1)),
         ],
-        out_specs=pl.BlockSpec((count, tokens, block), lambda j: (0, 0, 0)),
-        out_shape=jax.ShapeDtypeStruct((count, tokens, block), F32),
-        cost_estimate=cost(4 * tokens * words * width, 4 * words * width),
-        name="down_product",
-    )(out_grad, index, lookup)
+        compiler_params=pltpu.CompilerParams(collective_id=1, has_side_effects=True),
+        cost_estimate=cost(12 * tokens * words * width, 12 * words * width),
+        name="hidden_grads",
+    )(
+        out_grad, x_blocks, down_index, down_table, gate_index, gate_table, up_index, up_table, order
+    )
+
+
+def local_hidden(pre_gate, pre_up, hidden_grad):
+    sig_gate = jax.nn.sigmoid(pre_gate)
+    silu_gate = pre_gate * sig_gate
+    activ = (silu_gate * pre_up).astype(BF16)
+    gate_grad = (hidden_grad * pre_up * sig_gate * (1.0 + pre_gate * (1.0 - sig_gate))).astype(BF16)
+    up_grad = (hidden_grad * silu_gate).astype(BF16)
+    return gate_grad, up_grad, activ
 
 
 def signed_sums(sums, value, signs):
@@ -234,13 +464,16 @@
 
 
 def grad_kernel(starts, shares, *refs):
-    left_ref, right_ref, total_ref, idx_ref, sign_ref, ones_ref, table_ref = refs[:7]
+    left_ref, hidden_ref, total_ref, idx_ref, sign_ref, ones_ref, table_ref = refs[:7]
     refs = refs[7:]
     if starts:
         start_ref, refs = refs[0], refs[1:]
-    out_ref, sum_ref, acc_ref = refs[:3]
-    values, leaves = refs[3:5], refs[5:7]
-    grad_ref = refs[7] if shares else sum_ref
+    out_ref, sum_ref, right_ref, acc_ref = refs[:4]
+    values, leaves = refs[4:6], refs[6:8]
+    grad_ref = refs[8] if shares else sum_ref
+    size, _, per, _ = hidden_ref.shape
+    for p in range(size):
+        right_ref[p * per : (p + 1) * per, :] = hidden_ref[p, 0]
     count, _, block = grad_ref.shape
     tables = tables_of(table_ref)
 
@@ -418,10 +651,6 @@
     return (row == col // SUB).astype(BF16)
 
 
-def fixed(shape):
-    return pl.BlockSpec(shape, lambda j: (0,) * len(shape))
-
-
 def bins_operands(left, total, right, index, most):
     count, block, tokens = left.shape
     words, width = index.shape
@@ -439,10 +668,13 @@
     return cols, specs, [left, right, total, index, sign_table(), group_ones()], scratch
 
 
-def grad_bins(left, total, right, index, lookup, start=None, shares=0):
+def grad_bins(left, total, hidden, which, index, lookup, start=None, shares=0):
     count, block, tokens = left.shape
     words, width = index.shape
-    cols, specs, args, scratch = bins_operands(left, total, right, index, 256)
+    cols, specs, args, scratch = bins_operands(left, total, hidden, index, 256)
+    size, _, rows, _ = hidden.shape
+    specs[1] = pl.BlockSpec((size, 1, rows, cols), lambda j: (0, which, 0, j))
+    scratch = [pltpu.VMEM((tokens, cols), BF16)] + scratch
     specs.append(pl.BlockSpec((ENTRIES, cols), lambda j: (0, j)))
     args.append(lookup)
     blocks = (count, tokens, block)
@@ -536,98 +768,26 @@
     return jnp.swapaxes(out.astype(array.dtype), 0, 1)
 
 
-def from_blocks(blocks):
-    count, rows, block = blocks.shape
-    out = lax.dot_general(
-        blocks, pairing(block, blocks.dtype), (((2,), (1,)), ((), ())), precision=lax.Precision.HIGHEST,
-        preferred_element_type=F32,
-    )
-    return jnp.swapaxes(out, 0, 1).reshape(rows, count * block)
-
-
-def shift(array, axis, size, by):
-    return lax.ppermute(array, axis, [(i, i ^ by) for i in range(size)])
-
-
-def axis_bits(size):
-    return [1 << i for i in range(size.bit_length() - 1)]
-
-
-def power_of_two(size):
-    return size & (size - 1) == 0
-
-
-def sum_scatter(array, axis, dim):
-    size = lax.axis_size(axis)
-    if not power_of_two(size):
-        return lax.psum_scatter(array, axis, scatter_dimension=dim, tiled=True)
-    me = lax.axis_index(axis)
-    shape = array.shape
-    rows = shape[dim] // size
-    left = size
-    for bit in axis_bits(size):
-        left //= 2
-        pairs = array.reshape(shape[:dim] + (left, 2, rows) + shape[dim + 1 :])
-        mine = jnp.bitwise_and(me // bit, 1)
-        sent = lax.dynamic_index_in_dim(pairs, 1 - mine, dim + 1, False).astype(BF16)
-        kept = lax.dynamic_index_in_dim(pairs, mine, dim + 1, False)
-        array = kept + shift(sent, axis, size, bit).astype(F32)
-    return array.reshape(shape[:dim] + (rows,) + shape[dim + 1 :])
-
-
-def gather(array, axis):
-    size = lax.axis_size(axis)
-    if not power_of_two(size):
-        return lax.all_gather(array, axis, axis=0, tiled=True)
-    me = lax.axis_index(axis)
-    rows, cols = array.shape
-    array = array[None]
-    for bit in reversed(axis_bits(size)):
-        other = shift(array, axis, size, bit)
-        first = jnp.bitwise_and(me // bit, 1) == 0
-        low, high = jnp.where(first, array, other), jnp.where(first, other, array)
-        array = jnp.stack([low, high], axis=1).reshape(-1, rows, cols)
-    return array.reshape(size * rows, cols)
-
-
-def after(array, *done):
-    return lax.optimization_barrier((array, *done))[0]
-
-
-def local_hidden(pre_gate, pre_up, hidden_grad):
-    sig_gate = jax.nn.sigmoid(pre_gate)
-    silu_gate = pre_gate * sig_gate
-    activ = (silu_gate * pre_up).astype(BF16)
-    gate_grad = (hidden_grad * pre_up * sig_gate * (1.0 + pre_gate * (1.0 - sig_gate))).astype(BF16)
-    up_grad = (hidden_grad * silu_gate).astype(BF16)
-    return activ, gate_grad, up_grad
-
-
 def shards(inputs, out_grad, gate_index, up_index, down_index, gate_table, up_table, down_table):
     tokens = inputs.shape[0]
-    hid_blocks = down_product(out_grad, down_index, down_table)
-    hid = sum_scatter(hid_blocks, "inp", 1)
+    width = gate_index.shape[1]
     x_blocks = to_blocks(inputs)
+    order = pairing(x_blocks.shape[2], BF16)
+    hidden = hidden_grads(
+        x_blocks, out_grad, gate_index, up_index, down_index, gate_table, up_table, down_table,
+        pairing(math.gcd(width, 256), BF16),
+    )
     x_turned = jnp.swapaxes(x_blocks, 1, 2)
     x_total = row_totals(inputs)
-    pre_gate = up_product(x_blocks, gate_index, after(gate_table, hid_blocks))
-    gate_share = sum_scatter(pre_gate, "inp", 0)
-    pre_up = up_product(x_blocks, up_index, after(up_table, pre_gate))
-    up_share = sum_scatter(pre_up, "inp", 0)
-    activ, gate_grad, up_grad = local_hidden(gate_share, up_share, from_blocks(hid))
-    gate_grad = gather(gate_grad, "inp")
-    up_grad = gather(after(up_grad, gate_grad), "inp")
-    acts = gather(after(activ, gate_grad), "inp")
-    gate_part, din_blocks = grad_bins(x_turned, x_total, gate_grad, gate_index, gate_table)
+    acts = hidden[:, 2].reshape(tokens, width)
+    gate_part, din_blocks = grad_bins(x_turned, x_total, hidden, 0, gate_index, gate_table)
     up_part, shares = grad_bins(
-        x_turned, x_total, after(up_grad, gate_part), up_index, up_table, din_blocks, lax.axis_size("hid")
+        x_turned, x_total, hidden, 1, up_index, up_table, din_blocks, lax.axis_size("hid")
     )
     sums = down_bins(
         jnp.swapaxes(to_blocks(acts), 1, 2), row_totals(acts), out_grad, down_index, gate_part, up_part, shares
     )
-    down_sum, gate_sum, up_sum, input_grad = finish(
-        *sums, pairing(x_blocks.shape[2], BF16), 1.0 / (tokens * ENTRIES)
-    )
+    down_sum, gate_sum, up_sum, input_grad = finish(*sums, order, 1.0 / (tokens * ENTRIES))
     return input_grad, gate_sum, up_sum, down_sum
 
 

time: 303 us -> 275 us (0.908)
  waiting for transfers between devices: 14.2 us -> 0 us
  Pallas kernels: 249 us -> 262 us
  starting transfers between devices: 10.2 us -> 0 us
  local copies, waits for them, and re-layouts: 14.2 us -> 5.25 us
  other arithmetic: 10.1 us -> 1.72 us
    pallas_call x3 -> x1, Pallas kernels: 56.7 us -> 71.1 us  [hidden_grads(): pl.pallas_call(functools.partial(hidden_kernel, size, down_steps), grid=(...]
    ppermute x12 -> x0, waiting for transfers between devices: 14.2 us -> none  [shift(): return lax.ppermute(array, axis, [(i, i ^ by) for i in range(size)])]
    ppermute x12 -> x0, starting transfers between devices: 10.2 us -> none  [shift(): return lax.ppermute(array, axis, [(i, i ^ by) for i in range(size)])]
    convert_element_type x6 -> x0, local copies, waits for them, and re-layouts: 7.61 us -> none  [sum_scatter(): lax.dynamic_index_in_dim(pairs, 1 - mine, dim + 1, False).astype(BF16)]
    add x3 -> x0, other arithmetic: 3.28 us -> none  [sum_scatter(): array = kept + shift(sent, axis, size, bit).astype(F32)]
  transfers between devices with their start and end apart: 12 -> 0, of which waited for: 6 -> 0; matrix products, arithmetic and copies ran while one was open for 7% -> 0% of each run, Pallas kernels for 32% -> 0%
where the time goes in v3:
time: 275 us; the launch traced here: 274 us
  Pallas kernels  262 us (95%)
  local copies, waits for them, and re-layouts  5.25 us (2%)
  matrix products  4.58 us (2%)
    pallas_call x2, Pallas kernels, grad_bins(): pl.pallas_call(functools.partial(grad_kernel, start is not None, shares),...  114 us
    pallas_call x1, Pallas kernels, down_bins(): pl.pallas_call(functools.partial(down_bins_kernel, n_hid, n_inp), grid=(s...  73.4 us
    pallas_call x1, Pallas kernels, hidden_grads(): pl.pallas_call(functools.partial(hidden_kernel, size, down_steps), grid=(...  71.1 us

profile of v3, /device:TPU:0, one launch (start us, length us, event | category | flops | bytes accessed | tf_op | source)
XLA Modules:
  0.0 274.0 jit_solution(2295560709216150000)
XLA Ops:
  0.6 1.7 convolution_convert_fusion
  2.4 0.0 copy-start.2
  2.4 1.3 copy.19.refs_1_
  3.7 0.7 fusion.4.refs_8_.order_ref
  4.4 0.0 copy-start.1
  4.4 71.1 %hidden_grads.1.refs_1_ = bf16[4,3,32,3328]{3,2,1,0:T(8,128)(2,1)} custom-call(bf16[128,4096]{1,0:T(8,128)(2,1)} %refs_1_.1, bf16[16,128,256]{2,1,0:T(8,128)(2,1)} %copy.19.refs_1_, s32[1664,4096]{1,0:T(8,128)} %refs_3_.7, f32[16,4096]{1,0:T(8,128)} %refs_3_.4, s32[2048,3328]{1,0:T(8,128)} %refs_3_.5, f32[16,3328]{1,0:T(8,128)} %refs_6_.4, ...), custom_call_target="tpu_custom_call" | custom-call | flops 10468982784 | bytes 81788928 | tf_op jit(solution)/shard_map/hidden_grads/pallas_call | solution.py:335
  75.5 0.0 copy-done.2
  75.6 0.1 sub.53
  75.6 0.7 broadcast_in_dim.14.refs_4_
  76.3 0.6 fusion.11.refs_5_
  76.9 0.0 copy-done.1
  76.9 0.2 convert_reduce_fusion
  77.2 0.7 broadcast_in_dim.15.refs_2_
  77.9 57.2 %grad_bins.2 = (f32[16,3328]{1,0:T(8,128)}, f32[16,128,256]{2,1,0:T(8,128)}) custom-call(bf16[16,256,128]{2,1,0:T(8,128)(2,1)} %bitcast.19, bf16[4,3,32,3328]{3,2,1,0:T(8,128)(2,1)} %hidden_grads.1.refs_1_, f32[128,128]{1,0:T(8,128)} %broadcast_in_dim.15.refs_2_, s32[2048,3328]{1,0:T(8,128)} %refs_3_.5, bf16[64,128]{1,0:T(8,128)(2,1)} %broadcast_in_dim.14.refs_4_, ...), custom_call_target="tpu_custom_call" | custom-call | flops 34896609280 | bytes 27262976 | tf_op jit(solution)/shard_map/grad_bins/pallas_call | solution.py:689
  135.1 0.0 slice-start
  135.1 57.3 %grad_bins.3 = (f32[16,3328]{1,0:T(8,128)}, bf16[8,16,16,256]{3,2,1,0:T(8,128)(2,1)}) custom-call(bf16[16,256,128]{2,1,0:T(8,128)(2,1)} %bitcast.20, bf16[4,3,32,3328]{3,2,1,0:T(8,128)(2,1)} %hidden_grads.1.refs_1_, f32[128,128]{1,0:T(8,128)} %broadcast_in_dim.15.refs_2_, s32[2048,3328]{1,0:T(8,128)} %refs_3_.6, bf16[64,128]{1,0:T(8,128)(2,1)} %broadcast_in_dim.14.refs_4_, ...), custom_call_target="tpu_custom_call" | custom-call | flops 34896609280 | bytes 27262976 | tf_op jit(solution)/shard_map/grad_bins/pallas_call | solution.py:689
  192.3 0.0 copy-start
  192.3 0.0 slice-done
  192.4 1.6 reshape_reshape_squeeze.3
  193.9 2.9 %fusion.refs_0_ = bf16[13,256,128]{2,1,0:T(8,128)(2,1)} fusion(bf16[128,13,256]{2,1,0:T(8,128)(2,1)} %reshape_reshape_squeeze.3, s32[256]{0:T(256)S(1)} %fusion.15), kind=kOutput, calls=%fused_computation.4 | convolution fusion | flops 218595328 | bytes 1704960 | tf_op jit(solution)/shard_map/dot_general | solution.py:764
  196.8 0.0 copy-done
  196.8 0.2 convert_reduce_fusion.1
  197.0 0.1 broadcast_in_dim.12
  197.1 0.7 broadcast_in_dim.13.refs_2_
  197.8 73.4 %down_bins.1 = (f32[8,2,4096]{2,1,0:T(2,128)}, f32[16,3328]{1,0:T(8,128)}, f32[16,3328]{1,0:T(8,128)}, f32[16,16,256]{2,1,0:T(8,128)}) custom-call(bf16[13,256,128]{2,1,0:T(8,128)(2,1)} %fusion.refs_0_, bf16[128,4096]{1,0:T(8,128)(2,1)} %refs_1_.1, f32[128,128]{1,0:T(8,128)} %broadcast_in_dim.13.refs_2_, s32[1664,4096]{1,0:T(8,128)} %refs_3_.7, ...), custom_call_target="tpu_custom_call" | custom-call | flops 34896609280 | bytes 27262976 | tf_op jit(solution)/shard_map/down_bins/pallas_call | solution.py:731
  271.3 2.7 finish.1
  (3 shorter events, 0.0 us)
Async XLA Ops:
  2.4 73.2 %copy-start.2 = (bf16[256,128,16]{1,0,2:T(8,128)(2,1)}, bf16[256,128,16]{1,0,2:T(8,128)(2,1)S(1)}, u32[]{:S(2)}) copy-start(bf16[256,128,16]{1,0,2:T(8,128)(2,1)S(1)} %convolution_convert_fusion) | copy-start | bytes 3145732
  4.4 72.5 %copy-start.1 = (bf16[128,4096]{1,0:T(8,128)(2,1)S(1)}, bf16[128,4096]{1,0:T(8,128)(2,1)}, u32[]{:S(2)}) copy-start(bf16[128,4096]{1,0:T(8,128)(2,1)} %param.8) | copy-start | bytes 3145732
  135.1 57.3 %slice-start = ((bf16[4,3,32,3328]{3,2,1,0:T(8,128)(2,1)}), bf16[4,1,32,3328]{3,2,1,0:T(8,128)(2,1)S(1)}, s32[]{:S(2)}) async-start(bf16[4,3,32,3328]{3,2,1,0:T(8,128)(2,1)} %hidden_grads.1.refs_1_), calls=%async_computation | async-start | bytes 1703936 | tf_op jit(solution)/shard_map/slice | solution.py:782
  192.3 4.5 %copy-start = (bf16[4,3,32,3328]{3,2,1,0:T(8,128)(2,1)S(1)}, bf16[4,3,32,3328]{3,2,1,0:T(8,128)(2,1)}, u32[]{:S(2)}) copy-start(bf16[4,3,32,3328]{3,2,1,0:T(8,128)(2,1)} %hidden_grads.1.refs_1_) | copy-start | bytes 7667716

commit v4 on v3

--- a/solution.py
+++ b/solution.py
@@ -3,6 +3,7 @@
 
 import jax
 import jax.numpy as jnp
+import numpy as np
 from jax import lax
 from jax.experimental import pallas as pl
 from jax.experimental.pallas import tpu as pltpu
@@ -38,8 +39,8 @@
 
 
 def nibbles(words):
-    low = jnp.bitwise_and(words.astype(jnp.int16), jnp.int16(15))
-    return low, jnp.right_shift(words, 4).astype(jnp.int16)
+    words = words.astype(jnp.int16)
+    return jnp.bitwise_and(words, jnp.int16(15)), lax.shift_right_logical(words, jnp.int16(4))
 
 
 def fixed(shape):
@@ -82,9 +83,11 @@
         body(count - count % size, count % size)
 
 
-LAG_CHIP = 2
-LAG_HIDDEN = 5
-LAG_RELAY = 8
+LAG_CHIP = 1
+LAG_HIDDEN = 3
+LAG_RELAY = 5
+HIDDEN_FROM = 5
+RELAY_FROM = 7
 
 
 def mesh_copy(src, dst, send, recv, **device):
@@ -168,8 +171,11 @@
         for k, there in far:
             hid_far(k, there).start()
 
-    def chip_sum(u):
-        a, tile = u // tiles, lax.rem(u, tiles)
+    def chip_sum(tile):
+        for a in range(2):
+            chip_part(a, tile)
+
+    def chip_part(a, tile):
         lanes = lanes_of(tile)
         sib_copy(a, tile).wait_recv()
         for c in range(chips):
@@ -217,30 +223,28 @@
         pl.semaphore_wait(barrier, chips)
         hid_acc[...] = jnp.zeros_like(hid_acc)
 
-    @pl.when(step == down_steps + LAG_CHIP)
-    def _():
-        hid_sum()
-
     unit = step - down_steps - LAG_CHIP
 
     @pl.when(unit >= 0)
     def _():
         chip_sum(unit)
 
-    ready = step - down_steps - tiles - LAG_HIDDEN
-
-    @pl.when(ready == 0)
+    turn = step - down_steps
+
+    @pl.when(turn == HIDDEN_FROM)
     def _():
         for k, there in far:
             hid_far(k, there).wait_recv()
 
-    @pl.when(ready >= 0)
-    def _():
-        hidden(ready)
-
-    @pl.when(step >= down_steps + tiles + LAG_RELAY)
-    def _():
-        relay(step - down_steps - tiles - LAG_RELAY)
+    @pl.when(turn >= HIDDEN_FROM)
+    def _():
+        now = turn - LAG_HIDDEN
+        repeat(jnp.where(turn == HIDDEN_FROM, 0, now), now + 1, hidden)
+
+    @pl.when(turn >= RELAY_FROM)
+    def _():
+        now = turn - LAG_RELAY
+        repeat(jnp.where(turn == RELAY_FROM, 0, now), now + 1, relay)
 
     @pl.when(step < down_steps)
     def _():
@@ -263,38 +267,41 @@
                     hid_part[s, c, i] = hid_acc[i, first : first + rows, :].astype(BF16)
         hid_copy().start()
 
-    def product(a, idx_ref, table_ref, tile):
-        tables = tables_of(table_ref)
-        pre_ref = hid_acc.at[0]
-        pre_ref[...] = jnp.zeros_like(pre_ref)
+    def product(tile):
+        tables = tables_of(gate_table), tables_of(up_table)
+        pre = hid_acc.at[0], hid_acc.at[1]
+        for pre_ref in pre:
+            pre_ref[...] = jnp.zeros_like(pre_ref)
 
         def body(first, n):
-            pre_ref[...] += sum(
-                jnp.dot(
-                    x_ref[first + k], decode_block(idx_ref, tables, first + k, block // 2),
-                    preferred_element_type=F32,
+            for a, idx_ref in enumerate((gate_ref, up_ref)):
+                pre[a][...] += sum(
+                    jnp.dot(
+                        x_ref[first + k], decode_block(idx_ref, tables[a], first + k, block // 2),
+                        preferred_element_type=F32,
+                    )
+                    for k in range(n)
                 )
-                for k in range(n)
-            )
 
         grouped(count, 8, body)
-        for c in range(chips):
-            for s in range(2):
-                first = (2 * c + s) * rows
-                part[a, s, c, :, lanes_of(tile)] = pre_ref[first : first + rows, :].astype(BF16)
-        sib_copy(a, tile).start()
-
-    @pl.when(jnp.logical_and(step >= down_steps, step < down_steps + tiles))
-    def _():
-        product(0, gate_ref, gate_table, step - down_steps)
-
-    @pl.when(step >= down_steps + tiles)
-    def _():
-        product(1, up_ref, up_table, step - down_steps - tiles)
+        for a in range(2):
+            for c in range(chips):
+                for s in range(2):
+                    first = (2 * c + s) * rows
+                    part[a, s, c, :, lanes_of(tile)] = pre[a][first : first + rows, :].astype(BF16)
+            sib_copy(a, tile).start()
+
+    @pl.when(step >= down_steps)
+    def _():
+        product(step - down_steps)
+
+    @pl.when(turn == 0)
+    def _():
+        hid_sum()
 
     @pl.when(step == steps - 1)
     def _():
-        repeat(2 * tiles - LAG_CHIP, 2 * tiles, chip_sum)
+        repeat(tiles - LAG_CHIP, tiles, chip_sum)
         repeat(tiles - LAG_HIDDEN, tiles, hidden)
         repeat(tiles - LAG_RELAY, tiles, relay)
         hid_copy().wait_send()
@@ -334,7 +341,7 @@
     dma = pltpu.SemaphoreType.DMA
     return pl.pallas_call(
         functools.partial(hidden_kernel, size, down_steps),
-        grid=(down_steps + 2 * tiles,),
+        grid=(down_steps + tiles,),
         in_specs=[
             pl.BlockSpec((tokens, wide), at(0, down_steps)),
             fixed((count, tokens, block)),
@@ -342,8 +349,8 @@
             pl.BlockSpec((ENTRIES, wide), at(0, down_steps)),
             pl.BlockSpec((words, cols), at(down_steps, tiles)),
             pl.BlockSpec((ENTRIES, cols), at(down_steps, tiles)),
-            pl.BlockSpec((words, cols), at(down_steps + tiles, tiles)),
-            pl.BlockSpec((ENTRIES, cols), at(down_steps + tiles, tiles)),
+            pl.BlockSpec((words, cols), at(down_steps, tiles)),
+            pl.BlockSpec((ENTRIES, cols), at(down_steps, tiles)),
             fixed(order.shape),
         ],
         out_specs=fixed(gathered),
@@ -382,129 +389,158 @@
 
 
 def signed_sums(sums, value, signs):
-    parts = [value]
-    for sign in signs:
-        parts = parts + [sign * part for part in parts]
-    parts = parts[1:]
-    return parts if sums is None else [a + b for a, b in zip(sums, parts)]
-
-
-def bins_tile(left_ref, right_ref, total_ref, idx_ref, sign_ref, ones_ref, acc_ref, values, leaves, grad):
-    count, block, _ = left_ref.shape
-    half = block // 2
-    cols = idx_ref.shape[1]
-    signs = [sign_ref[SUB * b : SUB * b + SUB, :] for b in range(4)]
-    acc_ref[...] = jnp.zeros_like(acc_ref)
-    leaves[0][0:SUB, :] = jnp.zeros((SUB, cols), BF16)
-    leaves[1][...] = jnp.zeros_like(leaves[1])
-
-    def make(i, slot):
-        values[slot][...] = jnp.dot(left_ref[i], right_ref[...], preferred_element_type=F32)
-
-    def use(i, slot):
-        for lanes in lane_chunks(cols):
-            runs = []
-            sums = None
-            for step in range(half // SUB):
-                row = pl.multiple_of(i * half + step * SUB, SUB)
-                for parity, index in enumerate(nibbles(idx_ref[pl.ds(row, SUB), lanes])):
-                    first = parity * half + step * SUB
-                    value = values[slot][first : first + SUB, lanes].astype(BF16)
-                    sums = signed_sums(sums, value, [look_up(sign, index) for sign in signs])
-                if step % 4 == 3 or step == half // SUB - 1:
-                    runs.append(sums)
-                    sums = None
-            while len(runs) > 1:
-                runs = [[a + b for a, b in zip(*runs[:2])]] + runs[2:]
-            for a, total in enumerate(runs[0]):
-                leaves[slot][SUB * (a + 1) : SUB * (a + 2), lanes] = total
-
-    def close(slot):
-        acc_ref[...] += jnp.dot(ones_ref[...], leaves[slot][...], preferred_element_type=F32)
-
-    make(0, 0)
-
-    def body(j, carry):
-        close(1)
-        make(2 * j + 1, 1)
-        grad(2 * j)
-        grad(2 * j + 1)
-        use(2 * j, 0)
-        close(0)
-        make(jnp.minimum(2 * j + 2, count - 1), 0)
-        use(2 * j + 1, 1)
-        return carry
-
-    lax.fori_loop(0, count // 2, body, 0)
-    close(1)
-    if count % 2:
-        grad(count - 1)
-        use(count - 1, 0)
-        close(0)
+    out = [None] * ENTRIES
+
+    def walk(part, bits, chosen):
+        if chosen:
+            out[chosen] = part if sums is None else sums[chosen - 1] + part
+        for bit in range(bits):
+            walk(signs[bit] * part, bit, chosen | 1 << bit)
+
+    walk(value, len(signs), 0)
+    return out[1:]
+
+
+def start_bins(accs, leaf_ref):
+    for acc_ref in accs:
+        acc_ref[...] = jnp.zeros_like(acc_ref)
+    leaf_ref[...] = jnp.zeros_like(leaf_ref)
+
+
+def make_values(left_ref, right_ref, i, value_ref):
+    value_ref[...] = jnp.dot(left_ref[i], right_ref[...], preferred_element_type=F32)
+
+
+def add_signed(idx_ref, signs, i, value_ref, tables=None):
+    half = value_ref.shape[0] // 2
+    leaves, weights = [], []
+    for c, lanes in enumerate(lane_chunks(idx_ref.shape[1])):
+        runs, sums, pieces = [], None, ([], [])
+        for step in range(half // SUB):
+            row = pl.multiple_of(i * half + step * SUB, SUB)
+            for parity, index in enumerate(nibbles(idx_ref[pl.ds(row, SUB), lanes])):
+                first = parity * half + step * SUB
+                if tables is not None:
+                    pieces[parity].append(look_up(tables[c], index))
+                value = value_ref[first : first + SUB, lanes].astype(BF16)
+                sums = signed_sums(sums, value, [look_up(sign, index) for sign in signs])
+            if step % 4 == 3 or step == half // SUB - 1:
+                runs.append(sums)
+                sums = None
+        while len(runs) > 1:
+            runs = [[a + b for a, b in zip(*runs[:2])]] + runs[2:]
+        leaves.append(runs[0])
+        if tables is not None:
+            weights.append(jnp.concatenate(pieces[0] + pieces[1], axis=0))
+    return leaves, jnp.concatenate(weights, axis=1) if weights else None
+
+
+def keep_leaves(leaves, leaf_ref):
+    for c, sums in enumerate(leaves):
+        for a, total in enumerate(sums):
+            leaf_ref[SUB * (a + 1) : SUB * (a + 2), c * LANES : (c + 1) * LANES] = total
+
+
+def close_now(ones_ref, leaves, acc_ref):
+    blank = jnp.zeros((SUB, LANES), BF16)
+    whole = jnp.concatenate([jnp.concatenate([blank] + sums, axis=0) for sums in leaves], axis=1)
+    acc_ref[...] += jnp.dot(ones_ref[...], whole, preferred_element_type=F32)
+
+
+def close_block(ones_ref, leaf_ref, acc_ref):
+    acc_ref[...] += jnp.dot(ones_ref[...], leaf_ref[...], preferred_element_type=F32)
+
+
+def all_sums(acc_ref, right_ref, total_ref):
     whole = jnp.concatenate(
         [
             jnp.sum(right_ref[:, lanes].astype(F32) * total_ref[...], axis=0, keepdims=True)
-            for lanes in lane_chunks(cols)
+            for lanes in lane_chunks(right_ref.shape[1])
         ],
         axis=1,
     )
     return [whole] + [acc_ref[k : k + 1, :] for k in range(1, ENTRIES)]
 
 
-def entry_sums(sums):
-    step = 1
-    while step < ENTRIES:
-        mixed = list(sums)
-        for k in range(ENTRIES):
-            if not k & step:
-                mixed[k], mixed[k | step] = sums[k] + sums[k | step], sums[k] - sums[k | step]
-        sums = mixed
-        step *= 2
-    return sums
-
-
-def grad_kernel(starts, shares, *refs):
-    left_ref, hidden_ref, total_ref, idx_ref, sign_ref, ones_ref, table_ref = refs[:7]
-    refs = refs[7:]
-    if starts:
-        start_ref, refs = refs[0], refs[1:]
-    out_ref, sum_ref, right_ref, acc_ref = refs[:4]
-    values, leaves = refs[4:6], refs[6:8]
-    grad_ref = refs[8] if shares else sum_ref
-    size, _, per, _ = hidden_ref.shape
+def signs_of(sign_ref):
+    return [sign_ref[SUB * b : SUB * b + SUB, :] for b in range(4)]
+
+
+def bins_tile(left_ref, right_ref, total_ref, idx_ref, sign_ref, ones_ref, acc_ref, values, leaf_ref):
+    count = left_ref.shape[0]
+    signs = signs_of(sign_ref)
+    start_bins([acc_ref], leaf_ref)
+    make_values(left_ref, right_ref, 0, values[0])
+
+    def body(j, carry):
+        close_block(ones_ref, leaf_ref, acc_ref)
+        make_values(left_ref, right_ref, 2 * j + 1, values[1])
+        leaves, _ = add_signed(idx_ref, signs, 2 * j, values[0])
+        close_now(ones_ref, leaves, acc_ref)
+        make_values(left_ref, right_ref, jnp.minimum(2 * j + 2, count - 1), values[0])
+        leaves, _ = add_signed(idx_ref, signs, 2 * j + 1, values[1])
+        keep_leaves(leaves, leaf_ref)
+        return carry
+
+    lax.fori_loop(0, count // 2, body, 0)
+    close_block(ones_ref, leaf_ref, acc_ref)
+    if count % 2:
+        leaves, _ = add_signed(idx_ref, signs, count - 1, values[0])
+        close_now(ones_ref, leaves, acc_ref)
+    return all_sums(acc_ref, right_ref, total_ref)
+
+
+def grad_kernel(
+    left_ref, gate_hidden, up_hidden, total_ref, gate_idx, up_idx, sign_ref, ones_ref, gate_table, up_table,
+    gate_out, up_out, share_ref, gate_ref, up_ref, gate_acc, up_acc, gate_value, up_value, up_leaf, grad_ref,
+):
+    count, block, _ = left_ref.shape
+    half = block // 2
+    size, _, per, _ = gate_hidden.shape
+    signs = signs_of(sign_ref)
+    tables = tables_of(gate_table), tables_of(up_table)
+
+    @pl.when(pl.program_id(0) == 0)
+    def _():
+        grad_ref[...] = jnp.zeros_like(grad_ref)
+
     for p in range(size):
-        right_ref[p * per : (p + 1) * per, :] = hidden_ref[p, 0]
-    count, _, block = grad_ref.shape
-    tables = tables_of(table_ref)
-
-    @pl.when(pl.program_id(0) == 0)
-    def _():
-        grad_ref[...] = start_ref[...] if starts else jnp.zeros_like(grad_ref)
-
-    def grad(i):
-        grad_ref[i] += contract_cols(right_ref[...], decode_block(idx_ref, tables, i, block // 2))
-
-    sums = bins_tile(
-        left_ref, right_ref, total_ref, idx_ref, sign_ref, ones_ref, acc_ref, values, leaves, grad
-    )
-    for k, total in enumerate(entry_sums(sums)):
-        out_ref[k : k + 1, :] = total
-
-    if shares:
-        rows = sum_ref.shape[2]
-
-        @pl.when(pl.program_id(0) == pl.num_programs(0) - 1)
-        def _():
-            for p in range(shares):
-                sum_ref[p] = grad_ref[:, p * rows : (p + 1) * rows, :].astype(BF16)
+        gate_ref[p * per : (p + 1) * per, :] = gate_hidden[p, 0]
+        up_ref[p * per : (p + 1) * per, :] = up_hidden[p, 0]
+    start_bins([gate_acc, up_acc], up_leaf)
+    make_values(left_ref, gate_ref, 0, gate_value)
+
+    def body(i, carry):
+        close_block(ones_ref, up_leaf, up_acc)
+        make_values(left_ref, up_ref, i, up_value)
+        grad = contract_cols(up_ref[...], decode_block(up_idx, tables[1], i, half))
+        leaves, weights = add_signed(gate_idx, signs, i, gate_value, tables[0])
+        close_now(ones_ref, leaves, gate_acc)
+        grad_ref[i] += grad + contract_cols(gate_ref[...], weights)
+        make_values(left_ref, gate_ref, jnp.minimum(i + 1, count - 1), gate_value)
+        leaves, _ = add_signed(up_idx, signs, i, up_value)
+        keep_leaves(leaves, up_leaf)
+        return carry
+
+    lax.fori_loop(0, count, body, 0)
+    close_block(ones_ref, up_leaf, up_acc)
+    for out, acc_ref, right_ref in ((gate_out, gate_acc, gate_ref), (up_out, up_acc, up_ref)):
+        for k, total in enumerate(all_sums(acc_ref, right_ref, total_ref)):
+            out[k : k + 1, :] = total
+
+    @pl.when(pl.program_id(0) == pl.num_programs(0) - 1)
+    def _():
+        shares, _, rows, _ = share_ref.shape
+        for p in range(shares):
+            share_ref[p] = grad_ref[:, p * rows : (p + 1) * rows, :].astype(BF16)
 
 
 def down_bins_kernel(n_hid, n_inp, *refs):
     (left_ref, right_ref, total_ref, idx_ref, sign_ref, ones_ref, gate_ref, up_ref, shares_ref) = refs[:9]
     out_ref, gate_out, up_out, grad_out = refs[9:13]
-    acc_ref, values, leaves = refs[13], refs[14:16], refs[16:18]
-    (own_ref, got_ref, gate_got, up_got, part_ref, part_got, final_ref) = refs[18:25]
-    (own_sem, share_send, share_recv, table_send, table_recv, part_send, part_recv, final_send, final_recv) = refs[25:]
+    acc_ref, values, leaf_ref = refs[13], refs[14:16], refs[16]
+    (own_ref, got_ref, gate_got, up_got, part_ref, part_got, final_ref) = refs[17:24]
+    (own_sem, share_send, share_recv, table_send, table_recv, part_send, part_recv, final_send, final_recv) = refs[24:]
     step, steps = pl.program_id(0), pl.num_programs(0)
     hid, inp = lax.axis_index("hid"), lax.axis_index("inp")
     cols = idx_ref.shape[1]
@@ -576,9 +612,9 @@
         lax.fori_loop(0, steps - 1, early, 0)
 
     sums = bins_tile(
-        left_ref, right_ref, total_ref, idx_ref, sign_ref, ones_ref, acc_ref, values, leaves, lambda i: None
-    )
-    for k, total in enumerate(entry_sums(sums)):
+        left_ref, right_ref, total_ref, idx_ref, sign_ref, ones_ref, acc_ref, values, leaf_ref
+    )
+    for k, total in enumerate(sums):
         part_ref[k // rows, k % rows : k % rows + 1, lanes_of(step)] = total
     for k, peer in peers:
         part_copy(step, k, peer).start()
@@ -610,12 +646,16 @@
         out_ref[...] = final_ref[...]
 
 
-def finish_kernel(scale, down_ref, gate_ref, up_ref, grad_ref, order_ref, down_out, gate_out, up_out, grad_out):
+def finish_kernel(
+    scale, down_ref, gate_ref, up_ref, grad_ref, order_ref, signs_ref, down_out, gate_out, up_out, grad_out, down_all
+):
     groups, rows, _ = down_ref.shape
     for k in range(groups):
-        down_out[k * rows : (k + 1) * rows, :] = down_ref[k] * scale
-    gate_out[...] = gate_ref[...] * scale
-    up_out[...] = up_ref[...] * scale
+        down_all[k * rows : (k + 1) * rows, :] = down_ref[k]
+    for sums, out in ((down_all, down_out), (gate_ref, gate_out), (up_ref, up_out)):
+        out[...] = scale * jnp.dot(
+            signs_ref[...], sums[...], precision=lax.Precision.HIGHEST, preferred_element_type=F32
+        )
     count, _, block = grad_ref.shape
     for i in range(count):
         grad_out[:, i * block : (i + 1) * block] = contract_cols(
@@ -633,22 +673,27 @@
             jax.ShapeDtypeStruct(up.shape, F32),
             jax.ShapeDtypeStruct((rows, count * block), BF16),
         ],
+        scratch_shapes=[pltpu.VMEM((ENTRIES, down.shape[2]), F32)],
         cost_estimate=cost(rows * count * block * block, 8 * gate.size),
         name="finish",
-    )(down, gate, up, grad, order)
+    )(down, gate, up, grad, order, entry_signs())
+
+
+def entry_signs():
+    both = np.arange(ENTRIES)[:, None] & np.arange(ENTRIES)[None, :]
+    odd = sum(both >> bit & 1 for bit in range(4)) & 1
+    return jnp.asarray(1 - 2 * odd, F32)
 
 
 def sign_table():
-    entry = jnp.arange(ENTRIES)[None, :, None]
-    bit = jnp.arange(4)[:, None, None]
-    sign = 1 - 2 * jnp.bitwise_and(jnp.right_shift(entry, bit), 1)
-    return jnp.broadcast_to(sign, (4, ENTRIES, LANES)).reshape(4 * ENTRIES, LANES).astype(BF16)
+    entry = np.arange(ENTRIES)[None, :, None]
+    sign = 1 - 2 * (entry >> np.arange(4)[:, None, None] & 1)
+    return jnp.asarray(np.tile(sign, (1, 1, LANES)).reshape(4 * ENTRIES, LANES), BF16)
 
 
 def group_ones():
-    row = jnp.arange(ENTRIES)[:, None]
-    col = jnp.arange(ENTRIES * SUB)[None, :]
-    return (row == col // SUB).astype(BF16)
+    row = np.arange(ENTRIES)[:, None]
+    return jnp.asarray(row == np.arange(ENTRIES * SUB)[None, :] // SUB, BF16)
 
 
 def bins_operands(left, total, right, index, most):
@@ -664,45 +709,56 @@
         fixed((ENTRIES, ENTRIES * SUB)),
     ]
     scratch = [pltpu.VMEM((ENTRIES, cols), F32)]
-    scratch += [pltpu.VMEM((block, cols), F32)] * 2 + [pltpu.VMEM((ENTRIES * SUB, cols), BF16)] * 2
+    scratch += [pltpu.VMEM((block, cols), F32)] * 2 + [pltpu.VMEM((ENTRIES * SUB, cols), BF16)]
     return cols, specs, [left, right, total, index, sign_table(), group_ones()], scratch
 
 
-def grad_bins(left, total, hidden, which, index, lookup, start=None, shares=0):
+def grad_bins(left, total, hidden, gate_index, up_index, gate_table, up_table, shares):
     count, block, tokens = left.shape
-    words, width = index.shape
-    cols, specs, args, scratch = bins_operands(left, total, hidden, index, 256)
+    words, width = gate_index.shape
     size, _, rows, _ = hidden.shape
-    specs[1] = pl.BlockSpec((size, 1, rows, cols), lambda j: (0, which, 0, j))
-    scratch = [pltpu.VMEM((tokens, cols), BF16)] + scratch
-    specs.append(pl.BlockSpec((ENTRIES, cols), lambda j: (0, j)))
-    args.append(lookup)
-    blocks = (count, tokens, block)
-    if start is not None:
-        specs.append(fixed(blocks))
-        args.append(start)
-    if shares:
-        grad = jax.ShapeDtypeStruct((shares, count, tokens // shares, block), BF16)
-        scratch = scratch + [pltpu.VMEM(blocks, F32)]
-    else:
-        grad = jax.ShapeDtypeStruct(blocks, F32)
+    cols = divisor(width, 256)
+    index = pl.BlockSpec((words, cols), lambda j: (0, j))
+    table = pl.BlockSpec((ENTRIES, cols), lambda j: (0, j))
+    grad = (shares, count, tokens // shares, block)
     return pl.pallas_call(
-        functools.partial(grad_kernel, start is not None, shares),
+        grad_kernel,
         grid=(width // cols,),
-        in_specs=specs,
-        out_specs=[pl.BlockSpec((ENTRIES, cols), lambda j: (0, j)), fixed(grad.shape)],
-        out_shape=[jax.ShapeDtypeStruct((ENTRIES, width), F32), grad],
-        scratch_shapes=scratch,
-        cost_estimate=cost(40 * tokens * words * width, 4 * words * width),
+        in_specs=[
+            fixed((count, block, tokens)),
+            pl.BlockSpec((size, 1, rows, cols), lambda j: (0, 0, 0, j)),
+            pl.BlockSpec((size, 1, rows, cols), lambda j: (0, 1, 0, j)),
+            fixed((tokens, LANES)),
+            index,
+            index,
+            fixed((4 * ENTRIES, LANES)),
+            fixed((ENTRIES, ENTRIES * SUB)),
+            table,
+            table,
+        ],
+        out_specs=[table, table, fixed(grad)],
+        out_shape=[
+            jax.ShapeDtypeStruct((ENTRIES, width), F32),
+            jax.ShapeDtypeStruct((ENTRIES, width), F32),
+            jax.ShapeDtypeStruct(grad, BF16),
+        ],
+        scratch_shapes=[pltpu.VMEM((tokens, cols), BF16)] * 2
+        + [pltpu.VMEM((ENTRIES, cols), F32)] * 2
+        + [pltpu.VMEM((block, cols), F32)] * 2
+        + [pltpu.VMEM((ENTRIES * SUB, cols), BF16)]
+        + [pltpu.VMEM((count, tokens, block), F32)],
+        cost_estimate=cost(80 * tokens * words * width, 8 * words * width),
         name="grad_bins",
-    )(*args)
+    )(
+        left, hidden, hidden, total, gate_index, up_index, sign_table(), group_ones(), gate_table, up_table
+    )
 
 
 def down_bins(left, total, right, index, gate_part, up_part, shares):
     count, block, tokens = left.shape
     words, width = index.shape
     n_hid, n_inp = lax.axis_size("hid"), lax.axis_size("inp")
-    cols, specs, args, scratch = bins_operands(left, total, right, index, 512)
+    cols, specs, args, scratch = bins_operands(left, total, right, index, 256)
     steps = width // cols
     table = gate_part.shape
     share = shares.shape[1:]
@@ -752,10 +808,10 @@
 
 
 def pairing(block, dtype):
-    row = jnp.arange(block)[:, None]
-    col = jnp.arange(block)[None, :]
+    row = np.arange(block)[:, None]
+    col = np.arange(block)[None, :]
     half = block // 2
-    return (row == 2 * (col % half) + col // half).astype(dtype)
+    return jnp.asarray(row == 2 * (col % half) + col // half, dtype)
 
 
 def to_blocks(array):
@@ -780,9 +836,8 @@
     x_turned = jnp.swapaxes(x_blocks, 1, 2)
     x_total = row_totals(inputs)
     acts = hidden[:, 2].reshape(tokens, width)
-    gate_part, din_blocks = grad_bins(x_turned, x_total, hidden, 0, gate_index, gate_table)
-    up_part, shares = grad_bins(
-        x_turned, x_total, hidden, 1, up_index, up_table, din_blocks, lax.axis_size("hid")
+    gate_part, up_part, shares = grad_bins(
+        x_turned, x_total, hidden, gate_index, up_index, gate_table, up_table, lax.axis_size("hid")
     )
     sums = down_bins(
         jnp.swapaxes(to_blocks(acts), 1, 2), row_totals(acts), out_grad, down_index, gate_part, up_part, shares

time: 275 us -> 254 us (0.924)
  Pallas kernels: 262 us -> 243 us
    pallas_call x2 -> x1, Pallas kernels: 114 us -> 100 us  [grad_bins(): pl.pallas_call(grad_kernel, grid=(width // cols,), in_specs=[fixed((count...]
    pallas_call x1, Pallas kernels: 71.1 us -> 65.7 us  [hidden_grads(): pl.pallas_call(functools.partial(hidden_kernel, size, down_steps), grid=(...]
where the time goes in v4:
time: 254 us
  Pallas kernels  243 us (96%)
  local copies, waits for them, and re-layouts  3.73 us (1%)
  matrix products  3.45 us (1%)
  other arithmetic  2.82 us (1%)
    pallas_call x1, Pallas kernels, grad_bins(): pl.pallas_call(grad_kernel, grid=(width // cols,), in_specs=[fixed((count...  100 us
    pallas_call x1, Pallas kernels, down_bins(): pl.pallas_call(functools.partial(down_bins_kernel, n_hid, n_inp), grid=(s...  73.9 us
    pallas_call x1, Pallas kernels, hidden_grads(): pl.pallas_call(functools.partial(hidden_kernel, size, down_steps), grid=(...  65.7 us

profile of v4, /device:TPU:0, one launch (start us, length us, event | category | flops | bytes accessed | tf_op | source)
XLA Modules:
  0.0 253.8 jit_solution(9679214526053474426)
XLA Ops:
  0.6 1.5 convert_reduce_fusion
  2.1 0.7 broadcast_in_dim.16.total_ref
  2.8 1.8 convolution_convert_fusion
  4.6 0.0 copy-start
  4.6 1.3 copy.26.refs_1_
  5.9 65.7 %hidden_grads.1.gate_hidden.up_hidden = bf16[4,3,32,3328]{3,2,1,0:T(8,128)(2,1)} custom-call(bf16[128,4096]{1,0:T(8,128)(2,1)} %refs_1_.1, bf16[16,128,256]{2,1,0:T(8,128)(2,1)} %copy.26.refs_1_, s32[1664,4096]{1,0:T(8,128)} %refs_3_.3, f32[16,4096]{1,0:T(8,128)} %refs_3_.2, s32[2048,3328]{1,0:T(8,128)} %gate_idx.1, f32[16,3328]{1,0:T(8,128)} %gate_table.1, ...), custom_call_target="tpu_custom_call" | custom-call | flops 10468982784 | bytes 81788928 | tf_op jit(solution)/shard_map/hidden_grads/pallas_call | solution.py:342
  71.6 0.0 copy-done
  71.6 1.4 convert_reduce_fusion.1
  73.0 0.1 broadcast_in_dim.6
  73.1 0.7 broadcast_in_dim.7.refs_2_
  73.8 0.0 slice-start
  73.8 100.1 %grad_bins.1 = (f32[16,3328]{1,0:T(8,128)}, f32[16,3328]{1,0:T(8,128)}, bf16[8,16,16,256]{3,2,1,0:T(8,128)(2,1)}) custom-call(bf16[16,256,128]{2,1,0:T(8,128)(2,1)} %bitcast.15, bf16[4,3,32,3328]{3,2,1,0:T(8,128)(2,1)} %hidden_grads.1.gate_hidden.up_hidden, bf16[4,3,32,3328]{3,2,1,0:T(8,128)(2,1)} %hidden_grads.1.gate_hidden.up_hidden, ...), custom_call_target="tpu_custom_call" | custom-call | flops 69793218560 | bytes 54525952 | tf_op jit(solution)/shard_map/grad_bins/pallas_call | solution.py:724
  174.0 0.0 copy-start.1
  174.0 0.0 slice-done
  174.0 0.6 reshape_reshape_squeeze.3
  174.6 0.3 copy-done.1
  174.9 1.7 fusion.refs_0_
  176.5 73.9 %down_bins.1 = (f32[8,2,4096]{2,1,0:T(2,128)}, f32[16,3328]{1,0:T(8,128)}, f32[16,3328]{1,0:T(8,128)}, f32[16,16,256]{2,1,0:T(8,128)}) custom-call(bf16[13,256,128]{2,1,0:T(8,128)(2,1)} %fusion.refs_0_, bf16[128,4096]{1,0:T(8,128)(2,1)} %refs_1_.1, f32[128,128]{1,0:T(8,128)} %broadcast_in_dim.7.refs_2_, s32[1664,4096]{1,0:T(8,128)} %refs_3_.3, ...), custom_call_target="tpu_custom_call" | custom-call | flops 34896609280 | bytes 27262976 | tf_op jit(solution)/shard_map/down_bins/pallas_call | solution.py:787
  250.4 3.3 %finish.1 = (f32[16,4096]{1,0:T(8,128)}, f32[16,3328]{1,0:T(8,128)}, f32[16,3328]{1,0:T(8,128)}, bf16[16,4096]{1,0:T(8,128)(2,1)}) custom-call(f32[8,2,4096]{2,1,0:T(2,128)} %get-tuple-element.18.down_ref, f32[16,3328]{1,0:T(8,128)} %get-tuple-element.19.gate_ref, f32[16,3328]{1,0:T(8,128)} %get-tuple-element.20.up_ref, ...), custom_call_target="tpu_custom_call" | custom-call | flops 16777216 | bytes 425984 | tf_op jit(solution)/shard_map/finish/pallas_call | solution.py:668
Async XLA Ops:
  4.6 67.0 %copy-start = (bf16[256,128,16]{1,0,2:T(8,128)(2,1)}, bf16[256,128,16]{1,0,2:T(8,128)(2,1)S(1)}, u32[]{:S(2)}) copy-start(bf16[256,128,16]{1,0,2:T(8,128)(2,1)S(1)} %convolution_convert_fusion) | copy-start | bytes 3145732
  73.8 100.2 %slice-start = ((bf16[4,3,32,3328]{3,2,1,0:T(8,128)(2,1)}), bf16[4,1,32,3328]{3,2,1,0:T(8,128)(2,1)S(1)}, s32[]{:S(2)}) async-start(bf16[4,3,32,3328]{3,2,1,0:T(8,128)(2,1)} %hidden_grads.1.gate_hidden.up_hidden), calls=%async_computation | async-start | bytes 1703936 | tf_op jit(solution)/shard_map/slice | solution.py:838
  174.0 0.9 copy-start.1

commit v5 on v4

--- a/solution.py
+++ b/solution.py
@@ -83,6 +83,7 @@
         body(count - count % size, count % size)
 
 
+LATE_TILES = 4
 LAG_CHIP = 1
 LAG_HIDDEN = 3
 LAG_RELAY = 5
@@ -202,7 +203,7 @@
         gate_grad, up_grad, activ = local_hidden(shares[0], shares[1], grad)
         all_ref[me, 0, :, lanes] = gate_grad
         all_ref[me, 1, :, lanes] = up_grad
-        all_ref[me, 2, :, lanes] = activ
+        all_ref[me, 2, :, lanes] = jnp.dot(activ, order_ref[...], preferred_element_type=F32).astype(BF16)
         pair_copy(tile).start()
         for k, there in far:
             far_copy(tile, k, there).start()
@@ -256,7 +257,7 @@
                     og_ref[...], decode_block(down_ref, tables, first + k, cols // 2)
                 )
 
-        grouped(hid_count, 3, body)
+        grouped(hid_count, 7, body)
 
     @pl.when(step == down_steps - 1)
     def _():
@@ -283,7 +284,7 @@
                     for k in range(n)
                 )
 
-        grouped(count, 8, body)
+        grouped(count, 16, body)
         for a in range(2):
             for c in range(chips):
                 for s in range(2):
@@ -451,22 +452,35 @@
     acc_ref[...] += jnp.dot(ones_ref[...], leaf_ref[...], preferred_element_type=F32)
 
 
-def all_sums(acc_ref, right_ref, total_ref):
-    whole = jnp.concatenate(
-        [
-            jnp.sum(right_ref[:, lanes].astype(F32) * total_ref[...], axis=0, keepdims=True)
-            for lanes in lane_chunks(right_ref.shape[1])
-        ],
-        axis=1,
-    )
-    return [whole] + [acc_ref[k : k + 1, :] for k in range(1, ENTRIES)]
+def take_totals(left_ref, total_ref):
+    count, block, tokens = left_ref.shape
+    totals = [jnp.zeros((8, tokens), F32)] * 8
+    for i in range(count):
+        for first in range(0, block, SUB):
+            rows = left_ref[i, first : first + SUB, :].astype(F32)
+            k = first // SUB % 4 * 2
+            totals[k : k + 2] = totals[k] + rows[:8], totals[k + 1] + rows[8:]
+    total = sum(totals)
+    rest = jnp.broadcast_to(jnp.sum(total, axis=0, keepdims=True), total_ref.shape)
+    row = lax.broadcasted_iota(jnp.int32, total_ref.shape, 0)
+    parts = jnp.zeros(total_ref.shape, F32)
+    for k in range(3):
+        part = rest.astype(BF16).astype(F32)
+        parts = jnp.where(row == k, part, parts)
+        rest = rest - part
+    total_ref[...] = parts.astype(BF16)
+
+
+def empty_sum(right_ref, total_ref):
+    whole = jnp.dot(total_ref[...], right_ref[...], preferred_element_type=F32)
+    return whole[:1] + whole[1:2] + whole[2:3]
 
 
 def signs_of(sign_ref):
     return [sign_ref[SUB * b : SUB * b + SUB, :] for b in range(4)]
 
 
-def bins_tile(left_ref, right_ref, total_ref, idx_ref, sign_ref, ones_ref, acc_ref, values, leaf_ref):
+def bins_tile(left_ref, right_ref, idx_ref, sign_ref, ones_ref, acc_ref, values, leaf_ref):
     count = left_ref.shape[0]
     signs = signs_of(sign_ref)
     start_bins([acc_ref], leaf_ref)
@@ -487,12 +501,12 @@
     if count % 2:
         leaves, _ = add_signed(idx_ref, signs, count - 1, values[0])
         close_now(ones_ref, leaves, acc_ref)
-    return all_sums(acc_ref, right_ref, total_ref)
 
 
 def grad_kernel(
-    left_ref, gate_hidden, up_hidden, total_ref, gate_idx, up_idx, sign_ref, ones_ref, gate_table, up_table,
+    left_ref, gate_hidden, up_hidden, gate_idx, up_idx, sign_ref, ones_ref, gate_table, up_table,
     gate_out, up_out, share_ref, gate_ref, up_ref, gate_acc, up_acc, gate_value, up_value, up_leaf, grad_ref,
+    total_ref,
 ):
     count, block, _ = left_ref.shape
     half = block // 2
@@ -503,10 +517,13 @@
     @pl.when(pl.program_id(0) == 0)
     def _():
         grad_ref[...] = jnp.zeros_like(grad_ref)
+        take_totals(left_ref, total_ref)
 
     for p in range(size):
         gate_ref[p * per : (p + 1) * per, :] = gate_hidden[p, 0]
         up_ref[p * per : (p + 1) * per, :] = up_hidden[p, 0]
+    gate_out[0:1, :] = empty_sum(gate_ref, total_ref)
+    up_out[0:1, :] = empty_sum(up_ref, total_ref)
     start_bins([gate_acc, up_acc], up_leaf)
     make_values(left_ref, gate_ref, 0, gate_value)
 
@@ -524,9 +541,8 @@
 
     lax.fori_loop(0, count, body, 0)
     close_block(ones_ref, up_leaf, up_acc)
-    for out, acc_ref, right_ref in ((gate_out, gate_acc, gate_ref), (up_out, up_acc, up_ref)):
-        for k, total in enumerate(all_sums(acc_ref, right_ref, total_ref)):
-            out[k : k + 1, :] = total
+    for out, acc_ref in ((gate_out, gate_acc), (up_out, up_acc)):
+        out[1:, :] = acc_ref[1:, :]
 
     @pl.when(pl.program_id(0) == pl.num_programs(0) - 1)
     def _():
@@ -535,10 +551,10 @@
             share_ref[p] = grad_ref[:, p * rows : (p + 1) * rows, :].astype(BF16)
 
 
-def down_bins_kernel(n_hid, n_inp, *refs):
-    (left_ref, right_ref, total_ref, idx_ref, sign_ref, ones_ref, gate_ref, up_ref, shares_ref) = refs[:9]
-    out_ref, gate_out, up_out, grad_out = refs[9:13]
-    acc_ref, values, leaf_ref = refs[13], refs[14:16], refs[16]
+def down_bins_kernel(n_hid, n_inp, tiles, *refs):
+    (left_ref, right_ref, idx_ref, sign_ref, ones_ref, gate_ref, up_ref, shares_ref) = refs[:8]
+    out_ref, gate_out, up_out, grad_out = refs[8:12]
+    total_ref, acc_ref, values, leaf_ref = refs[12], refs[13], refs[14:16], refs[16]
     (own_ref, got_ref, gate_got, up_got, part_ref, part_got, final_ref) = refs[17:24]
     (own_sem, share_send, share_recv, table_send, table_recv, part_send, part_recv, final_send, final_recv) = refs[24:]
     step, steps = pl.program_id(0), pl.num_programs(0)
@@ -568,17 +584,36 @@
     def lanes_of(tile):
         return pl.ds(pl.multiple_of(tile * cols, LANES), cols)
 
-    def part_copy(tile, k, peer):
+    late = min(LATE_TILES, tiles)
+    groups = [(0, (tiles - late) * cols), ((tiles - late) * cols, late * cols)]
+
+    def part_copy(g, k, peer):
+        lanes = pl.ds(*groups[g])
         return pltpu.make_async_remote_copy(
-            src_ref=part_ref.at[peer, :, lanes_of(tile)], dst_ref=part_got.at[k - 1, :, lanes_of(tile)],
-            send_sem=part_send.at[tile, k - 1], recv_sem=part_recv.at[tile, k - 1], device_id={"hid": peer},
+            src_ref=part_ref.at[peer, :, lanes], dst_ref=part_got.at[k - 1, :, lanes],
+            send_sem=part_send.at[g, k - 1], recv_sem=part_recv.at[g, k - 1], device_id={"hid": peer},
             device_id_type=pl.DeviceIdType.MESH)
 
-    def final_copy(tile, k, peer):
+    def final_copy(g, k, peer):
+        own = final_ref.at[hid, :, pl.ds(*groups[g])]
         return pltpu.make_async_remote_copy(
-            src_ref=final_ref.at[hid, :, lanes_of(tile)], dst_ref=final_ref.at[hid, :, lanes_of(tile)],
-            send_sem=final_send.at[tile, k - 1], recv_sem=final_recv.at[tile, k - 1], device_id={"hid": peer},
-            device_id_type=pl.DeviceIdType.MESH)
+            src_ref=own, dst_ref=own, send_sem=final_send.at[g, k - 1], recv_sem=final_recv.at[g, k - 1],
+            device_id={"hid": peer}, device_id_type=pl.DeviceIdType.MESH)
+
+    def send(g):
+        for k, peer in peers:
+            part_copy(g, k, peer).start()
+
+    def settle(g):
+        for k, peer in peers:
+            part_copy(g, k, peer).wait()
+        lanes = pl.ds(*groups[g])
+        total = part_ref[hid, :, lanes]
+        for k, _ in peers:
+            total = total + part_got[k - 1, :, lanes]
+        final_ref[hid, :, lanes] = total
+        for k, peer in peers:
+            final_copy(g, k, peer).start()
 
     @pl.when(step == 0)
     def _():
@@ -591,36 +626,26 @@
         for copy in copies():
             copy.start()
         own_copy().start()
-
-    def settle(tile):
-        for k, peer in peers:
-            part_copy(tile, k, peer).wait()
-        lanes = lanes_of(tile)
-        total = part_ref[hid, :, lanes]
-        for k, _ in peers:
-            total = total + part_got[k - 1, :, lanes]
-        final_ref[hid, :, lanes] = total
-        for k, peer in peers:
-            final_copy(tile, k, peer).start()
+        take_totals(left_ref, total_ref)
+
+    if tiles > late:
+
+        @pl.when(step == tiles - late)
+        def _():
+            send(0)
+
+        @pl.when(step == tiles - late // 2)
+        def _():
+            settle(0)
+
+    part_ref[0, 0:1, lanes_of(step)] = empty_sum(right_ref, total_ref)
+    bins_tile(left_ref, right_ref, idx_ref, sign_ref, ones_ref, acc_ref, values, leaf_ref)
+    for k in range(1, ENTRIES):
+        part_ref[k // rows, k % rows : k % rows + 1, lanes_of(step)] = acc_ref[k : k + 1, :]
 
     @pl.when(step == steps - 1)
     def _():
-        def early(tile, carry):
-            settle(tile)
-            return carry
-
-        lax.fori_loop(0, steps - 1, early, 0)
-
-    sums = bins_tile(
-        left_ref, right_ref, total_ref, idx_ref, sign_ref, ones_ref, acc_ref, values, leaf_ref
-    )
-    for k, total in enumerate(sums):
-        part_ref[k // rows, k % rows : k % rows + 1, lanes_of(step)] = total
-    for k, peer in peers:
-        part_copy(step, k, peer).start()
-
-    @pl.when(step == steps - 1)
-    def _():
+        send(1)
         for copy in copies():
             copy.wait()
         own_copy().wait()
@@ -635,14 +660,11 @@
             for k, _ in peers:
                 total = total + got_ref[k - 1, i].astype(F32)
             grad_out[i] = total
-        settle(steps - 1)
-
-        def finish(tile, carry):
-            for k, peer in peers:
-                final_copy(tile, k, peer).wait()
-            return carry
-
-        lax.fori_loop(0, steps, finish, 0)
+        settle(1)
+        for g in range(2):
+            if groups[g][1]:
+                for k, peer in peers:
+                    final_copy(g, k, peer).wait()
         out_ref[...] = final_ref[...]
 
 
@@ -696,24 +718,7 @@
     return jnp.asarray(row == np.arange(ENTRIES * SUB)[None, :] // SUB, BF16)
 
 
-def bins_operands(left, total, right, index, most):
-    count, block, tokens = left.shape
-    words, width = index.shape
-    cols = divisor(width, most)
-    specs = [
-        fixed((count, block, tokens)),
-        pl.BlockSpec((tokens, cols), lambda j: (0, j)),
-        fixed((tokens, LANES)),
-        pl.BlockSpec((words, cols), lambda j: (0, j)),
-        fixed((4 * ENTRIES, LANES)),
-        fixed((ENTRIES, ENTRIES * SUB)),
-    ]
-    scratch = [pltpu.VMEM((ENTRIES, cols), F32)]
-    scratch += [pltpu.VMEM((block, cols), F32)] * 2 + [pltpu.VMEM((ENTRIES * SUB, cols), BF16)]
-    return cols, specs, [left, right, total, index, sign_table(), group_ones()], scratch
-
-
-def grad_bins(left, total, hidden, gate_index, up_index, gate_table, up_table, shares):
+def grad_bins(left, hidden, gate_index, up_index, gate_table, up_table, shares):
     count, block, tokens = left.shape
     words, width = gate_index.shape
     size, _, rows, _ = hidden.shape
@@ -728,7 +733,6 @@
             fixed((count, block, tokens)),
             pl.BlockSpec((size, 1, rows, cols), lambda j: (0, 0, 0, j)),
             pl.BlockSpec((size, 1, rows, cols), lambda j: (0, 1, 0, j)),
-            fixed((tokens, LANES)),
             index,
             index,
             fixed((4 * ENTRIES, LANES)),
@@ -746,27 +750,41 @@
         + [pltpu.VMEM((ENTRIES, cols), F32)] * 2
         + [pltpu.VMEM((block, cols), F32)] * 2
         + [pltpu.VMEM((ENTRIES * SUB, cols), BF16)]
-        + [pltpu.VMEM((count, tokens, block), F32)],
+        + [pltpu.VMEM((count, tokens, block), F32), pltpu.VMEM((SUB, tokens), BF16)],
         cost_estimate=cost(80 * tokens * words * width, 8 * words * width),
         name="grad_bins",
     )(
-        left, hidden, hidden, total, gate_index, up_index, sign_table(), group_ones(), gate_table, up_table
+        left, hidden, hidden, gate_index, up_index, sign_table(), group_ones(), gate_table, up_table
     )
 
 
-def down_bins(left, total, right, index, gate_part, up_part, shares):
+def down_bins(left, right, index, gate_part, up_part, shares):
     count, block, tokens = left.shape
     words, width = index.shape
     n_hid, n_inp = lax.axis_size("hid"), lax.axis_size("inp")
-    cols, specs, args, scratch = bins_operands(left, total, right, index, 256)
+    cols = divisor(width, 256)
     steps = width // cols
     table = gate_part.shape
     share = shares.shape[1:]
-    specs += [fixed(table), fixed(table), pl.BlockSpec(memory_space=pl.ANY)]
-    args += [gate_part, up_part, shares]
+    specs = [
+        fixed((count, block, tokens)),
+        pl.BlockSpec((tokens, cols), lambda j: (0, j)),
+        pl.BlockSpec((words, cols), lambda j: (0, j)),
+        fixed((4 * ENTRIES, LANES)),
+        fixed((ENTRIES, ENTRIES * SUB)),
+        fixed(table),
+        fixed(table),
+        pl.BlockSpec(memory_space=pl.ANY),
+    ]
+    args = [left, right, index, sign_table(), group_ones(), gate_part, up_part, shares]
     rows = ENTRIES // n_hid
     groups = (n_hid, rows, width)
-    scratch = scratch + [
+    scratch = [
+        pltpu.VMEM((SUB, tokens), BF16),
+        pltpu.VMEM((ENTRIES, cols), F32),
+        pltpu.VMEM((block, cols), F32),
+        pltpu.VMEM((block, cols), F32),
+        pltpu.VMEM((ENTRIES * SUB, cols), BF16),
         pltpu.VMEM(share, BF16),
         pltpu.VMEM((n_hid - 1,) + share, BF16),
         pltpu.VMEM((n_inp - 1,) + table, F32),
@@ -779,13 +797,13 @@
         pltpu.SemaphoreType.DMA((n_hid - 1,)),
         pltpu.SemaphoreType.DMA((2 * (n_inp - 1),)),
         pltpu.SemaphoreType.DMA((2 * (n_inp - 1),)),
-        pltpu.SemaphoreType.DMA((steps, n_hid - 1)),
-        pltpu.SemaphoreType.DMA((steps, n_hid - 1)),
-        pltpu.SemaphoreType.DMA((steps, n_hid - 1)),
-        pltpu.SemaphoreType.DMA((steps, n_hid - 1)),
+        pltpu.SemaphoreType.DMA((2, n_hid - 1)),
+        pltpu.SemaphoreType.DMA((2, n_hid - 1)),
+        pltpu.SemaphoreType.DMA((2, n_hid - 1)),
+        pltpu.SemaphoreType.DMA((2, n_hid - 1)),
     ]
     return pl.pallas_call(
-        functools.partial(down_bins_kernel, n_hid, n_inp),
+        functools.partial(down_bins_kernel, n_hid, n_inp, steps),
         grid=(steps,),
         in_specs=specs,
         out_specs=[fixed(groups), fixed(table), fixed(table), fixed(share)],
@@ -802,11 +820,6 @@
     )(*args)
 
 
-def row_totals(array):
-    total = jnp.sum(array.astype(F32), axis=1, keepdims=True)
-    return jnp.broadcast_to(total, (array.shape[0], LANES))
-
-
 def pairing(block, dtype):
     row = np.arange(block)[:, None]
     col = np.arange(block)[None, :]
@@ -834,14 +847,12 @@
         pairing(math.gcd(width, 256), BF16),
     )
     x_turned = jnp.swapaxes(x_blocks, 1, 2)
-    x_total = row_totals(inputs)
-    acts = hidden[:, 2].reshape(tokens, width)
+    block = math.gcd(width, 256)
+    acts = hidden[:, 2].reshape(tokens, width // block, block)
     gate_part, up_part, shares = grad_bins(
-        x_turned, x_total, hidden, gate_index, up_index, gate_table, up_table, lax.axis_size("hid")
+        x_turned, hidden, gate_index, up_index, gate_table, up_table, lax.axis_size("hid")
     )
-    sums = down_bins(
-        jnp.swapaxes(to_blocks(acts), 1, 2), row_totals(acts), out_grad, down_index, gate_part, up_part, shares
-    )
+    sums = down_bins(jnp.transpose(acts, (1, 2, 0)), out_grad, down_index, gate_part, up_part, shares)
     down_sum, gate_sum, up_sum, input_grad = finish(*sums, order, 1.0 / (tokens * ENTRIES))
     return input_grad, gate_sum, up_sum, down_sum
 

time: 254 us -> 242 us (0.953)
  Pallas kernels: 243 us -> 236 us
  other arithmetic: 2.82 us -> 0 us
    pallas_call x1, Pallas kernels: 65.7 us -> 60.3 us  [hidden_grads(): pl.pallas_call(functools.partial(hidden_kernel, size, down_steps), grid=(...]
    pallas_call x1, Pallas kernels: 73.9 us -> 69.2 us  [down_bins(): pl.pallas_call(functools.partial(down_bins_kernel, n_hid, n_inp, steps),...]
    reduce_sum x2 -> x0, other arithmetic: 2.82 us -> none  [row_totals(): total = jnp.sum(array.astype(F32), axis=1, keepdims=True)]
where the time goes in v5:
time: 242 us
  Pallas kernels  236 us (98%)
  local copies, waits for them, and re-layouts  3.62 us (1%)
    pallas_call x1, Pallas kernels, grad_bins(): pl.pallas_call(grad_kernel, grid=(width // cols,), in_specs=[fixed((count...  103 us
    pallas_call x1, Pallas kernels, down_bins(): pl.pallas_call(functools.partial(down_bins_kernel, n_hid, n_inp, steps),...  69.2 us
    pallas_call x1, Pallas kernels, hidden_grads(): pl.pallas_call(functools.partial(hidden_kernel, size, down_steps), grid=(...  60.3 us

profile of v5, /device:TPU:0, one launch (start us, length us, event | category | flops | bytes accessed | tf_op | source)
XLA Modules:
  0.0 241.6 jit_solution(1942426705126289529)
XLA Ops:
  0.6 1.8 convolution_convert_fusion
  2.4 0.0 copy-start
  2.4 1.3 copy.24.refs_1_
  3.8 60.3 %hidden_grads.1.gate_hidden.up_hidden = bf16[4,3,32,3328]{3,2,1,0:T(8,128)(2,1)} custom-call(bf16[128,4096]{1,0:T(8,128)(2,1)} %refs_1_.1, bf16[16,128,256]{2,1,0:T(8,128)(2,1)} %copy.24.refs_1_, s32[1664,4096]{1,0:T(8,128)} %refs_2_.3, f32[16,4096]{1,0:T(8,128)} %refs_3_.2, s32[2048,3328]{1,0:T(8,128)} %gate_idx.1, f32[16,3328]{1,0:T(8,128)} %gate_table.1, ...), custom_call_target="tpu_custom_call" | custom-call | flops 10468982784 | bytes 81788928 | tf_op jit(solution)/shard_map/hidden_grads/pallas_call | solution.py:343
  64.0 0.0 copy-done
  64.0 0.0 slice-start
  64.0 102.6 %grad_bins.1 = (f32[16,3328]{1,0:T(8,128)}, f32[16,3328]{1,0:T(8,128)}, bf16[8,16,16,256]{3,2,1,0:T(8,128)(2,1)}) custom-call(bf16[16,256,128]{2,1,0:T(8,128)(2,1)} %bitcast.12, bf16[4,3,32,3328]{3,2,1,0:T(8,128)(2,1)} %hidden_grads.1.gate_hidden.up_hidden, bf16[4,3,32,3328]{3,2,1,0:T(8,128)(2,1)} %hidden_grads.1.gate_hidden.up_hidden, ...), custom_call_target="tpu_custom_call" | custom-call | flops 69793218560 | bytes 54525952 | tf_op jit(solution)/shard_map/grad_bins/pallas_call | solution.py:729
  166.6 0.0 slice-done
  166.7 0.6 reshape_squeeze.3
  167.3 1.7 copy.25
  169.0 69.2 %down_bins.1 = (f32[8,2,4096]{2,1,0:T(2,128)}, f32[16,3328]{1,0:T(8,128)}, f32[16,3328]{1,0:T(8,128)}, f32[16,16,256]{2,1,0:T(8,128)}) custom-call(bf16[13,256,128]{2,1,0:T(8,128)(2,1)} %bitcast.14, bf16[128,4096]{1,0:T(8,128)(2,1)} %refs_1_.1, s32[1664,4096]{1,0:T(8,128)} %refs_2_.3, bf16[64,128]{1,0:T(8,128)(2,1)} %constant.9.clone.sign_ref.refs_3_, ...), custom_call_target="tpu_custom_call" | custom-call | flops 34896609280 | bytes 27262976 | tf_op jit(solution)/shard_map/down_bins/pallas_call | solution.py:805
  238.1 3.5 %finish.1 = (f32[16,4096]{1,0:T(8,128)}, f32[16,3328]{1,0:T(8,128)}, f32[16,3328]{1,0:T(8,128)}, bf16[16,4096]{1,0:T(8,128)(2,1)}) custom-call(f32[8,2,4096]{2,1,0:T(2,128)} %get-tuple-element.18.down_ref, f32[16,3328]{1,0:T(8,128)} %get-tuple-element.19.gate_ref, f32[16,3328]{1,0:T(8,128)} %get-tuple-element.20.up_ref, ...), custom_call_target="tpu_custom_call" | custom-call | flops 16777216 | bytes 425984 | tf_op jit(solution)/shard_map/finish/pallas_call | solution.py:690
Async XLA Ops:
  2.4 61.6 %copy-start = (bf16[256,128,16]{1,0,2:T(8,128)(2,1)}, bf16[256,128,16]{1,0,2:T(8,128)(2,1)S(1)}, u32[]{:S(2)}) copy-start(bf16[256,128,16]{1,0,2:T(8,128)(2,1)S(1)} %convolution_convert_fusion) | copy-start | bytes 3145732
  64.0 102.6 %slice-start = ((bf16[4,3,32,3328]{3,2,1,0:T(8,128)(2,1)}), bf16[4,1,32,3328]{3,2,1,0:T(8,128)(2,1)S(1)}, s32[]{:S(2)}) async-start(bf16[4,3,32,3328]{3,2,1,0:T(8,128)(2,1)} %hidden_grads.1.gate_hidden.up_hidden), calls=%async_computation | async-start | bytes 1703936 | tf_op jit(solution)/shard_map/slice | solution.py:851

commit v6 on v5

--- a/solution.py
+++ b/solution.py
@@ -257,7 +257,7 @@
                     og_ref[...], decode_block(down_ref, tables, first + k, cols // 2)
                 )
 
-        grouped(hid_count, 7, body)
+        grouped(hid_count, 13, body)
 
     @pl.when(step == down_steps - 1)
     def _():
@@ -505,7 +505,7 @@
 
 def grad_kernel(
     left_ref, gate_hidden, up_hidden, gate_idx, up_idx, sign_ref, ones_ref, gate_table, up_table,
-    gate_out, up_out, share_ref, gate_ref, up_ref, gate_acc, up_acc, gate_value, up_value, up_leaf, grad_ref,
+    gate_out, up_out, share_ref, gate_ref, up_ref, gate_acc, up_acc, gate_value, up_value, grad_ref,
     total_ref,
 ):
     count, block, _ = left_ref.shape
@@ -524,23 +524,27 @@
         up_ref[p * per : (p + 1) * per, :] = up_hidden[p, 0]
     gate_out[0:1, :] = empty_sum(gate_ref, total_ref)
     up_out[0:1, :] = empty_sum(up_ref, total_ref)
-    start_bins([gate_acc, up_acc], up_leaf)
+    gate_acc[...] = jnp.zeros_like(gate_acc)
+    up_acc[...] = jnp.zeros_like(up_acc)
     make_values(left_ref, gate_ref, 0, gate_value)
 
+    def close_up(i, leaves, weights):
+        close_now(ones_ref, leaves, up_acc)
+        grad_ref[i] += contract_cols(up_ref[...], weights)
+
     def body(i, carry):
-        close_block(ones_ref, up_leaf, up_acc)
+        close_up(jnp.maximum(i - 1, 0), *carry)
         make_values(left_ref, up_ref, i, up_value)
-        grad = contract_cols(up_ref[...], decode_block(up_idx, tables[1], i, half))
         leaves, weights = add_signed(gate_idx, signs, i, gate_value, tables[0])
         close_now(ones_ref, leaves, gate_acc)
-        grad_ref[i] += grad + contract_cols(gate_ref[...], weights)
+        grad_ref[i] += contract_cols(gate_ref[...], weights)
         make_values(left_ref, gate_ref, jnp.minimum(i + 1, count - 1), gate_value)
-        leaves, _ = add_signed(up_idx, signs, i, up_value)
-        keep_leaves(leaves, up_leaf)
-        return carry
-
-    lax.fori_loop(0, count, body, 0)
-    close_block(ones_ref, up_leaf, up_acc)
+        return add_signed(up_idx, signs, i, up_value, tables[1])
+
+    cols = up_ref.shape[1]
+    blank = [[jnp.zeros((SUB, LANES), BF16)] * (ENTRIES - 1)] * (cols // LANES)
+    last = lax.fori_loop(0, count, body, (blank, jnp.zeros((block, cols), BF16)))
+    close_up(count - 1, *last)
     for out, acc_ref in ((gate_out, gate_acc), (up_out, up_acc)):
         out[1:, :] = acc_ref[1:, :]
 
@@ -749,7 +753,6 @@
         scratch_shapes=[pltpu.VMEM((tokens, cols), BF16)] * 2
         + [pltpu.VMEM((ENTRIES, cols), F32)] * 2
         + [pltpu.VMEM((block, cols), F32)] * 2
-        + [pltpu.VMEM((ENTRIES * SUB, cols), BF16)]
         + [pltpu.VMEM((count, tokens, block), F32), pltpu.VMEM((SUB, tokens), BF16)],
         cost_estimate=cost(80 * tokens * words * width, 8 * words * width),
         name="grad_bins",

time: 242 us -> 241 us (level)
  no operation moved by 1% of the time
where the time goes in v6:
time: 241 us
  Pallas kernels  234 us (97%)
  local copies, waits for them, and re-layouts  3.62 us (2%)
    pallas_call x1, Pallas kernels, grad_bins(): pl.pallas_call(grad_kernel, grid=(width // cols,), in_specs=[fixed((count...  102 us
    pallas_call x1, Pallas kernels, down_bins(): pl.pallas_call(functools.partial(down_bins_kernel, n_hid, n_inp, steps),...  69.2 us
    pallas_call x1, Pallas kernels, hidden_grads(): pl.pallas_call(functools.partial(hidden_kernel, size, down_steps), grid=(...  60.3 us

profile of v6, /device:TPU:0, one launch (start us, length us, event | category | flops | bytes accessed | tf_op | source)
XLA Modules:
  0.0 240.6 jit_solution(15514045759931800375)
XLA Ops:
  0.6 1.8 convolution_convert_fusion
  2.4 0.0 copy-start
  2.4 1.3 copy.24.refs_1_
  3.8 60.3 %hidden_grads.1.gate_hidden.up_hidden = bf16[4,3,32,3328]{3,2,1,0:T(8,128)(2,1)} custom-call(bf16[128,4096]{1,0:T(8,128)(2,1)} %refs_1_.1, bf16[16,128,256]{2,1,0:T(8,128)(2,1)} %copy.24.refs_1_, s32[1664,4096]{1,0:T(8,128)} %refs_2_.3, f32[16,4096]{1,0:T(8,128)} %refs_3_.2, s32[2048,3328]{1,0:T(8,128)} %gate_idx.1, f32[16,3328]{1,0:T(8,128)} %gate_table.1, ...), custom_call_target="tpu_custom_call" | custom-call | flops 10468982784 | bytes 81788928 | tf_op jit(solution)/shard_map/hidden_grads/pallas_call | solution.py:343
  64.0 0.0 copy-done
  64.0 0.0 slice-start
  64.0 101.5 %grad_bins.1 = (f32[16,3328]{1,0:T(8,128)}, f32[16,3328]{1,0:T(8,128)}, bf16[8,16,16,256]{3,2,1,0:T(8,128)(2,1)}) custom-call(bf16[16,256,128]{2,1,0:T(8,128)(2,1)} %bitcast.12, bf16[4,3,32,3328]{3,2,1,0:T(8,128)(2,1)} %hidden_grads.1.gate_hidden.up_hidden, bf16[4,3,32,3328]{3,2,1,0:T(8,128)(2,1)} %hidden_grads.1.gate_hidden.up_hidden, ...), custom_call_target="tpu_custom_call" | custom-call | flops 69793218560 | bytes 54525952 | tf_op jit(solution)/shard_map/grad_bins/pallas_call | solution.py:733
  165.6 0.0 slice-done
  165.6 0.6 reshape_squeeze.3
  166.2 1.7 copy.25
  167.9 69.2 %down_bins.1 = (f32[8,2,4096]{2,1,0:T(2,128)}, f32[16,3328]{1,0:T(8,128)}, f32[16,3328]{1,0:T(8,128)}, f32[16,16,256]{2,1,0:T(8,128)}) custom-call(bf16[13,256,128]{2,1,0:T(8,128)(2,1)} %bitcast.14, bf16[128,4096]{1,0:T(8,128)(2,1)} %refs_1_.1, s32[1664,4096]{1,0:T(8,128)} %refs_2_.3, bf16[64,128]{1,0:T(8,128)(2,1)} %constant.9.clone.sign_ref.refs_3_, ...), custom_call_target="tpu_custom_call" | custom-call | flops 34896609280 | bytes 27262976 | tf_op jit(solution)/shard_map/down_bins/pallas_call | solution.py:808
  237.1 3.5 %finish.1 = (f32[16,4096]{1,0:T(8,128)}, f32[16,3328]{1,0:T(8,128)}, f32[16,3328]{1,0:T(8,128)}, bf16[16,4096]{1,0:T(8,128)(2,1)}) custom-call(f32[8,2,4096]{2,1,0:T(2,128)} %get-tuple-element.18.down_ref, f32[16,3328]{1,0:T(8,128)} %get-tuple-element.19.gate_ref, f32[16,3328]{1,0:T(8,128)} %get-tuple-element.20.up_ref, ...), custom_call_target="tpu_custom_call" | custom-call | flops 16777216 | bytes 425984 | tf_op jit(solution)/shard_map/finish/pallas_call | solution.py:694
Async XLA Ops:
  2.4 61.6 %copy-start = (bf16[256,128,16]{1,0,2:T(8,128)(2,1)}, bf16[256,128,16]{1,0,2:T(8,128)(2,1)S(1)}, u32[]{:S(2)}) copy-start(bf16[256,128,16]{1,0,2:T(8,128)(2,1)S(1)} %convolution_convert_fusion) | copy-start | bytes 3145732
  64.0 101.6 %slice-start = ((bf16[4,3,32,3328]{3,2,1,0:T(8,128)(2,1)}), bf16[4,1,32,3328]{3,2,1,0:T(8,128)(2,1)S(1)}, s32[]{:S(2)}) async-start(bf16[4,3,32,3328]{3,2,1,0:T(8,128)(2,1)} %hidden_grads.1.gate_hidden.up_hidden), calls=%async_computation | async-start | bytes 1703936 | tf_op jit(solution)/shard_map/slice | solution.py:854
